TPU v7x, 32 devices: a whole 2x2x4 slice. The times are simulated.
32 devices in a mesh: dp: 16 (over z, y, x), tensor: 2 (over core).
Axes of the slice: x: 2, y: 2, z: 4, core: 2. Of those that a mesh axis runs over, the one named last changes fastest.
Arguments:
- tokens: bfloat16 [64, 196, 512], P('dp'), may hold values from -6 to 6
- region_ids: int32 [64, 196], P('dp'), may hold values from 0 to 3
- norm1_gain: float32 [512], replicated, may hold values from 0.1 to 1.9
- norm1_bias: float32 [512], replicated, may hold values from -3 to 3
- w_qkv: bfloat16 [512, 3, 512], P(None, None, 'tensor'), may hold values from -0.25 to 0.25
- qv_bias: float32 [2, 512], P(None, 'tensor'), may hold values from -3 to 3
- rel_table: float32 [169, 16], P(None, 'tensor'), may hold values from -4 to 304
- w_proj: bfloat16 [512, 512], P(None, 'tensor'), may hold values from -0.75 to 0.75
- b_proj: float32 [512], replicated, may hold values from -3 to 3
- norm2_gain: float32 [512], replicated, may hold values from 0.1 to 1.9
- norm2_bias: float32 [512], replicated, may hold values from -3 to 3
- w_fc1: bfloat16 [512, 2048], P(None, 'tensor'), may hold values from -0.25 to 0.25
- b_fc1: float32 [2048], P('tensor'), may hold values from -3 to 3
- w_fc2: bfloat16 [512, 2048], P(None, 'tensor'), may hold values from -0.125 to 0.125
- b_fc2: float32 [512], replicated, may hold values from -3 to 3
- cotangent: bfloat16 [64, 196, 512], P('dp'), may hold values from -6 to 6
Outputs:
- out: bfloat16 [64, 196, 512], P('dp')
- grad_tokens: float32 [64, 196, 512], P('dp')
- grad_norm1_gain: float32 [512], replicated
- grad_norm1_bias: float32 [512], replicated
- grad_w_qkv: float32 [512, 3, 512], P('dp', None, 'tensor')
- grad_qv_bias: float32 [2, 512], P(None, 'tensor')
- grad_rel_table: float32 [169, 16], P(None, 'tensor')
- grad_w_proj: float32 [512, 512], P('dp', 'tensor')
- grad_b_proj: float32 [512], replicated
- grad_norm2_gain: float32 [512], replicated
- grad_norm2_bias: float32 [512], replicated
- grad_w_fc1: float32 [512, 2048], P('dp', 'tensor')
- grad_b_fc1: float32 [2048], P('tensor')
- grad_w_fc2: float32 [512, 2048], P('dp', 'tensor')
- grad_b_fc2: float32 [512], replicated
Inputs may be any that keep to these rules, and one draw needn't show every extreme that they name: `region_ids`: tokens of a window attend only to tokens with the same label.
All inputs are finite; a program needn't handle non-finite values.
Results may differ from a plain program's by a relative error of at most 0.012.
Values may be sent and summed in bfloat16 or wider, within the bound.
No kernel may reach another device: no remote copies, remote signals or barrier semaphores. Data moves between devices by JAX's collectives and lax.ppermute only.
A program may use at most 128 MiB of HBM per device.

v0:
```python
import functools

import jax
import jax.numpy as jnp
from jax import lax
from jax.experimental import pallas as pl
from jax.experimental.pallas import tpu as pltpu
from jax.sharding import PartitionSpec as P


HEAD_DIM = 32
SIDE = 14
WIN = 7
SHIFT = 3
NORM_EPS = 1e-05

TOK = SIDE * SIDE
TPAD = 208
WTOK = WIN * WIN
WPAD = 64
BLOCKS = SIDE // WIN
WINS = BLOCKS * BLOCKS
F32 = jnp.float32
BF16 = jnp.bfloat16
LIMIT = 16


def nn(a, b):
    return lax.dot_general(a, b, (((1,), (0,)), ((), ())), preferred_element_type=F32)


def nt(a, b):
    return lax.dot_general(a, b, (((1,), (1,)), ((), ())), preferred_element_type=F32)


def tn(a, b):
    return lax.dot_general(a, b, (((0,), (0,)), ((), ())), preferred_element_type=F32)


def iota(shape, axis):
    return lax.broadcasted_iota(jnp.int32, shape, axis)


def normalize(source):
    center = jnp.mean(source, axis=-1, keepdims=True)
    centred = source - center
    inverse = lax.rsqrt(jnp.mean(centred * centred, axis=-1, keepdims=True) + NORM_EPS)
    return centred * inverse, inverse


def norm_back(upstream, normed, inverse, gain_vec):
    scaled = upstream * gain_vec
    return inverse * (
        scaled
        - jnp.mean(scaled, axis=-1, keepdims=True)
        - normed * jnp.mean(scaled * normed, axis=-1, keepdims=True)
    )


def seventh(value):
    return (value * 37) >> 8


def window_source(slot):
    window, at = slot >> 6, slot & (WPAD - 1)
    row = (window >> 1) * WIN + seventh(at) + SHIFT
    col = (window & 1) * WIN + (at - seventh(at) * WIN) + SHIFT
    row = jnp.where(row >= SIDE, row - SIDE, row)
    col = jnp.where(col >= SIDE, col - SIDE, col)
    return jnp.where(at < WTOK, row * SIDE + col, -1)


def gather_matrix():
    shape = (WINS * WPAD, TPAD)
    hit = window_source(iota(shape, 0)) == iota(shape, 1)
    return jnp.where(hit, 1.0, 0.0).astype(BF16)


def scatter_matrix():
    shape = (TPAD, WINS * WPAD)
    hit = window_source(iota(shape, 1)) == iota(shape, 0)
    return jnp.where(hit, 1.0, 0.0).astype(BF16)


def head_mask(heads):
    shape = (heads * WPAD, 2 * heads * HEAD_DIM)
    hit = (iota(shape, 0) >> 6) == ((iota(shape, 1) & (heads * HEAD_DIM - 1)) >> 5)
    return jnp.where(hit, 1.0, 0.0).astype(BF16)


def log2(value):
    return value.bit_length() - 1


def row_order(slot, rows, digits, order):
    rest, block = slot >> log2(rows), 0
    for digit in reversed(order):
        stride, size = digits[digit]
        block = block + (rest & (size - 1)) * stride
        rest = rest >> log2(size)
    return block * rows + (slot & (rows - 1))


def order_matrix(width, layout):
    shape = (width, width)
    hit = row_order(iota(shape, 0), *layout) == iota(shape, 1)
    return jnp.where(hit, 1.0, 0.0).astype(BF16)


def fill_rows(rows_ref, block_ref, first, images):
    rows_ref[...] = jnp.zeros(rows_ref.shape, rows_ref.dtype)
    for image in range(images):
        rows_ref[image * TPAD : image * TPAD + TOK, :] = block_ref[first + image].astype(
            rows_ref.dtype
        )


def window_mask(ids_row, pick):
    ids_b = jnp.broadcast_to(ids_row.astype(F32), (2 * WPAD, TOK)).astype(BF16)
    pick = pick[:, :TOK]
    keys = nt(pick, ids_b)
    queries = nt(ids_b[:16], jnp.concatenate([pick, pick], axis=0))[0:1]
    shape = (WPAD, 2 * WPAD)
    key_at = iota(shape, 0)
    query_at = iota(shape, 1) & (WPAD - 1)
    same = jnp.logical_or(keys == queries, query_at >= WTOK)
    return jnp.where(jnp.logical_and(same, key_at < WTOK), 0.0, -jnp.inf)


def two_groups(rows):
    half = rows.shape[1] // 2
    zero = jnp.zeros((rows.shape[0], half), rows.dtype)
    return jnp.concatenate(
        [
            jnp.concatenate([rows[:, :half], zero], axis=1),
            jnp.concatenate([zero, rows[:, half:]], axis=1),
        ],
        axis=0,
    )


def own_groups(rows):
    half = rows.shape[1] // 2
    return jnp.concatenate([rows[:WPAD, :half], rows[WPAD:, half:]], axis=1)


def per_head(rows, mask, heads):
    return jnp.concatenate([rows] * heads, axis=0) * mask


def table_offsets(rows_half):
    shape = (2 * rows_half, 2 * WPAD)
    entry, query = iota(shape, 0), iota(shape, 1)
    group_e = jnp.where(entry >= rows_half, 1, 0)
    at = query & (WPAD - 1)
    place = seventh(at) * (2 * WIN - 1) + (at - seventh(at) * WIN)
    fits = jnp.logical_and(group_e == (query >> 6), at < WTOK)
    return jnp.where(fits, entry - group_e * rows_half - place, 4096)


def key_offset(key):
    row = key // WIN
    return 2 * WIN * (WIN - 1) - (row * (2 * WIN - 1) + key - row * WIN)


def bias_kernel(heads, rows_half, sel_ref, mine_ref, other_ref, bias_ref, off_ref, table_ref):
    off_ref[...] = table_offsets(rows_half)
    bias_ref[...] = jnp.zeros(bias_ref.shape, F32)
    entries = mine_ref.shape[1]
    table_ref[...] = jnp.zeros(table_ref.shape, F32)
    table_ref[:, :entries] = mine_ref[...]
    table_ref[:, rows_half : rows_half + entries] = other_ref[...]
    table = table_ref[...]
    part_a = table.astype(BF16).astype(F32)
    part_b = (table - part_a).astype(BF16).astype(F32)
    part_c = table - part_a - part_b
    parts = jnp.concatenate([part_a, part_b, part_c], axis=0).astype(BF16)
    for key in range(WTOK):
        pick = jnp.where(off_ref[...] == key_offset(key), 1.0, 0.0).astype(BF16)
        rows = nn(parts, pick)
        bias_ref[pl.ds(key, heads, stride=WPAD), :] = (
            rows[:heads] + rows[heads : 2 * heads] + rows[2 * heads :]
        )


def attend_kernel(
    images,
    heads,
    me_ref,
    tok_ref,
    ids_ref,
    gain_ref,
    shift_ref,
    wm_ref,
    wo_ref,
    qvbm_ref,
    qvbo_ref,
    bias_ref,
    pm_ref,
    po_ref,
    bproj_ref,
    q_ref,
    k_ref,
    v_ref,
    win_ref,
    lse_ref,
    merged_ref,
    resid_ref,
    x_ref,
    pick_ref,
    att_ref,
    mask_ref,
):
    chan = heads * HEAD_DIM
    factor = HEAD_DIM ** (-0.5)
    fill_rows(x_ref, tok_ref, me_ref[0] * images, images)
    normed, _ = normalize(x_ref[...])
    ln_one = (normed * gain_ref[...] + shift_ref[...]).astype(BF16)
    pick_ref[...] = gather_matrix()
    mask_ref[...] = head_mask(heads)
    slots = WINS * WPAD
    for image in range(images):
        win_ref[image * slots : (image + 1) * slots, :] = nn(
            pick_ref[...], ln_one[image * TPAD : (image + 1) * TPAD]
        ).astype(BF16)
    for group, (w_ref, b_ref) in enumerate(((wm_ref, qvbm_ref), (wo_ref, qvbo_ref))):
        cols = slice(group * chan, (group + 1) * chan)
        win = win_ref[...]
        q_ref[:, cols] = ((nn(win, w_ref[0]) + b_ref[0:1, :]) * factor).astype(BF16)
        k_ref[:, cols] = nn(win, w_ref[1]).astype(BF16)
        v_ref[:, cols] = (nn(win, w_ref[2]) + b_ref[1:2, :]).astype(BF16)

    def one_window(window, carry):
        rows = pl.ds(pl.multiple_of(window * WPAD, WPAD), WPAD)
        image = window // WINS
        local = pl.multiple_of((window - image * WINS) * WPAD, WPAD)
        ids_row = ids_ref[pl.ds(me_ref[0] * images + image, 1), :]
        allowed = window_mask(ids_row, pick_ref[pl.ds(local, WPAD), :])
        k_all = per_head(k_ref[rows, :], mask_ref[...], heads)
        v_all = per_head(v_ref[rows, :], mask_ref[...], heads)
        scores = nt(k_all, two_groups(q_ref[rows, :])) + bias_ref[...]
        scores = scores.reshape(heads, WPAD, 2 * WPAD) + allowed[None]
        top = jnp.max(scores, axis=1, keepdims=True)
        grown = jnp.exp(scores - top)
        total = jnp.sum(grown, axis=1, keepdims=True)
        lse_ref[window] = (top + jnp.log(total)).reshape(heads, 2 * WPAD)
        probs = (grown * (1.0 / total)).astype(BF16).reshape(heads * WPAD, 2 * WPAD)
        att_ref[rows, :] = own_groups(tn(probs, v_all)).astype(BF16)
        return carry

    lax.fori_loop(0, images * WINS, one_window, 0)
    back = scatter_matrix()
    for image in range(images):
        merged_ref[image * TPAD : (image + 1) * TPAD, :] = nn(
            back, att_ref[image * slots : (image + 1) * slots, :]
        ).astype(BF16)
    resid_ref[...] = (
        x_ref[...]
        + (nt(merged_ref[:, :chan], pm_ref[...]) + nt(merged_ref[:, chan:], po_ref[...]))
        + bproj_ref[...]
    )


def ffn_kernel(
    images,
    layouts,
    last,
    me_ref,
    resid_ref,
    cot_ref,
    gain_ref,
    shift_ref,
    w1_ref,
    w2_ref,
    b1_ref,
    *refs,
):
    if last:
        b2_ref, ln_ref, lnt_ref, cot_b_ref, cot_t_ref, ffn_in, gln_in = refs[:7]
        g1_ref, g2_ref, gb_ref, out_ref, half_ref, gres_ref, sums_ref = refs[7:14]
        ffn_ref, gln_ref = refs[14:]
    else:
        g1_ref, g2_ref, gb_ref = refs[:3]
        ln_ref, lnt_ref, cot_b_ref, cot_t_ref, ffn_ref, gln_ref = refs[3:]
    if last:
        ffn_ref[...] = ffn_in[...]
        gln_ref[...] = gln_in[...]
    else:
        normed, _ = normalize(resid_ref[...])
        ln_ref[...] = (normed * gain_ref[...] + shift_ref[...]).astype(BF16)
        fill_rows(cot_b_ref, cot_ref, me_ref[0] * images, images)
        width = ln_ref.shape[1]
        lnt_ref[...] = nt(order_matrix(width, layouts[0]), ln_ref[...]).astype(BF16)
        cot_t_ref[...] = nt(order_matrix(width, layouts[1]), cot_b_ref[...]).astype(BF16)
        ffn_ref[...] = jnp.zeros(ffn_ref.shape, F32)
        gln_ref[...] = jnp.zeros(gln_ref.shape, F32)
    chunk = 256

    def one_chunk(at, carry):
        cols = pl.ds(pl.multiple_of(at * chunk, chunk), chunk)
        pre = nn(ln_ref[...], w1_ref[:, cols]) + b1_ref[:, cols]
        phi = 0.5 * (1.0 + lax.erf(pre * 0.7071067811865476))
        act = (pre * phi).astype(BF16)
        slope = phi + pre * jnp.exp(-0.5 * pre * pre) * 0.3989422804014327
        grad_pre = nn(cot_b_ref[...], w2_ref[:, cols]) * slope
        gb_ref[:, cols] = jnp.sum(grad_pre, axis=0, keepdims=True)
        grad_pre = grad_pre.astype(BF16)
        ffn_ref[...] += nt(act, w2_ref[:, cols])
        gln_ref[...] += nt(grad_pre, w1_ref[:, cols])
        g2_ref[:, cols] = nn(cot_t_ref[...], act).astype(BF16)
        g1_ref[:, cols] = nn(lnt_ref[...], grad_pre).astype(BF16)
        return carry

    lax.fori_loop(0, w1_ref.shape[1] // chunk, one_chunk, 0)
    if not last:
        return
    resid = resid_ref[...]
    result = (resid + ffn_ref[...] + b2_ref[...]).astype(BF16)
    for image in range(images):
        piece = result[image * TPAD : image * TPAD + TOK]
        out_ref[me_ref[0] * images + image] = piece
        half_ref[image] = piece
    normed, inverse = normalize(resid)
    upstream = gln_ref[...]
    cot = cot_b_ref[...].astype(F32)
    grad_resid = cot + norm_back(upstream, normed, inverse, gain_ref[...])
    gres_ref[...] = grad_resid
    sums_ref[0:1, :] = jnp.sum(grad_resid, axis=0, keepdims=True)
    sums_ref[1:2, :] = jnp.sum(upstream * normed, axis=0, keepdims=True)
    sums_ref[2:3, :] = jnp.sum(upstream, axis=0, keepdims=True)
    sums_ref[3:4, :] = jnp.sum(cot, axis=0, keepdims=True)
    sums_ref[4:8, :] = jnp.zeros((4, sums_ref.shape[1]), F32)


def attend_back_kernel(
    images,
    heads,
    layouts,
    me_ref,
    gres_ref,
    ids_ref,
    merged_ref,
    pm_ref,
    po_ref,
    q_ref,
    k_ref,
    v_ref,
    win_ref,
    lse_ref,
    bias_ref,
    gqkm_ref,
    gqko_ref,
    gvpm_ref,
    gvpo_ref,
    gqkv_ref,
    sums_ref,
    gbias_ref,
    pick_ref,
    gatt_ref,
    mask_ref,
    qsum_ref,
    vsum_ref,
):
    chan = heads * HEAD_DIM
    wide = 2 * chan
    factor = HEAD_DIM ** (-0.5)
    slots = WINS * WPAD
    pick_ref[...] = gather_matrix()
    mask_ref[...] = head_mask(heads)
    gres = gres_ref[...]
    gres_b = gres.astype(BF16)
    width = gres.shape[1]
    gres_t = nt(order_matrix(width, layouts[1]), gres_b).astype(BF16)
    gvpm_ref[:, chan:] = nn(gres_t, merged_ref[:, :chan]).astype(BF16)
    gvpo_ref[:, chan:] = nn(gres_t, merged_ref[:, chan:]).astype(BF16)
    grad_m = jnp.concatenate(
        [nn(gres_b, pm_ref[...]).astype(BF16), nn(gres_b, po_ref[...]).astype(BF16)], axis=1
    )
    for image in range(images):
        gatt_ref[image * slots : (image + 1) * slots, :] = nn(
            pick_ref[...], grad_m[image * TPAD : (image + 1) * TPAD]
        ).astype(BF16)
    gbias_ref[...] = jnp.zeros(gbias_ref.shape, F32)
    qsum_ref[...] = jnp.zeros(qsum_ref.shape, F32)
    vsum_ref[...] = jnp.zeros(vsum_ref.shape, F32)

    def one_window(window, carry):
        rows = pl.ds(pl.multiple_of(window * WPAD, WPAD), WPAD)
        image = window // WINS
        local = pl.multiple_of((window - image * WINS) * WPAD, WPAD)
        ids_row = ids_ref[pl.ds(me_ref[0] * images + image, 1), :]
        allowed = window_mask(ids_row, pick_ref[pl.ds(local, WPAD), :])
        mask = mask_ref[...]
        k_all = per_head(k_ref[rows, :], mask, heads)
        v_all = per_head(v_ref[rows, :], mask, heads)
        q_two = two_groups(q_ref[rows, :])
        g_two = two_groups(gatt_ref[rows, :])
        scores = nt(k_all, q_two) + bias_ref[...]
        scores = scores.reshape(heads, WPAD, 2 * WPAD) + allowed[None]
        probs = jnp.exp(scores - lse_ref[window].reshape(heads, 1, 2 * WPAD))
        g_probs = nt(v_all, g_two).reshape(heads, WPAD, 2 * WPAD)
        inner = jnp.sum(probs * g_probs, axis=1, keepdims=True)
        g_scores = (probs * (g_probs - inner)).reshape(heads * WPAD, 2 * WPAD)
        gbias_ref[...] += g_scores
        probs_b = probs.astype(BF16).reshape(heads * WPAD, 2 * WPAD)
        g_scores = g_scores.astype(BF16)

        def fold(product):
            return jnp.sum((product * mask.astype(F32)).reshape(heads, WPAD, wide), axis=0)

        g_v = fold(nn(probs_b, g_two))
        g_k = fold(nn(g_scores, q_two))
        g_q = own_groups(tn(g_scores, k_all)) * factor
        qsum_ref[...] += g_q
        vsum_ref[...] += g_v
        for group in range(2):
            cols = slice(group * chan, (group + 1) * chan)
            base = group * 3 * chan
            gqkv_ref[rows, base : base + chan] = g_q[:, cols].astype(BF16)
            gqkv_ref[rows, base + chan : base + 2 * chan] = g_k[:, cols].astype(BF16)
            gqkv_ref[rows, base + 2 * chan : base + 3 * chan] = g_v[:, cols].astype(BF16)
        return carry

    lax.fori_loop(0, images * WINS, one_window, 0)
    sums_ref[...] = jnp.zeros(sums_ref.shape, F32)
    sums_ref[0:1, :] = jnp.sum(qsum_ref[...], axis=0, keepdims=True)
    sums_ref[1:2, :] = jnp.sum(vsum_ref[...], axis=0, keepdims=True)
    win_a = nt(order_matrix(width, layouts[0]), win_ref[...]).astype(BF16)
    win_b = nt(order_matrix(width, layouts[1]), win_ref[...]).astype(BF16)
    gqko_ref[...] = nn(win_a, gqkv_ref[:, 3 * chan : 5 * chan]).astype(BF16)
    gvpo_ref[:, :chan] = nn(win_b, gqkv_ref[:, 5 * chan :]).astype(BF16)
    gqkm_ref[...] = nn(win_a, gqkv_ref[:, : 2 * chan]).astype(BF16)
    gvpm_ref[:, :chan] = nn(win_b, gqkv_ref[:, 2 * chan : 3 * chan]).astype(BF16)


def last_kernel(
    images,
    heads,
    rows_half,
    me_ref,
    tok_ref,
    gres_ref,
    gqkv_ref,
    wm_ref,
    wo_ref,
    gain_ref,
    gbias_ref,
    two_ref,
    qv_ref,
    gbm_ref,
    gbo_ref,
    full_ref,
    half_ref,
    mine_ref,
    theirs_ref,
    x_ref,
    off_ref,
    acc_ref,
):
    chan = heads * HEAD_DIM
    slots = WINS * WPAD
    grad_win = nt(gqkv_ref[:, :chan], wm_ref[0])
    for at in range(1, 6):
        w_ref = wm_ref if at < 3 else wo_ref
        grad_win += nt(gqkv_ref[:, at * chan : (at + 1) * chan], w_ref[at % 3])
    high = grad_win.astype(BF16)
    low = (grad_win - high.astype(F32)).astype(BF16)
    back = scatter_matrix()
    upstream = jnp.concatenate(
        [
            nn(back, high[image * slots : (image + 1) * slots])
            + nn(back, low[image * slots : (image + 1) * slots])
            for image in range(images)
        ],
        axis=0,
    )
    fill_rows(x_ref, tok_ref, me_ref[0] * images, images)
    normed, inverse = normalize(x_ref[...])
    grad_in = gres_ref[...] + norm_back(upstream, normed, inverse, gain_ref[...])
    for image in range(images):
        piece = grad_in[image * TPAD : image * TPAD + TOK]
        full_ref[me_ref[0] * images + image] = piece
        half_ref[image] = piece
    width = upstream.shape[1]
    gain_sum = jnp.sum(upstream * normed, axis=0, keepdims=True)
    shift_sum = jnp.sum(upstream, axis=0, keepdims=True)
    off_ref[...] = table_offsets(rows_half)
    acc_ref[...] = jnp.zeros(acc_ref.shape, F32)
    for key in range(WTOK):
        pick = jnp.where(off_ref[...] == key_offset(key), 1.0, 0.0).astype(BF16)
        rows = gbias_ref[pl.ds(key, heads, stride=WPAD), :]
        top = rows.astype(BF16).astype(F32)
        parts = jnp.concatenate([top, rows - top], axis=0).astype(BF16)
        acc_ref[...] += nt(parts, pick)
    table = acc_ref[:heads] + acc_ref[heads:]
    for group, (pack_ref, gb_ref) in enumerate(((mine_ref, gbm_ref), (theirs_ref, gbo_ref))):
        pack_ref[...] = jnp.zeros(pack_ref.shape, F32)
        pack_ref[0:4, :] = two_ref[0:4, :]
        pack_ref[4:5, :] = gain_sum
        pack_ref[5:6, :] = shift_sum
        pack_ref[6:8, :chan] = qv_ref[0:2, group * chan : (group + 1) * chan]
        for at in range(gb_ref.shape[1] // width):
            pack_ref[8 + at : 9 + at, :] = gb_ref[:, at * width : (at + 1) * width]
        pack_ref[16 : 16 + heads, :rows_half] = table[:, group * rows_half : (group + 1) * rows_half]


def unpack_kernel(parts, sel_ref, *refs):
    ins, outs = refs[:parts], refs[parts:]
    if parts == 2:
        total = ins[0][...] + ins[1][...]
    else:
        total = (ins[0][...] + ins[1][...]) + (ins[2][...] + ins[3][...])
    for at in range(6):
        outs[at][...] = total[at : at + 1]
    qv_ref, b1_ref, table_ref = outs[6:]
    qv_ref[...] = total[6:8, : qv_ref.shape[1]]
    width = total.shape[1]
    for at in range(b1_ref.shape[1] // width):
        b1_ref[:, at * width : (at + 1) * width] = total[8 + at : 9 + at]
    table_ref[...] = total[16 : 16 + table_ref.shape[0], : table_ref.shape[1]]


def row_block(ref, sel_ref, blocks, form):
    index = form[0]
    for at, factor in enumerate(form[1:]):
        if factor:
            index = index + factor * sel_ref[at]
    rows = ref.shape[0] // blocks
    if blocks == 1:
        return ref[...].astype(F32)
    return ref[pl.ds(pl.multiple_of(index * rows, rows), rows), :].astype(F32)


def sum_kernel(groups, sel_ref, *refs):
    at, outs = 0, refs[sum(len(g) for g in groups) :]
    for picks, out_ref in zip(groups, outs):
        total = row_block(refs[at], sel_ref, *picks[0])
        for more in range(1, len(picks)):
            total = total + row_block(refs[at + more], sel_ref, *picks[more])
        out_ref[...] = total.astype(out_ref.dtype)
        at += len(picks)


def fan_kernel(groups, rows, sends, sel_ref, *refs):
    flat = sum(len(g) for g in groups)
    outs, total_ref, at, col = refs[flat:-1], refs[-1], 0, 0
    for picks in groups:
        total = row_block(refs[at], sel_ref, *picks[0])
        for more in range(1, len(picks)):
            total = total + row_block(refs[at + more], sel_ref, *picks[more])
        total_ref[:, col : col + total.shape[1]] = total
        col += total.shape[1]
        at += len(picks)
    own = sel_ref[3]
    for s in range(1, sends + 1):
        piece = total_ref[pl.ds(pl.multiple_of((own ^ s) * rows, rows), rows), :]
        outs[s - 1][...] = piece.astype(BF16)
    outs[sends][...] = total_ref[pl.ds(pl.multiple_of(own * rows, rows), rows), :]


def total_kernel(sel_ref, own_ref, *refs):
    ins, (a_ref, b_ref) = refs[:-2], refs[-2:]
    total = own_ref[...]
    for in_ref in ins:
        total = total + in_ref[...].astype(F32)
    a_ref[...] = total[:, : a_ref.shape[1]]
    b_ref[...] = total[:, a_ref.shape[1] :]


def pair_kernel(sel_ref, a_ref, b_ref, out_ref):
    out_ref[...] = a_ref[...] + b_ref[...]


def four_kernel(sel_ref, a_ref, b_ref, c_ref, d_ref, out_ref):
    out_ref[...] = (a_ref[...] + b_ref[...]) + (c_ref[...] + d_ref[...])


def struct(shape, kind):
    return jax.ShapeDtypeStruct(shape, kind)


def call(kernel, scalars, inputs, outs, scratch, flops, limit_mib):
    moved = sum(a.size * a.dtype.itemsize for a in inputs)
    moved += sum(a.size * a.dtype.itemsize for a in outs)
    vmem = pl.BlockSpec(memory_space=pltpu.VMEM)
    return pl.pallas_call(
        kernel,
        in_specs=[pl.BlockSpec(memory_space=pltpu.SMEM)] + [vmem] * len(inputs),
        out_specs=[vmem] * len(outs),
        out_shape=outs,
        scratch_shapes=scratch,
        compiler_params=pltpu.CompilerParams(vmem_limit_bytes=limit_mib << 20),
        cost_estimate=pl.CostEstimate(flops=flops, bytes_accessed=moved, transcendentals=0),
    )(scalars, *inputs)


def digits_of(count):
    digits, stride = [], 1
    for size in (2, 2):
        if (count // stride) % size == 0 and count // stride > 1:
            digits.append((stride, size))
            stride *= size
    while count // stride > 1:
        size = 4 if (count // stride) % 4 == 0 else 2
        digits.append((stride, size))
        stride *= size
    return digits


def xor_exchange(value, axis, count, mask):
    return lax.ppermute(value, axis, [(i, i ^ mask) for i in range(count)])


def scatter_sum(addends, axis, count, digits, order):
    index = lax.axis_index(axis)
    rows, cols = addends[0].shape
    shape = [size for _, size in reversed(digits)] + [rows // count, cols]
    addends = [a.reshape(shape) for a in addends]
    left = list(reversed(range(len(digits))))
    for digit in order:
        stride, size = digits[digit]
        place = left.index(digit)
        mine = (index // stride) % size

        def part(which):
            return [lax.dynamic_index_in_dim(a, which, place, keepdims=False) for a in addends]

        def total(pieces):
            result = pieces[0].astype(F32)
            for piece in pieces[1:]:
                result = result + piece.astype(F32)
            return result

        received = [
            xor_exchange(total(part(mine ^ s)).astype(BF16), axis, count, s * stride)
            for s in range(1, size)
        ]
        addends = part(mine) + received
        left.remove(digit)
    return total(addends)


def all_sum(sel, value, axis, count):
    mask = 1
    while True:
        size = 4 if 4 * mask <= count else 2
        terms = [value] + [xor_exchange(value, axis, count, s * mask) for s in range(1, size)]
        mask *= size
        if mask >= count:
            return terms
        kernel = four_kernel if size == 4 else pair_kernel
        (value,) = call(kernel, sel, terms, [struct(value.shape, F32)], [], 10**5, 2)


def add_blocks(sel, groups, kind):
    flat = [item for group in groups for item in group]
    outs = [
        struct((group[0][0].shape[0] // group[0][1], group[0][0].shape[1]), kind)
        for group in groups
    ]
    picks = tuple(tuple((blocks, form) for _, blocks, form in group) for group in groups)
    return call(
        functools.partial(sum_kernel, picks), sel, [a for a, _, _ in flat], outs, [], 10**6, 4
    )


def scatter_pairs(sel, pair_a, pair_b, axis, count, digits):
    (stride_x, _), (stride_y, _), (stride_z, size_z) = digits
    (a0, a1), (b0, b1) = pair_a, pair_b
    not_x, not_y = (1, 0, -1, 0, 0), (1, 0, 0, -1, 0)
    send_a, send_b = add_blocks(
        sel, [[(a0, 2, not_x), (a1, 2, not_x)], [(b0, 2, not_y), (b1, 2, not_y)]], BF16
    )
    got_a = xor_exchange(send_a, axis, count, stride_x)
    got_b = xor_exchange(send_b, axis, count, stride_y)
    at_a, at_b = (1, 0, 2, -1, 0), (1, 0, -1, 2, 0)
    send_a, send_b = add_blocks(
        sel,
        [
            [(a0, 4, at_a), (a1, 4, at_a), (got_a, 2, not_y)],
            [(b0, 4, at_b), (b1, 4, at_b), (got_b, 2, not_x)],
        ],
        BF16,
    )
    more_a = xor_exchange(send_a, axis, count, stride_y)
    more_b = xor_exchange(send_b, axis, count, stride_x)
    groups = (
        (
            (4, (0, 0, 2, 1, 0)),
            (4, (0, 0, 2, 1, 0)),
            (2, (0, 0, 0, 1, 0)),
            (1, (0, 0, 0, 0, 0)),
        ),
        (
            (4, (0, 0, 1, 2, 0)),
            (4, (0, 0, 1, 2, 0)),
            (2, (0, 0, 1, 0, 0)),
            (1, (0, 0, 0, 0, 0)),
        ),
    )
    cols = a0.shape[1] + b0.shape[1]
    deep = a0.shape[0] // 4
    rows = deep // size_z
    outs = (struct((rows, cols), BF16),) * (size_z - 1) + (struct((rows, cols), F32),)
    *sends, own = call(
        functools.partial(fan_kernel, groups, rows, size_z - 1),
        sel,
        [a0, a1, got_a, more_a, b0, b1, got_b, more_b],
        outs,
        [pltpu.VMEM((deep, cols), F32)],
        10**6,
        6,
    )
    received = [xor_exchange(send, axis, count, s * stride_z) for s, send in enumerate(sends, 1)]
    half = a0.shape[1]
    outs = (struct((rows, half), F32), struct((rows, cols - half), F32))
    return call(total_kernel, sel, [own] + received, outs, [], 10**6, 4)


def per_device(n_dp, n_tensor, *args):
    return block(n_dp, n_tensor, *args)


def block(
    n_dp,
    n_tensor,
    tokens,
    region_ids,
    norm1_gain,
    norm1_bias,
    w_qkv,
    qv_bias,
    rel_table,
    w_proj,
    b_proj,
    norm2_gain,
    norm2_bias,
    w_fc1,
    b_fc1,
    w_fc2,
    b_fc2,
    cotangent,
):
    all_images, _, width = tokens.shape
    images = all_images // n_tensor
    entries, heads = rel_table.shape
    chan = heads * HEAD_DIM
    hidden = w_fc1.shape[1]
    rows_t = images * TPAD
    rows_w = images * WINS * WPAD
    half_rows = -(-entries // 16) * 16
    digits = digits_of(n_dp)
    by_pairs = [size for _, size in digits] == [2, 2, 4] and width // n_dp % 16 == 0
    order_a = list(range(len(digits)))
    order_b = order_a[1:2] + order_a[:1] + order_a[2:]
    plain = order_a[::-1]
    layouts = tuple(
        (width // n_dp, digits, order if by_pairs else plain) for order in (order_a, order_b)
    )
    me = lax.axis_index("tensor")
    spot = lax.axis_index("dp")
    places = [(spot // stride) % size for stride, size in digits[:3]]
    me_arr = sel = jnp.stack([me] + places).astype(jnp.int32)

    def swap(value):
        return lax.ppermute(value, "tensor", [(i, i ^ 1) for i in range(n_tensor)])

    wm = w_qkv.transpose(1, 0, 2)
    wo = swap(wm)
    table_m = rel_table.T
    table_o = swap(table_m)
    qvb_o = swap(qv_bias)
    po = swap(w_proj)
    b1_o = swap(b_fc1.reshape(1, hidden))
    w1o = swap(w_fc1)
    w2o = swap(w_fc2)

    row = lambda vec: vec.reshape(1, -1)

    bias_shape = struct((heads * WPAD, 2 * WPAD), F32)
    (bias,) = call(
        functools.partial(bias_kernel, heads, half_rows),
        sel,
        [table_m, table_o],
        [bias_shape],
        [
            pltpu.VMEM((2 * half_rows, 2 * WPAD), jnp.int32),
            pltpu.VMEM((heads, 2 * half_rows), F32),
        ],
        10**9,
        4,
    )

    ins = (
        tokens,
        region_ids,
        row(norm1_gain),
        row(norm1_bias),
        wm,
        wo,
        qv_bias,
        qvb_o,
        bias,
        w_proj,
        po,
        row(b_proj),
    )
    outs = (
        struct((rows_w, 2 * chan), BF16),
        struct((rows_w, 2 * chan), BF16),
        struct((rows_w, 2 * chan), BF16),
        struct((rows_w, width), BF16),
        struct((images * WINS, heads, 2 * WPAD), F32),
        struct((rows_t, 2 * chan), BF16),
        struct((rows_t, width), F32),
    )
    q, k, v, win_in, lse, merged, resid = call(
        functools.partial(attend_kernel, images, heads),
        me_arr,
        ins,
        outs,
        [
            pltpu.VMEM((rows_t, width), F32),
            pltpu.VMEM((WINS * WPAD, TPAD), BF16),
            pltpu.VMEM((rows_w, 2 * chan), BF16),
            pltpu.VMEM((heads * WPAD, 2 * chan), BF16),
        ],
        3 * 10**9,
        LIMIT,
    )

    weight_grad = struct((width, hidden), BF16)
    acc = struct((rows_t, width), F32)
    kept = (
        struct((rows_t, width), BF16),
        struct((width, rows_t), BF16),
        struct((rows_t, width), BF16),
        struct((width, rows_t), BF16),
        acc,
        acc,
    )
    common = (resid, cotangent, row(norm2_gain), row(norm2_bias))
    ins = common + (w1o, w2o, b1_o)
    outs = (weight_grad, weight_grad, struct((1, hidden), F32)) + kept
    g1o, g2o, gbo, *carried = call(
        functools.partial(ffn_kernel, images, layouts, False),
        me_arr,
        ins,
        outs,
        [],
        3 * 10**9,
        LIMIT,
    )
    got1 = swap(g1o)
    got2 = swap(g2o)
    ins = common + (w_fc1, w_fc2, row(b_fc1), row(b_fc2), *carried)
    outs = (
        weight_grad,
        weight_grad,
        struct((1, hidden), F32),
        struct(tokens.shape, BF16),
        struct((images, TOK, width), BF16),
        acc,
        struct((8, width), F32),
    )
    g1m, g2m, gbm, out_full, out_half, gres, sums_two = call(
        functools.partial(ffn_kernel, images, layouts, True),
        me_arr,
        ins,
        outs,
        [pltpu.VMEM((rows_t, width), F32), pltpu.VMEM((rows_t, width), F32)],
        3 * 10**9,
        LIMIT,
    )

    def scatter(pair_a, pair_b):
        if by_pairs:
            return scatter_pairs(sel, pair_a, pair_b, "dp", n_dp, digits)
        return (
            scatter_sum(pair_a, "dp", n_dp, digits, order_a),
            scatter_sum(pair_b, "dp", n_dp, digits, order_b),
        )

    sent_fc1, sent_fc2 = scatter((g1m, got1), (g2m, got2))
    out_other = swap(out_half)
    output = lax.dynamic_update_slice_in_dim(out_full, out_other, (1 - me) * images, 0)

    ins = (gres, region_ids, merged, w_proj, po, q, k, v, win_in, lse, bias)
    outs = (
        struct((width, 2 * chan), BF16),
        struct((width, 2 * chan), BF16),
        struct((width, 2 * chan), BF16),
        struct((width, 2 * chan), BF16),
        struct((rows_w, 6 * chan), BF16),
        struct((8, 2 * chan), F32),
        bias_shape,
    )
    gqkm, gqko, gvpm, gvpo, gqkv, sums_qv, gbias = call(
        functools.partial(attend_back_kernel, images, heads, layouts),
        me_arr,
        ins,
        outs,
        [
            pltpu.VMEM((WINS * WPAD, TPAD), BF16),
            pltpu.VMEM((rows_w, 2 * chan), BF16),
            pltpu.VMEM((heads * WPAD, 2 * chan), BF16),
            pltpu.VMEM((WPAD, 2 * chan), F32),
            pltpu.VMEM((WPAD, 2 * chan), F32),
        ],
        5 * 10**9,
        LIMIT,
    )

    got_qk = swap(gqko)
    got_vp = swap(gvpo)
    sent_qk, sent_vp = scatter((gqkm, got_qk), (gvpm, got_vp))
    sent_qkv = jnp.stack(
        [sent_qk[:, :chan], sent_qk[:, chan:], sent_vp[:, :chan]], axis=0
    ).transpose(1, 0, 2)
    sent_proj = sent_vp[:, chan:]

    ins = (tokens, gres, gqkv, wm, wo, row(norm1_gain), gbias, sums_two, sums_qv, gbm, gbo)
    pack = struct((16 + heads, width), F32)
    outs = (struct(tokens.shape, F32), struct((images, TOK, width), F32), pack, pack)
    grad_full, grad_half, small, theirs = call(
        functools.partial(last_kernel, images, heads, half_rows),
        me_arr,
        ins,
        outs,
        [
            pltpu.VMEM((rows_t, width), F32),
            pltpu.VMEM((2 * half_rows, 2 * WPAD), jnp.int32),
            pltpu.VMEM((2 * heads, 2 * half_rows), F32),
        ],
        2 * 10**9,
        LIMIT,
    )
    grad_in = lax.dynamic_update_slice_in_dim(grad_full, swap(grad_half), (1 - me) * images, 0)

    got = swap(theirs)
    (small,) = call(pair_kernel, sel, [small, got], [struct(small.shape, F32)], [], 10**5, 2)
    terms = all_sum(sel, small, "dp", n_dp)
    outs = (struct((1, width), F32),) * 6 + (
        struct((2, chan), F32),
        struct((1, hidden), F32),
        struct((heads, entries), F32),
    )
    *vectors, sum_qv, sum_b1, sum_table = call(
        functools.partial(unpack_kernel, len(terms)), sel, terms, outs, [], 10**5, 2
    )
    vectors = [vec.reshape(width) for vec in vectors]
    return (
        output,
        grad_in,
        vectors[4],
        vectors[5],
        sent_qkv,
        sum_qv,
        sum_table.T,
        sent_proj,
        vectors[0],
        vectors[1],
        vectors[2],
        sent_fc1,
        sum_b1.reshape(hidden),
        sent_fc2,
        vectors[3],
    )


def solution(mesh):
    return jax.shard_map(
        functools.partial(per_device, mesh.shape["dp"], mesh.shape["tensor"]),
        mesh=mesh,
        in_specs=(
            P("dp", None, None),
            P("dp", None),
            P(),
            P(),
            P(None, None, "tensor"),
            P(None, "tensor"),
            P(None, "tensor"),
            P(None, "tensor"),
            P(),
            P(),
            P(),
            P(None, "tensor"),
            P("tensor"),
            P(None, "tensor"),
            P(),
            P("dp", None, None),
        ),
        out_specs=(
            P("dp", None, None),
            P("dp", None, None),
            P(),
            P(),
            P("dp", None, "tensor"),
            P(None, "tensor"),
            P(None, "tensor"),
            P("dp", "tensor"),
            P(),
            P(),
            P(),
            P("dp", "tensor"),
            P("tensor"),
            P("dp", "tensor"),
            P(),
        ),
        check_vma=False,
    )
```

profile of v0, /device:TPU:0, one launch (start us, length us, event | category | flops | bytes accessed | tf_op | source)
XLA Modules:
  0.0 133.1 jit_solution(4260292685797933428)
XLA Ops:
  2.3 1.3 copy.37.tok_ref
  3.9 2.9 %collective-permute-done.2.other_ref = f32[8,169]{1,0:T(8,128)S(1)} collective-permute-done((f32[8,169]{1,0:T(8,128)}, f32[8,169]{1,0:T(8,128)S(1)}, u32[]{:S(2)}, u32[]{:S(2)}) %collective-permute-start.2) | collective-permute-done | bytes 5440 | tf_op jit(solution)/shard_map/ppermute | solution.py:766
  7.1 1.5 %shard_map.271.bias_ref = f32[512,128]{1,0:T(8,128)S(1)} custom-call(s32[4]{0:T(128)S(1)} %pad_add_fusion.sel_ref.me_ref, f32[8,169]{1,0:T(8,128)S(1)} %bitcast.33, f32[8,169]{1,0:T(8,128)S(1)} %collective-permute-done.2.other_ref), custom_call_target="tpu_custom_call" | custom-call | flops 1000000000 | bytes 272960 | tf_op jit(solution)/shard_map/pallas_call | solution.py:586
  8.9 0.7 copy-done.25
  9.6 1.1 copy-done.26
  10.8 7.4 %shard_map.272 = (bf16[512,512]{1,0:T(8,128)(2,1)S(1)}, bf16[512,512]{1,0:T(8,128)(2,1)S(1)}, bf16[512,512]{1,0:T(8,128)(2,1)S(1)}, bf16[512,512]{1,0:T(8,128)(2...) custom-call(s32[4]{0:T(128)S(1)} %pad_add_fusion.sel_ref.me_ref, ...), custom_call_target="tpu_custom_call" | custom-call | flops 3000000000 | bytes 6583360 | tf_op jit(solution)/shard_map/pallas_call | solution.py:586
  18.3 6.8 %shard_map.273 = (bf16[512,1024]{1,0:T(8,128)(2,1)S(1)}, bf16[512,1024]{1,0:T(8,128)(2,1)S(1)}, f32[1,1024]{1,0:T(1,128)S(1)}, bf16[416,512]{1,0:T(8,128)(2,1)S(...) custom-call(s32[4]{0:T(128)S(1)} %pad_add_fusion.sel_ref.me_ref, ...), custom_call_target="tpu_custom_call" | custom-call | flops 3000000000 | bytes 9269248 | tf_op jit(solution)/shard_map/pallas_call | solution.py:586
  25.7 5.7 %shard_map.274 = (bf16[512,1024]{1,0:T(8,128)(2,1)S(1)}, bf16[512,1024]{1,0:T(8,128)(2,1)S(1)}, f32[1,1024]{1,0:T(1,128)S(1)}, bf16[4,196,512]{2,1,0:T(8,128)(2,...) custom-call(s32[4]{0:T(128)S(1)} %pad_add_fusion.sel_ref.me_ref, ...), custom_call_target="tpu_custom_call" | custom-call | flops 3000000000 | bytes 11343872 | tf_op jit(solution)/shard_map/pallas_call | solution.py:586
  31.4 0.9 copy-done.14
  32.3 10.2 %shard_map.275 = (bf16[512,512]{1,0:T(8,128)(2,1)S(1)}, bf16[512,512]{1,0:T(8,128)(2,1)S(1)}, bf16[512,512]{1,0:T(8,128)(2,1)S(1)}, bf16[512,512]{1,0:T(8,128)(2...) custom-call(s32[4]{0:T(128)S(1)} %pad_add_fusion.sel_ref.me_ref, ...), custom_call_target="tpu_custom_call" | custom-call | flops 5000000000 | bytes 8145984 | tf_op jit(solution)/shard_map/pallas_call | solution.py:586
  43.1 3.7 %shard_map.276 = (f32[4,196,512]{2,1,0:T(8,128)S(1)}, f32[2,196,512]{2,1,0:T(8,128)S(1)}, f32[24,512]{1,0:T(8,128)S(1)}, f32[24,512]{1,0:T(8,128)S(1)}) custom-call(s32[4]{0:T(128)S(1)} %pad_add_fusion.sel_ref.me_ref, bf16[4,196,512]{2,1,0:T(8,128)(2,1)S(1)} %copy.37.tok_ref, f32[416,512]{1,0:T(8,128)S(1)} %get-tuple-element.87.gres_ref, ...), custom_call_target="tpu_custom_call" | custom-call | flops 2000000000 | bytes 7612416 | tf_op jit(solution)/shard_map/pallas_call | solution.py:586
  47.1 1.5 %copy.41 = f32[2,196,512]{2,0,1:T(2,128)} copy(f32[2,196,512]{2,1,0:T(8,128)S(1)} %get-tuple-element.101) | data formatting | bytes 1605632 | tf_op jit(solution)/shard_map/pallas_call | solution.py:586
  49.4 3.8 %collective-permute-start.12 = (f32[24,512]{1,0:T(8,128)S(1)}, f32[24,512]{1,0:T(8,128)S(1)}, u32[]{:S(2)}, u32[]{:S(2)}) collective-permute-start(f32[24,512]{1,0:T(8,128)S(1)} %shard_map.277.a_ref), channel_id=1, source_target_pairs={{0,6},{2,4},{4,2},{6,0},{8,14},{10,12},{12,10},{14,8},{16,22},{18,... | collective-permute-start | bytes 147464 | tf_op jit(solution)/shard_map/ppermute | solution.py:611
  54.5 0.8 collective-permute-done.12.d_ref
  55.3 2.0 %collective-permute-start.11 = (f32[24,512]{1,0:T(8,128)S(1)}, f32[24,512]{1,0:T(8,128)S(1)}, u32[]{:S(2)}, u32[]{:S(2)}) collective-permute-start(f32[24,512]{1,0:T(8,128)S(1)} %shard_map.277.a_ref), channel_id=1, source_target_pairs={{0,4},{2,6},{4,0},{6,2},{8,12},{10,14},{12,8},{14,10},{16,20},{18,... | collective-permute-start | bytes 147464 | tf_op jit(solution)/shard_map/ppermute | solution.py:611
  57.3 2.1 %collective-permute-done.11.c_ref = f32[24,512]{1,0:T(8,128)S(1)} collective-permute-done((f32[24,512]{1,0:T(8,128)S(1)}, f32[24,512]{1,0:T(8,128)S(1)}, u32[]{:S(2)}, u32[]{:S(2)}) %collective-permute-start.11) | collective-permute-done | bytes 49184 | tf_op jit(solution)/shard_map/ppermute | solution.py:611
  59.4 2.4 %collective-permute-start.10 = (f32[24,512]{1,0:T(8,128)S(1)}, f32[24,512]{1,0:T(8,128)S(1)}, u32[]{:S(2)}, u32[]{:S(2)}) collective-permute-start(f32[24,512]{1,0:T(8,128)S(1)} %shard_map.277.a_ref), channel_id=1, source_target_pairs={{0,2},{2,0},{4,6},{6,4},{8,10},{10,8},{12,14},{14,12},{16,18},{18,... | collective-permute-start | bytes 147464 | tf_op jit(solution)/shard_map/ppermute | solution.py:611
  61.8 2.1 %collective-permute-done.10.b_ref = f32[24,512]{1,0:T(8,128)S(1)} collective-permute-done((f32[24,512]{1,0:T(8,128)S(1)}, f32[24,512]{1,0:T(8,128)S(1)}, u32[]{:S(2)}, u32[]{:S(2)}) %collective-permute-start.10) | collective-permute-done | bytes 49184 | tf_op jit(solution)/shard_map/ppermute | solution.py:611
  64.5 3.8 %collective-permute-start.15 = (f32[24,512]{1,0:T(8,128)S(1)}, f32[24,512]{1,0:T(8,128)S(1)}, u32[]{:S(2)}, u32[]{:S(2)}) collective-permute-start(f32[24,512]{1,0:T(8,128)S(1)} %shard_map.278.refs_0_), channel_id=1, source_target_pairs={{0,24},{2,26},{4,28},{6,30},{8,16},{10,18},{12,20},{14,22},{16,8},... | collective-permute-start | bytes 147464 | tf_op jit(solution)/shard_map/ppermute | solution.py:611
  68.3 1.8 %shard_map.284 = (bf16[256,1024]{1,0:T(8,128)(2,1)}, bf16[256,1024]{1,0:T(8,128)(2,1)}) custom-call(s32[4]{0:T(128)S(1)} %pad_add_fusion.sel_ref.me_ref, bf16[512,1024]{1,0:T(8,128)(2,1)S(1)} %get-tuple-element.125.refs_0_, bf16[512,1024]{1,0:T(8,128)(2,1)S(1)} %collective-permute-done.25.refs_1_, ...), custom_call_target="tpu_custom_call" | custom-call | flops 1000000 | bytes 5242880 | tf_op jit(solution)/shard_map/pallas_call | solution.py:586
  70.5 1.9 %collective-permute-start.27 = (bf16[256,1024]{1,0:T(8,128)(2,1)}, bf16[256,1024]{1,0:T(8,128)(2,1)}, u32[]{:S(2)}, u32[]{:S(2)}) collective-permute-start(bf16[256,1024]{1,0:T(8,128)(2,1)} %get-tuple-element.129), channel_id=1, source_target_pairs={{0,2},{2,0},{4,6},{6,4},{8,10},{10,8},{12,14},{14,12},{16,18},{18,... | collective-permute-start | bytes 1572872 | tf_op jit(solution)/shard_map/ppermute | solution.py:611
  72.4 0.8 collective-permute-done.14.refs_2_
  73.2 1.5 %collective-permute-start.28 = (bf16[256,1024]{1,0:T(8,128)(2,1)}, bf16[256,1024]{1,0:T(8,128)(2,1)}, u32[]{:S(2)}, u32[]{:S(2)}) collective-permute-start(bf16[256,1024]{1,0:T(8,128)(2,1)} %get-tuple-element.130), channel_id=1, source_target_pairs={{0,4},{2,6},{4,0},{6,2},{8,12},{10,14},{12,8},{14,10},{16,20},{18,... | collective-permute-start | bytes 1572872 | tf_op jit(solution)/shard_map/ppermute | solution.py:611
  75.3 16.6 %collective-permute-done.19.refs_5_.refs_6_ = bf16[256,512]{1,0:T(8,128)(2,1)S(1)} collective-permute-done((bf16[256,512]{1,0:T(8,128)(2,1)S(1)}, bf16[256,512]{1,0:T(8,128)(2,1)S(1)}, u32[]{:S(2)}, u32[]{:S(2)}) %collective-permute-start.19) | collective-permute-done | bytes 262176 | tf_op jit(solution)/shard_map/ppermute | solution.py:611
  91.8 0.8 collective-permute-start.13
  92.6 1.3 shard_map.281
  93.9 2.0 %collective-permute-done.13.refs_1_ = f32[24,512]{1,0:T(8,128)S(1)} collective-permute-done((f32[24,512]{1,0:T(8,128)S(1)}, f32[24,512]{1,0:T(8,128)S(1)}, u32[]{:S(2)}, u32[]{:S(2)}) %collective-permute-start.13) | collective-permute-done | bytes 49184 | tf_op jit(solution)/shard_map/ppermute | solution.py:611
  96.5 1.5 %collective-permute-start.20 = (bf16[128,512]{1,0:T(8,128)(2,1)}, bf16[128,512]{1,0:T(8,128)(2,1)}, u32[]{:S(2)}, u32[]{:S(2)}) collective-permute-start(bf16[128,512]{1,0:T(8,128)(2,1)} %get-tuple-element.112), channel_id=1, source_target_pairs={{0,4},{2,6},{4,0},{6,2},{8,12},{10,14},{12,8},{14,10},{16,20},{18,... | collective-permute-start | bytes 393224 | tf_op jit(solution)/shard_map/ppermute | solution.py:611
  98.0 0.8 copy-done.39
  99.1 0.8 copy-done.16
  99.9 0.8 copy-done.18
  100.7 1.2 shard_map.279
  101.9 1.8 %constant_dynamic-update-slice_fusion = bf16[4,196,512]{2,1,0:T(8,128)(2,1)} fusion(bf16[4,196,512]{2,1,0:T(8,128)(2,1)} %copy-done.14, bf16[2,196,512]{2,1,0:T(8,128)(2,1)} %copy-done.39, s32[]{:T(128)S(6)} %select_n.32), kind=kLoop, calls=%fused_computation.6 | loop fusion | bytes 819204 | tf_op jit(solution)/shard_map/dynamic_update_slice | solution.py:886
  103.7 2.4 %copy.43 = bf16[4,196,512]{2,0,1:T(4,128)(2,1)} copy(bf16[4,196,512]{2,1,0:T(8,128)(2,1)} %constant_dynamic-update-slice_fusion) | data formatting | bytes 1605632
  106.2 1.2 shard_map.282
  107.4 0.8 collective-permute-start.22
  108.2 2.2 %collective-permute-start.23 = (bf16[32,1024]{1,0:T(8,128)(2,1)S(1)}, bf16[32,1024]{1,0:T(8,128)(2,1)S(1)}, u32[]{:S(2)}, u32[]{:S(2)}) collective-permute-start(bf16[32,1024]{1,0:T(8,128)(2,1)S(1)} %get-tuple-element.116), channel_id=1, source_target_pairs={{0,16},{2,18},{4,20},{6,22},{8,24},{10,26},{12,28},{14,30},{16,0},... | collective-permute-start | bytes 196616 | tf_op jit(solution)/shard_map/ppermute | solution.py:611
  110.5 1.5 %collective-permute-start.24 = (bf16[32,1024]{1,0:T(8,128)(2,1)S(1)}, bf16[32,1024]{1,0:T(8,128)(2,1)S(1)}, u32[]{:S(2)}, u32[]{:S(2)}) collective-permute-start(bf16[32,1024]{1,0:T(8,128)(2,1)S(1)} %get-tuple-element.117), channel_id=1, source_target_pairs={{0,24},{2,26},{4,28},{6,30},{8,16},{10,18},{12,20},{14,22},{16,8},... | collective-permute-start | bytes 196616 | tf_op jit(solution)/shard_map/ppermute | solution.py:611
  111.9 1.4 %shard_map.285 = (bf16[128,1024]{1,0:T(8,128)(2,1)S(1)}, bf16[128,1024]{1,0:T(8,128)(2,1)S(1)}) custom-call(s32[4]{0:T(128)S(1)} %pad_add_fusion.sel_ref.me_ref, bf16[512,1024]{1,0:T(8,128)(2,1)S(1)} %get-tuple-element.125.refs_0_, bf16[512,1024]{1,0:T(8,128)(2,1)S(1)} %collective-permute-done.25.refs_1_, bf16[256,1024]{1,0:T(8,128)(2,1)} %collective-permute-done.27.refs_2_, ...), custom_call_target="tpu_custom_call" | custom-call | flops 1000000 | bytes 5767168 | tf_op jit(solution)/shard_map/pallas_call | solution.py:586
  114.0 1.7 %collective-permute-start.30 = (bf16[128,1024]{1,0:T(8,128)(2,1)S(1)}, bf16[128,1024]{1,0:T(8,128)(2,1)S(1)}, u32[]{:S(2)}, u32[]{:S(2)}) collective-permute-start(bf16[128,1024]{1,0:T(8,128)(2,1)S(1)} %get-tuple-element.132), channel_id=1, source_target_pairs={{0,2},{2,0},{4,6},{6,4},{8,10},{10,8},{12,14},{14,12},{16,18},{18,... | collective-permute-start | bytes 786440 | tf_op jit(solution)/shard_map/ppermute | solution.py:611
  115.6 1.4 %copy_dynamic-update-slice_fusion = f32[4,196,512]{2,1,0:T(8,128)S(1)} fusion(f32[4,196,512]{2,1,0:T(8,128)S(1)} %copy-done.11, s32[]{:T(128)S(6)} %select_n.32, f32[2,196,512]{2,0,1:T(2,128)} %collective-permute-done.8), kind=kLoop, calls=%fused_computation | loop fusion | bytes 1622020 | tf_op jit(solution)/shard_map/dynamic_update_slice | solution.py:938
  117.0 2.2 %copy.44 = f32[4,196,512]{2,0,1:T(4,128)} copy(f32[4,196,512]{2,1,0:T(8,128)S(1)} %copy_dynamic-update-slice_fusion) | data formatting | bytes 3211264
  120.3 1.7 %shard_map.286 = (bf16[32,2048]{1,0:T(8,128)(2,1)S(1)}, bf16[32,2048]{1,0:T(8,128)(2,1)S(1)}, bf16[32,2048]{1,0:T(8,128)(2,1)S(1)}, f32[32,2048]{1,0:T(8,128)S(1)}) custom-call(s32[4]{0:T(128)S(1)} %pad_add_fusion.sel_ref.me_ref, bf16[512,1024]{1,0:T(8,128)(2,1)S(1)} %get-tuple-element.125.refs_0_, bf16[512,1024]{1,0:T(8,128)(2,1)S(1)} %collective-permute-done.25.refs_1_, ...), custom_call_target="tpu_custom_call" | custom-call | flops 1000000 | bytes 6422528 | tf_op jit(solution)/shard_map/pallas_call | solution.py:586
  122.0 0.7 collective-permute-start.31
  122.7 2.3 %collective-permute-start.32 = (bf16[32,2048]{1,0:T(8,128)(2,1)S(1)}, bf16[32,2048]{1,0:T(8,128)(2,1)S(1)}, u32[]{:S(2)}, u32[]{:S(2)}) collective-permute-start(bf16[32,2048]{1,0:T(8,128)(2,1)S(1)} %get-tuple-element.135), channel_id=1, source_target_pairs={{0,16},{2,18},{4,20},{6,22},{8,24},{10,26},{12,28},{14,30},{16,0},... | collective-permute-start | bytes 393224 | tf_op jit(solution)/shard_map/ppermute | solution.py:611
  125.0 1.5 %collective-permute-start.33 = (bf16[32,2048]{1,0:T(8,128)(2,1)S(1)}, bf16[32,2048]{1,0:T(8,128)(2,1)S(1)}, u32[]{:S(2)}, u32[]{:S(2)}) collective-permute-start(bf16[32,2048]{1,0:T(8,128)(2,1)S(1)} %get-tuple-element.136), channel_id=1, source_target_pairs={{0,24},{2,26},{4,28},{6,30},{8,16},{10,18},{12,20},{14,22},{16,8},... | collective-permute-start | bytes 393224 | tf_op jit(solution)/shard_map/ppermute | solution.py:611
  128.2 3.7 %collective-permute-done.32.refs_1_ = bf16[32,2048]{1,0:T(8,128)(2,1)S(1)} collective-permute-done((bf16[32,2048]{1,0:T(8,128)(2,1)S(1)}, bf16[32,2048]{1,0:T(8,128)(2,1)S(1)}, u32[]{:S(2)}, u32[]{:S(2)}) %collective-permute-start.32) | collective-permute-done | bytes 131104 | tf_op jit(solution)/shard_map/ppermute | solution.py:611
  131.9 1.3 shard_map.287
  (128 shorter events, 12.1 us)
Async XLA Ops:
  0.7 8.9 %collective-permute-start = (bf16[3,512,256]{2,1,0:T(8,128)(2,1)}, bf16[3,512,256]{2,1,0:T(8,128)(2,1)S(1)}, u32[]{:S(2)}, u32[]{:S(2)}) collective-permute-start(bf16[3,512,256]{2,1,0:T(8,128)(2,1)} %bitcast.29), channel_id=1, source_target_pairs={{0,1},{1,0},{2,3},{3,2},{4,5},{5,4},{6,7},{7,6},{8,9},{9,8},{10,11... | collective-permute-start | bytes 2359304 | tf_op jit(solution)/shard_map/ppermute | solution.py:766
  1.2 17.0 %collective-permute-start.4 = (bf16[512,1024]{1,0:T(8,128)(2,1)}, bf16[512,1024]{1,0:T(8,128)(2,1)S(1)}, u32[]{:S(2)}, u32[]{:S(2)}) collective-permute-start(bf16[512,1024]{1,0:T(8,128)(2,1)} %w1_ref.1), channel_id=1, source_target_pairs={{0,1},{1,0},{2,3},{3,2},{4,5},{5,4},{6,7},{7,6},{8,9},{9,8},{10,11... | collective-permute-start | bytes 3145736 | tf_op jit(solution)/shard_map/ppermute | solution.py:766
  1.3 17.0 %collective-permute-start.5 = (bf16[512,1024]{1,0:T(8,128)(2,1)}, bf16[512,1024]{1,0:T(8,128)(2,1)}, u32[]{:S(2)}, u32[]{:S(2)}) collective-permute-start(bf16[512,1024]{1,0:T(8,128)(2,1)} %w2_ref.1), channel_id=1, source_target_pairs={{0,1},{1,0},{2,3},{3,2},{4,5},{5,4},{6,7},{7,6},{8,9},{9,8},{10,11... | collective-permute-start | bytes 3145736 | tf_op jit(solution)/shard_map/ppermute | solution.py:766
  1.7 7.2 %collective-permute-start.3 = (bf16[512,256]{1,0:T(8,128)(2,1)}, bf16[512,256]{1,0:T(8,128)(2,1)S(1)}, u32[]{:S(2)}, u32[]{:S(2)}) collective-permute-start(bf16[512,256]{1,0:T(8,128)(2,1)} %pm_ref.3), channel_id=1, source_target_pairs={{0,1},{1,0},{2,3},{3,2},{4,5},{5,4},{6,7},{7,6},{8,9},{9,8},{10,11... | collective-permute-start | bytes 786440 | tf_op jit(solution)/shard_map/ppermute | solution.py:766
  1.8 4.9 %collective-permute-start.2 = (f32[8,169]{1,0:T(8,128)}, f32[8,169]{1,0:T(8,128)S(1)}, u32[]{:S(2)}, u32[]{:S(2)}) collective-permute-start(f32[8,169]{1,0:T(8,128)} %bitcast.32), channel_id=1, source_target_pairs={{0,1},{1,0},{2,3},{3,2},{4,5},{5,4},{6,7},{7,6},{8,9},{9,8},{10,11... | collective-permute-start | bytes 16232 | tf_op jit(solution)/shard_map/ppermute | solution.py:766
  6.7 1.9 %collective-permute-start.1 = (f32[2,256]{1,0:T(2,128)S(1)}, f32[2,256]{1,0:T(2,128)S(1)}, u32[]{:S(2)}, u32[]{:S(2)}) collective-permute-start(f32[2,256]{1,0:T(2,128)S(1)} %copy-done.32), channel_id=1, source_target_pairs={{0,1},{1,0},{2,3},{3,2},{4,5},{5,4},{6,7},{7,6},{8,9},{9,8},{10,11... | collective-permute-start | bytes 6152 | tf_op jit(solution)/shard_map/ppermute | solution.py:766
  8.6 9.6 %collective-permute-start.6 = (f32[1,1024]{1,0:T(1,128)S(1)}, f32[1,1024]{1,0:T(1,128)S(1)}, u32[]{:S(2)}, u32[]{:S(2)}) collective-permute-start(f32[1,1024]{1,0:T(1,128)S(1)} %bitcast.34), channel_id=1, source_target_pairs={{0,1},{1,0},{2,3},{3,2},{4,5},{5,4},{6,7},{7,6},{8,9},{9,8},{10,11... | collective-permute-start | bytes 12296 | tf_op jit(solution)/shard_map/ppermute | solution.py:766
  9.6 8.6 %copy-start.22 = (bf16[3,512,256]{2,1,0:T(8,128)(2,1)}, bf16[3,512,256]{2,1,0:T(8,128)(2,1)S(1)}, u32[]{:S(2)}) copy-start(bf16[3,512,256]{2,1,0:T(8,128)(2,1)S(1)} %collective-permute-done.wo_ref) | copy-start | bytes 2359300
  10.8 7.5 %copy-start.34 = (f32[512]{0:T(512)S(1)}, f32[512]{0:T(512)}, u32[]{:S(2)}) copy-start(f32[512]{0:T(512)} %param.25) | copy-start | bytes 6148
  10.8 7.5 %copy-start.35 = (f32[512]{0:T(512)S(1)}, f32[512]{0:T(512)}, u32[]{:S(2)}) copy-start(f32[512]{0:T(512)} %param.26) | copy-start | bytes 6148
  18.3 7.4 %copy-start.19 = (bf16[512,1024]{1,0:T(8,128)(2,1)S(1)}, bf16[512,1024]{1,0:T(8,128)(2,1)}, u32[]{:S(2)}) copy-start(bf16[512,1024]{1,0:T(8,128)(2,1)} %w1_ref.1) | copy-start | bytes 3145732
  18.3 7.4 %copy-start.20 = (bf16[512,1024]{1,0:T(8,128)(2,1)S(1)}, bf16[512,1024]{1,0:T(8,128)(2,1)}, u32[]{:S(2)}) copy-start(bf16[512,1024]{1,0:T(8,128)(2,1)} %w2_ref.1) | copy-start | bytes 3145732
  18.3 7.4 %copy-start.36 = (f32[512]{0:T(512)S(1)}, f32[512]{0:T(512)}, u32[]{:S(2)}) copy-start(f32[512]{0:T(512)} %param.30) | copy-start | bytes 6148
  25.1 43.1 %collective-permute-start.25 = (bf16[512,1024]{1,0:T(8,128)(2,1)S(1)}, bf16[512,1024]{1,0:T(8,128)(2,1)S(1)}, u32[]{:S(2)}, u32[]{:S(2)}) collective-permute-start(bf16[512,1024]{1,0:T(8,128)(2,1)S(1)} %get-tuple-element.126), channel_id=1, source_target_pairs={{0,1},{1,0},{2,3},{3,2},{4,5},{5,4},{6,7},{7,6},{8,9},{9,8},{10,11... | collective-permute-start | bytes 3145736 | tf_op jit(solution)/shard_map/ppermute | solution.py:766
  25.5 42.7 %collective-permute-start.26 = (bf16[512,1024]{1,0:T(8,128)(2,1)S(1)}, bf16[512,1024]{1,0:T(8,128)(2,1)S(1)}, u32[]{:S(2)}, u32[]{:S(2)}) collective-permute-start(bf16[512,1024]{1,0:T(8,128)(2,1)S(1)} %get-tuple-element.128), channel_id=1, source_target_pairs={{0,1},{1,0},{2,3},{3,2},{4,5},{5,4},{6,7},{7,6},{8,9},{9,8},{10,11... | collective-permute-start | bytes 3145736 | tf_op jit(solution)/shard_map/ppermute | solution.py:766
  32.3 36.1 %copy-start = (bf16[512,1024]{1,0:T(8,128)(2,1)}, bf16[512,1024]{1,0:T(8,128)(2,1)S(1)}, u32[]{:S(2)}) copy-start(bf16[512,1024]{1,0:T(8,128)(2,1)S(1)} %get-tuple-element.127.refs_2_.refs_3_.refs_4_) | copy-start | bytes 3145732
  32.3 10.8 %copy-start.23 = (bf16[3,512,256]{2,1,0:T(8,128)(2,1)S(1)}, bf16[3,512,256]{2,1,0:T(8,128)(2,1)}, u32[]{:S(2)}) copy-start(bf16[3,512,256]{2,1,0:T(8,128)(2,1)} %copy-done.22) | copy-start | bytes 2359300
  42.5 50.1 %copy-start.2 = (bf16[512,512]{1,0:T(8,128)(2,1)}, bf16[512,512]{1,0:T(8,128)(2,1)S(1)}, u32[]{:S(2)}) copy-start(bf16[512,512]{1,0:T(8,128)(2,1)S(1)} %get-tuple-element.106.refs_0_) | copy-start | bytes 1572868
  42.5 50.1 %copy-start.4 = (bf16[512,512]{1,0:T(8,128)(2,1)}, bf16[512,512]{1,0:T(8,128)(2,1)S(1)}, u32[]{:S(2)}) copy-start(bf16[512,512]{1,0:T(8,128)(2,1)S(1)} %get-tuple-element.108.refs_2_.refs_3_.refs_4_) | copy-start | bytes 1572868
  42.5 6.9 %collective-permute-start.16 = (bf16[512,512]{1,0:T(8,128)(2,1)S(1)}, bf16[512,512]{1,0:T(8,128)(2,1)S(1)}, u32[]{:S(2)}, u32[]{:S(2)}) collective-permute-start(bf16[512,512]{1,0:T(8,128)(2,1)S(1)} %get-tuple-element.107), channel_id=1, source_target_pairs={{0,1},{1,0},{2,3},{3,2},{4,5},{5,4},{6,7},{7,6},{8,9},{9,8},{10,11... | collective-permute-start | bytes 1572872 | tf_op jit(solution)/shard_map/ppermute | solution.py:766
  42.9 10.3 %collective-permute-start.17 = (bf16[512,512]{1,0:T(8,128)(2,1)S(1)}, bf16[512,512]{1,0:T(8,128)(2,1)S(1)}, u32[]{:S(2)}, u32[]{:S(2)}) collective-permute-start(bf16[512,512]{1,0:T(8,128)(2,1)S(1)} %get-tuple-element.109), channel_id=1, source_target_pairs={{0,1},{1,0},{2,3},{3,2},{4,5},{5,4},{6,7},{7,6},{8,9},{9,8},{10,11... | collective-permute-start | bytes 1572872 | tf_op jit(solution)/shard_map/ppermute | solution.py:766
  46.8 7.1 %copy-start.10 = (f32[4,196,512]{2,1,0:T(8,128)}, f32[4,196,512]{2,1,0:T(8,128)S(1)}, u32[]{:S(2)}) copy-start(f32[4,196,512]{2,1,0:T(8,128)S(1)} %get-tuple-element.100) | copy-start | bytes 4816900
  46.8 1.9 %collective-permute-start.9 = (f32[24,512]{1,0:T(8,128)S(1)}, f32[24,512]{1,0:T(8,128)S(1)}, u32[]{:S(2)}, u32[]{:S(2)}) collective-permute-start(f32[24,512]{1,0:T(8,128)S(1)} %get-tuple-element.103), channel_id=1, source_target_pairs={{0,1},{1,0},{2,3},{3,2},{4,5},{5,4},{6,7},{7,6},{8,9},{9,8},{10,11... | collective-permute-start | bytes 147464 | tf_op jit(solution)/shard_map/ppermute | solution.py:766
  48.6 65.3 %collective-permute-start.8 = (f32[2,196,512]{2,0,1:T(2,128)}, f32[2,196,512]{2,0,1:T(2,128)}, u32[]{:S(2)}, u32[]{:S(2)}) collective-permute-start(f32[2,196,512]{2,0,1:T(2,128)} %copy.41), channel_id=1, source_target_pairs={{0,1},{1,0},{2,3},{3,2},{4,5},{5,4},{6,7},{7,6},{8,9},{9,8},{10,11... | collective-permute-start | bytes 2408456 | tf_op jit(solution)/shard_map/ppermute | solution.py:766
  49.4 43.2 %copy-start.6 = (bf16[512,512]{1,0:T(8,128)(2,1)}, bf16[512,512]{1,0:T(8,128)(2,1)S(1)}, u32[]{:S(2)}) copy-start(bf16[512,512]{1,0:T(8,128)(2,1)S(1)} %collective-permute-done.16.refs_1_) | copy-start | bytes 1572868
  49.4 5.9 %collective-permute-start.12 = (f32[24,512]{1,0:T(8,128)S(1)}, f32[24,512]{1,0:T(8,128)S(1)}, u32[]{:S(2)}, u32[]{:S(2)}) collective-permute-start(f32[24,512]{1,0:T(8,128)S(1)} %shard_map.277.a_ref), channel_id=1, source_target_pairs={{0,6},{2,4},{4,2},{6,0},{8,14},{10,12},{12,10},{14,8},{16,22},{18,... | collective-permute-start | bytes 147464 | tf_op jit(solution)/shard_map/ppermute | solution.py:611
  53.2 39.4 %copy-start.8 = (bf16[512,512]{1,0:T(8,128)(2,1)}, bf16[512,512]{1,0:T(8,128)(2,1)S(1)}, u32[]{:S(2)}) copy-start(bf16[512,512]{1,0:T(8,128)(2,1)S(1)} %collective-permute-done.17.refs_3_.refs_4_.refs_5_) | copy-start | bytes 1572868
  53.9 20.8 %collective-permute-start.18 = (bf16[256,512]{1,0:T(8,128)(2,1)S(1)}, bf16[256,512]{1,0:T(8,128)(2,1)S(1)}, u32[]{:S(2)}, u32[]{:S(2)}) collective-permute-start(bf16[256,512]{1,0:T(8,128)(2,1)S(1)} %get-tuple-element.110), channel_id=1, source_target_pairs={{0,2},{2,0},{4,6},{6,4},{8,10},{10,8},{12,14},{14,12},{16,18},{18,... | collective-permute-start | bytes 786440 | tf_op jit(solution)/shard_map/ppermute | solution.py:611
  55.3 4.1 %collective-permute-start.11 = (f32[24,512]{1,0:T(8,128)S(1)}, f32[24,512]{1,0:T(8,128)S(1)}, u32[]{:S(2)}, u32[]{:S(2)}) collective-permute-start(f32[24,512]{1,0:T(8,128)S(1)} %shard_map.277.a_ref), channel_id=1, source_target_pairs={{0,4},{2,6},{4,0},{6,2},{8,12},{10,14},{12,8},{14,10},{16,20},{18,... | collective-permute-start | bytes 147464 | tf_op jit(solution)/shard_map/ppermute | solution.py:611
  59.4 4.5 %collective-permute-start.10 = (f32[24,512]{1,0:T(8,128)S(1)}, f32[24,512]{1,0:T(8,128)S(1)}, u32[]{:S(2)}, u32[]{:S(2)}) collective-permute-start(f32[24,512]{1,0:T(8,128)S(1)} %shard_map.277.a_ref), channel_id=1, source_target_pairs={{0,2},{2,0},{4,6},{6,4},{8,10},{10,8},{12,14},{14,12},{16,18},{18,... | collective-permute-start | bytes 147464 | tf_op jit(solution)/shard_map/ppermute | solution.py:611
  64.5 6.1 %collective-permute-start.15 = (f32[24,512]{1,0:T(8,128)S(1)}, f32[24,512]{1,0:T(8,128)S(1)}, u32[]{:S(2)}, u32[]{:S(2)}) collective-permute-start(f32[24,512]{1,0:T(8,128)S(1)} %shard_map.278.refs_0_), channel_id=1, source_target_pairs={{0,24},{2,26},{4,28},{6,30},{8,16},{10,18},{12,20},{14,22},{16,8},... | collective-permute-start | bytes 147464 | tf_op jit(solution)/shard_map/ppermute | solution.py:611
  68.2 5.0 %collective-permute-start.14 = (f32[24,512]{1,0:T(8,128)S(1)}, f32[24,512]{1,0:T(8,128)S(1)}, u32[]{:S(2)}, u32[]{:S(2)}) collective-permute-start(f32[24,512]{1,0:T(8,128)S(1)} %shard_map.278.refs_0_), channel_id=1, source_target_pairs={{0,16},{2,18},{4,20},{6,22},{8,24},{10,26},{12,28},{14,30},{16,0},... | collective-permute-start | bytes 147464 | tf_op jit(solution)/shard_map/ppermute | solution.py:611
  68.3 29.7 %collective-permute-start.7 = (bf16[2,196,512]{2,1,0:T(8,128)(2,1)S(1)}, bf16[2,196,512]{2,1,0:T(8,128)(2,1)S(1)}, u32[]{:S(2)}, u32[]{:S(2)}) collective-permute-start(bf16[2,196,512]{2,1,0:T(8,128)(2,1)S(1)} %get-tuple-element.86), channel_id=1, source_target_pairs={{0,1},{1,0},{2,3},{3,2},{4,5},{5,4},{6,7},{7,6},{8,9},{9,8},{10,11... | collective-permute-start | bytes 1204232 | tf_op jit(solution)/shard_map/ppermute | solution.py:766
  70.5 39.9 %collective-permute-start.27 = (bf16[256,1024]{1,0:T(8,128)(2,1)}, bf16[256,1024]{1,0:T(8,128)(2,1)}, u32[]{:S(2)}, u32[]{:S(2)}) collective-permute-start(bf16[256,1024]{1,0:T(8,128)(2,1)} %get-tuple-element.129), channel_id=1, source_target_pairs={{0,2},{2,0},{4,6},{6,4},{8,10},{10,8},{12,14},{14,12},{16,18},{18,... | collective-permute-start | bytes 1572872 | tf_op jit(solution)/shard_map/ppermute | solution.py:611
  73.2 22.7 %copy-start.15 = (f32[24,512]{1,0:T(8,128)}, f32[24,512]{1,0:T(8,128)S(1)}, u32[]{:S(2)}) copy-start(f32[24,512]{1,0:T(8,128)S(1)} %collective-permute-done.14.refs_2_) | copy-start | bytes 147460
  73.2 38.7 %collective-permute-start.28 = (bf16[256,1024]{1,0:T(8,128)(2,1)}, bf16[256,1024]{1,0:T(8,128)(2,1)}, u32[]{:S(2)}, u32[]{:S(2)}) collective-permute-start(bf16[256,1024]{1,0:T(8,128)(2,1)} %get-tuple-element.130), channel_id=1, source_target_pairs={{0,4},{2,6},{4,0},{6,2},{8,12},{10,14},{12,8},{14,10},{16,20},{18,... | collective-permute-start | bytes 1572872 | tf_op jit(solution)/shard_map/ppermute | solution.py:611
  74.8 17.1 %collective-permute-start.19 = (bf16[256,512]{1,0:T(8,128)(2,1)S(1)}, bf16[256,512]{1,0:T(8,128)(2,1)S(1)}, u32[]{:S(2)}, u32[]{:S(2)}) collective-permute-start(bf16[256,512]{1,0:T(8,128)(2,1)S(1)} %get-tuple-element.111), channel_id=1, source_target_pairs={{0,4},{2,6},{4,0},{6,2},{8,12},{10,14},{12,8},{14,10},{16,20},{18,... | collective-permute-start | bytes 786440 | tf_op jit(solution)/shard_map/ppermute | solution.py:611
  91.8 4.1 %collective-permute-start.13 = (f32[24,512]{1,0:T(8,128)S(1)}, f32[24,512]{1,0:T(8,128)S(1)}, u32[]{:S(2)}, u32[]{:S(2)}) collective-permute-start(f32[24,512]{1,0:T(8,128)S(1)} %shard_map.278.refs_0_), channel_id=1, source_target_pairs={{0,8},{2,10},{4,12},{6,14},{8,0},{10,2},{12,4},{14,6},{16,24},{18,... | collective-permute-start | bytes 147464 | tf_op jit(solution)/shard_map/ppermute | solution.py:611
  96.5 9.6 %collective-permute-start.20 = (bf16[128,512]{1,0:T(8,128)(2,1)}, bf16[128,512]{1,0:T(8,128)(2,1)}, u32[]{:S(2)}, u32[]{:S(2)}) collective-permute-start(bf16[128,512]{1,0:T(8,128)(2,1)} %get-tuple-element.112), channel_id=1, source_target_pairs={{0,4},{2,6},{4,0},{6,2},{8,12},{10,14},{12,8},{14,10},{16,20},{18,... | collective-permute-start | bytes 393224 | tf_op jit(solution)/shard_map/ppermute | solution.py:611
  98.7 7.4 %collective-permute-start.21 = (bf16[128,512]{1,0:T(8,128)(2,1)}, bf16[128,512]{1,0:T(8,128)(2,1)}, u32[]{:S(2)}, u32[]{:S(2)}) collective-permute-start(bf16[128,512]{1,0:T(8,128)(2,1)} %get-tuple-element.113), channel_id=1, source_target_pairs={{0,2},{2,0},{4,6},{6,4},{8,10},{10,8},{12,14},{14,12},{16,18},{18,... | collective-permute-start | bytes 393224 | tf_op jit(solution)/shard_map/ppermute | solution.py:611
  107.4 11.8 %collective-permute-start.22 = (bf16[32,1024]{1,0:T(8,128)(2,1)S(1)}, bf16[32,1024]{1,0:T(8,128)(2,1)S(1)}, u32[]{:S(2)}, u32[]{:S(2)}) collective-permute-start(bf16[32,1024]{1,0:T(8,128)(2,1)S(1)} %get-tuple-element.115), channel_id=1, source_target_pairs={{0,8},{2,10},{4,12},{6,14},{8,0},{10,2},{12,4},{14,6},{16,24},{18,... | collective-permute-start | bytes 196616 | tf_op jit(solution)/shard_map/ppermute | solution.py:611
  108.2 11.0 %collective-permute-start.23 = (bf16[32,1024]{1,0:T(8,128)(2,1)S(1)}, bf16[32,1024]{1,0:T(8,128)(2,1)S(1)}, u32[]{:S(2)}, u32[]{:S(2)}) collective-permute-start(bf16[32,1024]{1,0:T(8,128)(2,1)S(1)} %get-tuple-element.116), channel_id=1, source_target_pairs={{0,16},{2,18},{4,20},{6,22},{8,24},{10,26},{12,28},{14,30},{16,0},... | collective-permute-start | bytes 196616 | tf_op jit(solution)/shard_map/ppermute | solution.py:611
  110.5 8.8 %collective-permute-start.24 = (bf16[32,1024]{1,0:T(8,128)(2,1)S(1)}, bf16[32,1024]{1,0:T(8,128)(2,1)S(1)}, u32[]{:S(2)}, u32[]{:S(2)}) collective-permute-start(bf16[32,1024]{1,0:T(8,128)(2,1)S(1)} %get-tuple-element.117), channel_id=1, source_target_pairs={{0,24},{2,26},{4,28},{6,30},{8,16},{10,18},{12,20},{14,22},{16,8},... | collective-permute-start | bytes 196616 | tf_op jit(solution)/shard_map/ppermute | solution.py:611
  113.3 6.5 %collective-permute-start.29 = (bf16[128,1024]{1,0:T(8,128)(2,1)S(1)}, bf16[128,1024]{1,0:T(8,128)(2,1)S(1)}, u32[]{:S(2)}, u32[]{:S(2)}) collective-permute-start(bf16[128,1024]{1,0:T(8,128)(2,1)S(1)} %get-tuple-element.131), channel_id=1, source_target_pairs={{0,4},{2,6},{4,0},{6,2},{8,12},{10,14},{12,8},{14,10},{16,20},{18,... | collective-permute-start | bytes 786440 | tf_op jit(solution)/shard_map/ppermute | solution.py:611
  114.0 6.4 %collective-permute-start.30 = (bf16[128,1024]{1,0:T(8,128)(2,1)S(1)}, bf16[128,1024]{1,0:T(8,128)(2,1)S(1)}, u32[]{:S(2)}, u32[]{:S(2)}) collective-permute-start(bf16[128,1024]{1,0:T(8,128)(2,1)S(1)} %get-tuple-element.132), channel_id=1, source_target_pairs={{0,2},{2,0},{4,6},{6,4},{8,10},{10,8},{12,14},{14,12},{16,18},{18,... | collective-permute-start | bytes 786440 | tf_op jit(solution)/shard_map/ppermute | solution.py:611
  122.0 6.2 %collective-permute-start.31 = (bf16[32,2048]{1,0:T(8,128)(2,1)S(1)}, bf16[32,2048]{1,0:T(8,128)(2,1)S(1)}, u32[]{:S(2)}, u32[]{:S(2)}) collective-permute-start(bf16[32,2048]{1,0:T(8,128)(2,1)S(1)} %get-tuple-element.134), channel_id=1, source_target_pairs={{0,8},{2,10},{4,12},{6,14},{8,0},{10,2},{12,4},{14,6},{16,24},{18,... | collective-permute-start | bytes 393224 | tf_op jit(solution)/shard_map/ppermute | solution.py:611
  122.7 9.1 %collective-permute-start.32 = (bf16[32,2048]{1,0:T(8,128)(2,1)S(1)}, bf16[32,2048]{1,0:T(8,128)(2,1)S(1)}, u32[]{:S(2)}, u32[]{:S(2)}) collective-permute-start(bf16[32,2048]{1,0:T(8,128)(2,1)S(1)} %get-tuple-element.135), channel_id=1, source_target_pairs={{0,16},{2,18},{4,20},{6,22},{8,24},{10,26},{12,28},{14,30},{16,0},... | collective-permute-start | bytes 393224 | tf_op jit(solution)/shard_map/ppermute | solution.py:611
  125.0 6.8 %collective-permute-start.33 = (bf16[32,2048]{1,0:T(8,128)(2,1)S(1)}, bf16[32,2048]{1,0:T(8,128)(2,1)S(1)}, u32[]{:S(2)}, u32[]{:S(2)}) collective-permute-start(bf16[32,2048]{1,0:T(8,128)(2,1)S(1)} %get-tuple-element.136), channel_id=1, source_target_pairs={{0,24},{2,26},{4,28},{6,30},{8,16},{10,18},{12,20},{14,22},{16,8},... | collective-permute-start | bytes 393224 | tf_op jit(solution)/shard_map/ppermute | solution.py:611
  (26 other events, 104.6 us)
where the time goes:
time: 134 us; the launch traced here: 133 us
  Pallas kernels  47.4 us (35%)
  starting transfers between devices  34.3 us (26%)
  waiting for transfers between devices  32.3 us (24%)
  local copies, waits for them, and re-layouts  17.2 us (13%)
    pallas_call x17, Pallas kernels, call(): pl.pallas_call(kernel, in_specs=[pl.BlockSpec(memory_space=pltpu.SMEM)] +...  47.4 us
    ppermute x20, starting transfers between devices, xor_exchange(): return lax.ppermute(value, axis, [(i, i ^ mask) for i in range(count)])  30.3 us
    ppermute x20, waiting for transfers between devices, xor_exchange(): return lax.ppermute(value, axis, [(i, i ^ mask) for i in range(count)])  29.4 us
    unnamed x84, local copies, waits for them, and re-layouts  11.9 us
    ppermute x14, starting transfers between devices, swap(): return lax.ppermute(value, 'tensor', [(i, i ^ 1) for i in range(n_tensor)])  3.96 us
    ppermute x14, waiting for transfers between devices, swap(): return lax.ppermute(value, 'tensor', [(i, i ^ 1) for i in range(n_tensor)])  2.9 us
  transfers between devices with their start and end apart: 34, of which 11 were waited for; matrix products, arithmetic and copies ran while one was open for 9% of the time, Pallas kernels for 28%

commit v1 on v0

--- a/solution.py
+++ b/solution.py
@@ -99,6 +99,18 @@
         block = block + (rest & (size - 1)) * stride
         rest = rest >> log2(size)
     return block * rows + (slot & (rows - 1))
+
+
+def put_rows(out_ref, layout, col, value):
+    rows = layout[0]
+    cols = slice(col, col + value.shape[1])
+    value = value.astype(out_ref.dtype)
+    sources = [row_order(at, *layout) for at in range(0, value.shape[0], rows)]
+    if sources == sorted(sources):
+        out_ref[:, cols] = value
+        return
+    for place, source in enumerate(sources):
+        out_ref[place * rows : (place + 1) * rows, cols] = value[source : source + rows]
 
 
 def order_matrix(width, layout):
@@ -248,7 +260,7 @@
         att_ref[rows, :] = own_groups(tn(probs, v_all)).astype(BF16)
         return carry
 
-    lax.fori_loop(0, images * WINS, one_window, 0)
+    lax.fori_loop(0, images * WINS, one_window, 0, unroll=2)
     back = scatter_matrix()
     for image in range(images):
         merged_ref[image * TPAD : (image + 1) * TPAD, :] = nn(
@@ -311,7 +323,7 @@
         g1_ref[:, cols] = nn(lnt_ref[...], grad_pre).astype(BF16)
         return carry
 
-    lax.fori_loop(0, w1_ref.shape[1] // chunk, one_chunk, 0)
+    lax.fori_loop(0, w1_ref.shape[1] // chunk, one_chunk, 0, unroll=True)
     if not last:
         return
     resid = resid_ref[...]
@@ -369,10 +381,8 @@
     mask_ref[...] = head_mask(heads)
     gres = gres_ref[...]
     gres_b = gres.astype(BF16)
-    width = gres.shape[1]
-    gres_t = nt(order_matrix(width, layouts[1]), gres_b).astype(BF16)
-    gvpm_ref[:, chan:] = nn(gres_t, merged_ref[:, :chan]).astype(BF16)
-    gvpo_ref[:, chan:] = nn(gres_t, merged_ref[:, chan:]).astype(BF16)
+    put_rows(gvpm_ref, layouts[1], chan, tn(gres_b, merged_ref[:, :chan]))
+    put_rows(gvpo_ref, layouts[1], chan, tn(gres_b, merged_ref[:, chan:]))
     grad_m = jnp.concatenate(
         [nn(gres_b, pm_ref[...]).astype(BF16), nn(gres_b, po_ref[...]).astype(BF16)], axis=1
     )
@@ -421,16 +431,15 @@
             gqkv_ref[rows, base + 2 * chan : base + 3 * chan] = g_v[:, cols].astype(BF16)
         return carry
 
-    lax.fori_loop(0, images * WINS, one_window, 0)
+    lax.fori_loop(0, images * WINS, one_window, 0, unroll=2)
     sums_ref[...] = jnp.zeros(sums_ref.shape, F32)
     sums_ref[0:1, :] = jnp.sum(qsum_ref[...], axis=0, keepdims=True)
     sums_ref[1:2, :] = jnp.sum(vsum_ref[...], axis=0, keepdims=True)
-    win_a = nt(order_matrix(width, layouts[0]), win_ref[...]).astype(BF16)
-    win_b = nt(order_matrix(width, layouts[1]), win_ref[...]).astype(BF16)
-    gqko_ref[...] = nn(win_a, gqkv_ref[:, 3 * chan : 5 * chan]).astype(BF16)
-    gvpo_ref[:, :chan] = nn(win_b, gqkv_ref[:, 5 * chan :]).astype(BF16)
-    gqkm_ref[...] = nn(win_a, gqkv_ref[:, : 2 * chan]).astype(BF16)
-    gvpm_ref[:, :chan] = nn(win_b, gqkv_ref[:, 2 * chan : 3 * chan]).astype(BF16)
+    win = win_ref[...]
+    put_rows(gqko_ref, layouts[0], 0, tn(win, gqkv_ref[:, 3 * chan : 5 * chan]))
+    put_rows(gvpo_ref, layouts[1], 0, tn(win, gqkv_ref[:, 5 * chan :]))
+    put_rows(gqkm_ref, layouts[0], 0, tn(win, gqkv_ref[:, : 2 * chan]))
+    put_rows(gvpm_ref, layouts[1], 0, tn(win, gqkv_ref[:, 2 * chan : 3 * chan]))
 
 
 def last_kernel(
@@ -498,10 +507,14 @@
         pack_ref[0:4, :] = two_ref[0:4, :]
         pack_ref[4:5, :] = gain_sum
         pack_ref[5:6, :] = shift_sum
-        pack_ref[6:8, :chan] = qv_ref[0:2, group * chan : (group + 1) * chan]
+        pack_ref[6:7, :chan] = qv_ref[0:1, group * chan : (group + 1) * chan]
+        pack_ref[6:7, chan:] = qv_ref[1:2, group * chan : (group + 1) * chan]
         for at in range(gb_ref.shape[1] // width):
-            pack_ref[8 + at : 9 + at, :] = gb_ref[:, at * width : (at + 1) * width]
-        pack_ref[16 : 16 + heads, :rows_half] = table[:, group * rows_half : (group + 1) * rows_half]
+            pack_ref[7 + at : 8 + at, :] = gb_ref[:, at * width : (at + 1) * width]
+        half = table[:, group * rows_half : (group + 1) * rows_half]
+        low = pack_ref.shape[0] - heads // 2
+        pack_ref[low:, :rows_half] = half[: heads // 2]
+        pack_ref[low:, chan : chan + rows_half] = half[heads // 2 :]
 
 
 def unpack_kernel(parts, sel_ref, *refs):
@@ -513,11 +526,15 @@
     for at in range(6):
         outs[at][...] = total[at : at + 1]
     qv_ref, b1_ref, table_ref = outs[6:]
-    qv_ref[...] = total[6:8, : qv_ref.shape[1]]
+    chan, (heads, entries) = qv_ref.shape[1], table_ref.shape
+    qv_ref[0:1, :] = total[6:7, :chan]
+    qv_ref[1:2, :] = total[6:7, chan:]
     width = total.shape[1]
     for at in range(b1_ref.shape[1] // width):
-        b1_ref[:, at * width : (at + 1) * width] = total[8 + at : 9 + at]
-    table_ref[...] = total[16 : 16 + table_ref.shape[0], : table_ref.shape[1]]
+        b1_ref[:, at * width : (at + 1) * width] = total[7 + at : 8 + at]
+    low = total.shape[0] - heads // 2
+    table_ref[: heads // 2, :] = total[low:, :entries]
+    table_ref[heads // 2 :, :] = total[low:, chan : chan + entries]
 
 
 def row_block(ref, sel_ref, blocks, form):
@@ -644,7 +661,9 @@
     mask = 1
     while True:
         size = 4 if 4 * mask <= count else 2
-        terms = [value] + [xor_exchange(value, axis, count, s * mask) for s in range(1, size)]
+        terms = [value]
+        for s in range(1, size):
+            terms.append(xor_exchange(value, axis, count, s * mask))
         mask *= size
         if mask >= count:
             return terms
@@ -711,7 +730,9 @@
         10**6,
         6,
     )
-    received = [xor_exchange(send, axis, count, s * stride_z) for s, send in enumerate(sends, 1)]
+    received = []
+    for s, send in enumerate(sends, 1):
+        received.append(xor_exchange(send, axis, count, s * stride_z))
     half = a0.shape[1]
     outs = (struct((rows, half), F32), struct((rows, cols - half), F32))
     return call(total_kernel, sel, [own] + received, outs, [], 10**6, 4)
@@ -920,7 +941,7 @@
     sent_proj = sent_vp[:, chan:]
 
     ins = (tokens, gres, gqkv, wm, wo, row(norm1_gain), gbias, sums_two, sums_qv, gbm, gbo)
-    pack = struct((16 + heads, width), F32)
+    pack = struct((-(-(7 + hidden // width + heads // 2) // 8) * 8, width), F32)
     outs = (struct(tokens.shape, F32), struct((images, TOK, width), F32), pack, pack)
     grad_full, grad_half, small, theirs = call(
         functools.partial(last_kernel, images, heads, half_rows),

time: 134 us -> 136 us (1.015)
  waiting for transfers between devices: 32.3 us -> 39.9 us
  Pallas kernels: 47.4 us -> 44 us
  starting transfers between devices: 34.3 us -> 30.9 us
  local copies, waits for them, and re-layouts: 17.2 us -> 18.7 us
    ppermute x20, waiting for transfers between devices: 29.4 us -> 35.9 us  [xor_exchange(): return lax.ppermute(value, axis, [(i, i ^ mask) for i in range(count)])]
    pallas_call x17, Pallas kernels: 47.4 us -> 44 us  [call(): pl.pallas_call(kernel, in_specs=[pl.BlockSpec(memory_space=pltpu.SMEM)] +...]
    ppermute x20, starting transfers between devices: 30.3 us -> 27 us  [xor_exchange(): return lax.ppermute(value, axis, [(i, i ^ mask) for i in range(count)])]
    unnamed x84 -> x92, local copies, waits for them, and re-layouts: 11.9 us -> 13.3 us
  transfers between devices with their start and end apart: 34 -> 34, of which waited for: 11 -> 13; matrix products, arithmetic and copies ran while one was open for 9% -> 9% of each run, Pallas kernels for 28% -> 26%
where the time goes in v1:
time: 136 us; the launch traced here: 135 us
  Pallas kernels  44 us (32%)
  waiting for transfers between devices  39.9 us (29%)
  starting transfers between devices  30.9 us (23%)
  local copies, waits for them, and re-layouts  18.7 us (14%)
    pallas_call x17, Pallas kernels, call(): pl.pallas_call(kernel, in_specs=[pl.BlockSpec(memory_space=pltpu.SMEM)] +...  44 us
    ppermute x20, waiting for transfers between devices, xor_exchange(): return lax.ppermute(value, axis, [(i, i ^ mask) for i in range(count)])  35.9 us
    ppermute x20, starting transfers between devices, xor_exchange(): return lax.ppermute(value, axis, [(i, i ^ mask) for i in range(count)])  27 us
    unnamed x92, local copies, waits for them, and re-layouts  13.3 us
    ppermute x14, waiting for transfers between devices, swap(): return lax.ppermute(value, 'tensor', [(i, i ^ 1) for i in range(n_tensor)])  4.01 us
    ppermute x14, starting transfers between devices, swap(): return lax.ppermute(value, 'tensor', [(i, i ^ 1) for i in range(n_tensor)])  3.85 us
  transfers between devices with their start and end apart: 34, of which 13 were waited for; matrix products, arithmetic and copies ran while one was open for 9% of the time, Pallas kernels for 26%

profile of v1, /device:TPU:0, one launch (start us, length us, event | category | flops | bytes accessed | tf_op | source)
XLA Modules:
  0.0 135.3 jit_solution(13914643925697586711)
XLA Ops:
  2.3 1.3 copy.37.tok_ref
  3.9 2.9 %collective-permute-done.2.other_ref = f32[8,169]{1,0:T(8,128)S(1)} collective-permute-done((f32[8,169]{1,0:T(8,128)}, f32[8,169]{1,0:T(8,128)S(1)}, u32[]{:S(2)}, u32[]{:S(2)}) %collective-permute-start.2) | collective-permute-done | bytes 5440 | tf_op jit(solution)/shard_map/ppermute | solution.py:787
  7.1 1.5 %shard_map.271.bias_ref = f32[512,128]{1,0:T(8,128)S(1)} custom-call(s32[4]{0:T(128)S(1)} %pad_add_fusion.sel_ref.me_ref, f32[8,169]{1,0:T(8,128)S(1)} %bitcast.33, f32[8,169]{1,0:T(8,128)S(1)} %collective-permute-done.2.other_ref), custom_call_target="tpu_custom_call" | custom-call | flops 1000000000 | bytes 272960 | tf_op jit(solution)/shard_map/pallas_call | solution.py:603
  9.6 1.1 copy-done.30
  10.8 7.0 %shard_map.272 = (bf16[512,512]{1,0:T(8,128)(2,1)S(1)}, bf16[512,512]{1,0:T(8,128)(2,1)S(1)}, bf16[512,512]{1,0:T(8,128)(2,1)S(1)}, bf16[512,512]{1,0:T(8,128)(2...) custom-call(s32[4]{0:T(128)S(1)} %pad_add_fusion.sel_ref.me_ref, ...), custom_call_target="tpu_custom_call" | custom-call | flops 3000000000 | bytes 6583360 | tf_op jit(solution)/shard_map/pallas_call | solution.py:603
  17.9 5.7 %shard_map.273 = (bf16[512,1024]{1,0:T(8,128)(2,1)S(1)}, bf16[512,1024]{1,0:T(8,128)(2,1)S(1)}, f32[1,1024]{1,0:T(1,128)S(1)}, bf16[416,512]{1,0:T(8,128)(2,1)S(...) custom-call(s32[4]{0:T(128)S(1)} %pad_add_fusion.sel_ref.me_ref, ...), custom_call_target="tpu_custom_call" | custom-call | flops 3000000000 | bytes 9269248 | tf_op jit(solution)/shard_map/pallas_call | solution.py:603
  24.3 4.7 %shard_map.274 = (bf16[512,1024]{1,0:T(8,128)(2,1)S(1)}, bf16[512,1024]{1,0:T(8,128)(2,1)S(1)}, f32[1,1024]{1,0:T(1,128)S(1)}, bf16[4,196,512]{2,1,0:T(8,128)(2,...) custom-call(s32[4]{0:T(128)S(1)} %pad_add_fusion.sel_ref.me_ref, ...), custom_call_target="tpu_custom_call" | custom-call | flops 3000000000 | bytes 11343872 | tf_op jit(solution)/shard_map/pallas_call | solution.py:603
  29.0 0.9 copy-done.14
  29.9 9.2 %shard_map.275 = (bf16[512,512]{1,0:T(8,128)(2,1)S(1)}, bf16[512,512]{1,0:T(8,128)(2,1)S(1)}, bf16[512,512]{1,0:T(8,128)(2,1)S(1)}, bf16[512,512]{1,0:T(8,128)(2...) custom-call(s32[4]{0:T(128)S(1)} %pad_add_fusion.sel_ref.me_ref, ...), custom_call_target="tpu_custom_call" | custom-call | flops 5000000000 | bytes 8145984 | tf_op jit(solution)/shard_map/pallas_call | solution.py:603
  39.7 3.7 %shard_map.276 = (f32[4,196,512]{2,1,0:T(8,128)S(1)}, f32[2,196,512]{2,1,0:T(8,128)S(1)}, f32[16,512]{1,0:T(8,128)S(1)}, f32[16,512]{1,0:T(8,128)S(1)}) custom-call(s32[4]{0:T(128)S(1)} %pad_add_fusion.sel_ref.me_ref, bf16[4,196,512]{2,1,0:T(8,128)(2,1)S(1)} %copy.37.tok_ref, f32[416,512]{1,0:T(8,128)S(1)} %get-tuple-element.87.gres_ref, ...), custom_call_target="tpu_custom_call" | custom-call | flops 2000000000 | bytes 7579648 | tf_op jit(solution)/shard_map/pallas_call | solution.py:603
  43.4 1.5 %copy.41 = f32[2,196,512]{2,0,1:T(2,128)} copy(f32[2,196,512]{2,1,0:T(8,128)S(1)} %get-tuple-element.101) | data formatting | bytes 1605632 | tf_op jit(solution)/shard_map/pallas_call | solution.py:603
  45.9 2.7 %collective-permute-start.18 = (bf16[256,512]{1,0:T(8,128)(2,1)S(1)}, bf16[256,512]{1,0:T(8,128)(2,1)S(1)}, u32[]{:S(2)}, u32[]{:S(2)}) collective-permute-start(bf16[256,512]{1,0:T(8,128)(2,1)S(1)} %get-tuple-element.110), channel_id=1, source_target_pairs={{0,2},{2,0},{4,6},{6,4},{8,10},{10,8},{12,14},{14,12},{16,18},{18,... | collective-permute-start | bytes 786440 | tf_op jit(solution)/shard_map/ppermute | solution.py:628
  48.7 1.1 collective-permute-done.9.b_ref
  50.3 1.6 %collective-permute-start.12 = (f32[16,512]{1,0:T(8,128)S(1)}, f32[16,512]{1,0:T(8,128)S(1)}, u32[]{:S(2)}, u32[]{:S(2)}) collective-permute-start(f32[16,512]{1,0:T(8,128)S(1)} %shard_map.277.a_ref), channel_id=1, source_target_pairs={{0,6},{2,4},{4,2},{6,0},{8,14},{10,12},{12,10},{14,8},{16,22},{18,... | collective-permute-start | bytes 98312 | tf_op jit(solution)/shard_map/ppermute | solution.py:628
  51.9 5.4 %collective-permute-done.12.d_ref = f32[16,512]{1,0:T(8,128)S(1)} collective-permute-done((f32[16,512]{1,0:T(8,128)S(1)}, f32[16,512]{1,0:T(8,128)S(1)}, u32[]{:S(2)}, u32[]{:S(2)}) %collective-permute-start.12) | collective-permute-done | bytes 32800 | tf_op jit(solution)/shard_map/ppermute | solution.py:628
  57.6 3.6 %collective-permute-done.11.c_ref = f32[16,512]{1,0:T(8,128)S(1)} collective-permute-done((f32[16,512]{1,0:T(8,128)S(1)}, f32[16,512]{1,0:T(8,128)S(1)}, u32[]{:S(2)}, u32[]{:S(2)}) %collective-permute-start.11) | collective-permute-done | bytes 32800 | tf_op jit(solution)/shard_map/ppermute | solution.py:628
  61.2 1.5 %collective-permute-start.10 = (f32[16,512]{1,0:T(8,128)S(1)}, f32[16,512]{1,0:T(8,128)S(1)}, u32[]{:S(2)}, u32[]{:S(2)}) collective-permute-start(f32[16,512]{1,0:T(8,128)S(1)} %shard_map.277.a_ref), channel_id=1, source_target_pairs={{0,2},{2,0},{4,6},{6,4},{8,10},{10,8},{12,14},{14,12},{16,18},{18,... | collective-permute-start | bytes 98312 | tf_op jit(solution)/shard_map/ppermute | solution.py:628
  62.7 2.4 %collective-permute-done.10.b_ref = f32[16,512]{1,0:T(8,128)S(1)} collective-permute-done((f32[16,512]{1,0:T(8,128)S(1)}, f32[16,512]{1,0:T(8,128)S(1)}, u32[]{:S(2)}, u32[]{:S(2)}) %collective-permute-start.10) | collective-permute-done | bytes 32800 | tf_op jit(solution)/shard_map/ppermute | solution.py:628
  65.7 3.7 %collective-permute-start.15 = (f32[16,512]{1,0:T(8,128)S(1)}, f32[16,512]{1,0:T(8,128)S(1)}, u32[]{:S(2)}, u32[]{:S(2)}) collective-permute-start(f32[16,512]{1,0:T(8,128)S(1)} %shard_map.278.refs_0_), channel_id=1, source_target_pairs={{0,24},{2,26},{4,28},{6,30},{8,16},{10,18},{12,20},{14,22},{16,8},... | collective-permute-start | bytes 98312 | tf_op jit(solution)/shard_map/ppermute | solution.py:628
  69.6 1.8 %shard_map.284 = (bf16[256,1024]{1,0:T(8,128)(2,1)}, bf16[256,1024]{1,0:T(8,128)(2,1)}) custom-call(s32[4]{0:T(128)S(1)} %pad_add_fusion.sel_ref.me_ref, bf16[512,1024]{1,0:T(8,128)(2,1)S(1)} %get-tuple-element.125.refs_0_, bf16[512,1024]{1,0:T(8,128)(2,1)S(1)} %collective-permute-done.25.refs_1_, ...), custom_call_target="tpu_custom_call" | custom-call | flops 1000000 | bytes 5242880 | tf_op jit(solution)/shard_map/pallas_call | solution.py:603
  71.5 1.5 %collective-permute-start.27 = (bf16[256,1024]{1,0:T(8,128)(2,1)}, bf16[256,1024]{1,0:T(8,128)(2,1)}, u32[]{:S(2)}, u32[]{:S(2)}) collective-permute-start(bf16[256,1024]{1,0:T(8,128)(2,1)} %get-tuple-element.129), channel_id=1, source_target_pairs={{0,2},{2,0},{4,6},{6,4},{8,10},{10,8},{12,14},{14,12},{16,18},{18,... | collective-permute-start | bytes 1572872 | tf_op jit(solution)/shard_map/ppermute | solution.py:628
  73.0 1.3 collective-permute-done.14.refs_2_
  74.8 1.5 %collective-permute-start.19 = (bf16[256,512]{1,0:T(8,128)(2,1)S(1)}, bf16[256,512]{1,0:T(8,128)(2,1)S(1)}, u32[]{:S(2)}, u32[]{:S(2)}) collective-permute-start(bf16[256,512]{1,0:T(8,128)(2,1)S(1)} %get-tuple-element.111), channel_id=1, source_target_pairs={{0,4},{2,6},{4,0},{6,2},{8,12},{10,14},{12,8},{14,10},{16,20},{18,... | collective-permute-start | bytes 786440 | tf_op jit(solution)/shard_map/ppermute | solution.py:628
  76.3 16.3 %collective-permute-done.19.refs_5_.refs_6_ = bf16[256,512]{1,0:T(8,128)(2,1)S(1)} collective-permute-done((bf16[256,512]{1,0:T(8,128)(2,1)S(1)}, bf16[256,512]{1,0:T(8,128)(2,1)S(1)}, u32[]{:S(2)}, u32[]{:S(2)}) %collective-permute-start.19) | collective-permute-done | bytes 262176 | tf_op jit(solution)/shard_map/ppermute | solution.py:628
  93.4 1.3 shard_map.281
  94.7 1.9 %collective-permute-done.13.refs_1_ = f32[16,512]{1,0:T(8,128)S(1)} collective-permute-done((f32[16,512]{1,0:T(8,128)S(1)}, f32[16,512]{1,0:T(8,128)S(1)}, u32[]{:S(2)}, u32[]{:S(2)}) %collective-permute-start.13) | collective-permute-done | bytes 32800 | tf_op jit(solution)/shard_map/ppermute | solution.py:628
  97.8 0.8 copy-done.43
  99.1 0.8 copy-done.16
  99.8 0.8 copy-done.18
  100.6 0.8 copy-done.20
  101.3 0.8 copy-done.22
  102.1 1.2 shard_map.279
  103.3 1.8 %constant_dynamic-update-slice_fusion = bf16[4,196,512]{2,1,0:T(8,128)(2,1)} fusion(bf16[4,196,512]{2,1,0:T(8,128)(2,1)} %copy-done.14, bf16[2,196,512]{2,1,0:T(8,128)(2,1)} %copy-done.43, s32[]{:T(128)S(6)} %select_n.32), kind=kLoop, calls=%fused_computation.6 | loop fusion | bytes 819204 | tf_op jit(solution)/shard_map/dynamic_update_slice | solution.py:907
  105.1 2.4 %copy.43 = bf16[4,196,512]{2,0,1:T(4,128)(2,1)} copy(bf16[4,196,512]{2,1,0:T(8,128)(2,1)} %constant_dynamic-update-slice_fusion) | data formatting | bytes 1605632
  107.6 1.2 shard_map.282
  109.4 2.4 %collective-permute-start.23 = (bf16[32,1024]{1,0:T(8,128)(2,1)S(1)}, bf16[32,1024]{1,0:T(8,128)(2,1)S(1)}, u32[]{:S(2)}, u32[]{:S(2)}) collective-permute-start(bf16[32,1024]{1,0:T(8,128)(2,1)S(1)} %get-tuple-element.116), channel_id=1, source_target_pairs={{0,16},{2,18},{4,20},{6,22},{8,24},{10,26},{12,28},{14,30},{16,0},... | collective-permute-start | bytes 196616 | tf_op jit(solution)/shard_map/ppermute | solution.py:628
  111.8 1.5 %collective-permute-start.24 = (bf16[32,1024]{1,0:T(8,128)(2,1)S(1)}, bf16[32,1024]{1,0:T(8,128)(2,1)S(1)}, u32[]{:S(2)}, u32[]{:S(2)}) collective-permute-start(bf16[32,1024]{1,0:T(8,128)(2,1)S(1)} %get-tuple-element.117), channel_id=1, source_target_pairs={{0,24},{2,26},{4,28},{6,30},{8,16},{10,18},{12,20},{14,22},{16,8},... | collective-permute-start | bytes 196616 | tf_op jit(solution)/shard_map/ppermute | solution.py:628
  113.2 1.4 %shard_map.285 = (bf16[128,1024]{1,0:T(8,128)(2,1)S(1)}, bf16[128,1024]{1,0:T(8,128)(2,1)S(1)}) custom-call(s32[4]{0:T(128)S(1)} %pad_add_fusion.sel_ref.me_ref, bf16[512,1024]{1,0:T(8,128)(2,1)S(1)} %get-tuple-element.125.refs_0_, bf16[512,1024]{1,0:T(8,128)(2,1)S(1)} %collective-permute-done.25.refs_1_, bf16[256,1024]{1,0:T(8,128)(2,1)} %collective-permute-done.27.refs_2_, ...), custom_call_target="tpu_custom_call" | custom-call | flops 1000000 | bytes 5767168 | tf_op jit(solution)/shard_map/pallas_call | solution.py:603
  114.6 1.6 %collective-permute-start.29 = (bf16[128,1024]{1,0:T(8,128)(2,1)S(1)}, bf16[128,1024]{1,0:T(8,128)(2,1)S(1)}, u32[]{:S(2)}, u32[]{:S(2)}) collective-permute-start(bf16[128,1024]{1,0:T(8,128)(2,1)S(1)} %get-tuple-element.131), channel_id=1, source_target_pairs={{0,4},{2,6},{4,0},{6,2},{8,12},{10,14},{12,8},{14,10},{16,20},{18,... | collective-permute-start | bytes 786440 | tf_op jit(solution)/shard_map/ppermute | solution.py:628
  116.2 1.4 %collective-permute-start.30 = (bf16[128,1024]{1,0:T(8,128)(2,1)S(1)}, bf16[128,1024]{1,0:T(8,128)(2,1)S(1)}, u32[]{:S(2)}, u32[]{:S(2)}) collective-permute-start(bf16[128,1024]{1,0:T(8,128)(2,1)S(1)} %get-tuple-element.132), channel_id=1, source_target_pairs={{0,2},{2,0},{4,6},{6,4},{8,10},{10,8},{12,14},{14,12},{16,18},{18,... | collective-permute-start | bytes 786440 | tf_op jit(solution)/shard_map/ppermute | solution.py:628
  117.7 1.4 %copy_dynamic-update-slice_fusion = f32[4,196,512]{2,1,0:T(8,128)S(1)} fusion(f32[4,196,512]{2,1,0:T(8,128)S(1)} %copy-done.11, s32[]{:T(128)S(6)} %select_n.32, f32[2,196,512]{2,0,1:T(2,128)} %collective-permute-done.8), kind=kLoop, calls=%fused_computation | loop fusion | bytes 1622020 | tf_op jit(solution)/shard_map/dynamic_update_slice | solution.py:959
  119.1 2.2 %copy.44 = f32[4,196,512]{2,0,1:T(4,128)} copy(f32[4,196,512]{2,1,0:T(8,128)S(1)} %copy_dynamic-update-slice_fusion) | data formatting | bytes 3211264
  122.6 1.7 %shard_map.286 = (bf16[32,2048]{1,0:T(8,128)(2,1)S(1)}, bf16[32,2048]{1,0:T(8,128)(2,1)S(1)}, bf16[32,2048]{1,0:T(8,128)(2,1)S(1)}, f32[32,2048]{1,0:T(8,128)S(1)}) custom-call(s32[4]{0:T(128)S(1)} %pad_add_fusion.sel_ref.me_ref, bf16[512,1024]{1,0:T(8,128)(2,1)S(1)} %get-tuple-element.125.refs_0_, bf16[512,1024]{1,0:T(8,128)(2,1)S(1)} %collective-permute-done.25.refs_1_, ...), custom_call_target="tpu_custom_call" | custom-call | flops 1000000 | bytes 6422528 | tf_op jit(solution)/shard_map/pallas_call | solution.py:603
  125.0 2.3 %collective-permute-start.32 = (bf16[32,2048]{1,0:T(8,128)(2,1)S(1)}, bf16[32,2048]{1,0:T(8,128)(2,1)S(1)}, u32[]{:S(2)}, u32[]{:S(2)}) collective-permute-start(bf16[32,2048]{1,0:T(8,128)(2,1)S(1)} %get-tuple-element.135), channel_id=1, source_target_pairs={{0,16},{2,18},{4,20},{6,22},{8,24},{10,26},{12,28},{14,30},{16,0},... | collective-permute-start | bytes 393224 | tf_op jit(solution)/shard_map/ppermute | solution.py:628
  127.3 1.5 %collective-permute-start.33 = (bf16[32,2048]{1,0:T(8,128)(2,1)S(1)}, bf16[32,2048]{1,0:T(8,128)(2,1)S(1)}, u32[]{:S(2)}, u32[]{:S(2)}) collective-permute-start(bf16[32,2048]{1,0:T(8,128)(2,1)S(1)} %get-tuple-element.136), channel_id=1, source_target_pairs={{0,24},{2,26},{4,28},{6,30},{8,16},{10,18},{12,20},{14,22},{16,8},... | collective-permute-start | bytes 393224 | tf_op jit(solution)/shard_map/ppermute | solution.py:628
  130.3 2.4 %collective-permute-done.32.refs_1_ = bf16[32,2048]{1,0:T(8,128)(2,1)S(1)} collective-permute-done((bf16[32,2048]{1,0:T(8,128)(2,1)S(1)}, bf16[32,2048]{1,0:T(8,128)(2,1)S(1)}, u32[]{:S(2)}, u32[]{:S(2)}) %collective-permute-start.32) | collective-permute-done | bytes 131104 | tf_op jit(solution)/shard_map/ppermute | solution.py:628
  132.6 1.4 %collective-permute-done.33.refs_2_ = bf16[32,2048]{1,0:T(8,128)(2,1)S(1)} collective-permute-done((bf16[32,2048]{1,0:T(8,128)(2,1)S(1)}, bf16[32,2048]{1,0:T(8,128)(2,1)S(1)}, u32[]{:S(2)}, u32[]{:S(2)}) %collective-permute-start.33) | collective-permute-done | bytes 131104 | tf_op jit(solution)/shard_map/ppermute | solution.py:628
  134.0 1.3 shard_map.287
  (136 shorter events, 14.3 us)
Async XLA Ops:
  0.7 8.9 %collective-permute-start = (bf16[3,512,256]{2,1,0:T(8,128)(2,1)}, bf16[3,512,256]{2,1,0:T(8,128)(2,1)S(1)}, u32[]{:S(2)}, u32[]{:S(2)}) collective-permute-start(bf16[3,512,256]{2,1,0:T(8,128)(2,1)} %bitcast.29), channel_id=1, source_target_pairs={{0,1},{1,0},{2,3},{3,2},{4,5},{5,4},{6,7},{7,6},{8,9},{9,8},{10,11... | collective-permute-start | bytes 2359304 | tf_op jit(solution)/shard_map/ppermute | solution.py:787
  1.2 16.6 %collective-permute-start.4 = (bf16[512,1024]{1,0:T(8,128)(2,1)}, bf16[512,1024]{1,0:T(8,128)(2,1)S(1)}, u32[]{:S(2)}, u32[]{:S(2)}) collective-permute-start(bf16[512,1024]{1,0:T(8,128)(2,1)} %w1_ref.1), channel_id=1, source_target_pairs={{0,1},{1,0},{2,3},{3,2},{4,5},{5,4},{6,7},{7,6},{8,9},{9,8},{10,11... | collective-permute-start | bytes 3145736 | tf_op jit(solution)/shard_map/ppermute | solution.py:787
  1.3 16.6 %collective-permute-start.5 = (bf16[512,1024]{1,0:T(8,128)(2,1)}, bf16[512,1024]{1,0:T(8,128)(2,1)}, u32[]{:S(2)}, u32[]{:S(2)}) collective-permute-start(bf16[512,1024]{1,0:T(8,128)(2,1)} %w2_ref.1), channel_id=1, source_target_pairs={{0,1},{1,0},{2,3},{3,2},{4,5},{5,4},{6,7},{7,6},{8,9},{9,8},{10,11... | collective-permute-start | bytes 3145736 | tf_op jit(solution)/shard_map/ppermute | solution.py:787
  1.7 7.2 %collective-permute-start.3 = (bf16[512,256]{1,0:T(8,128)(2,1)}, bf16[512,256]{1,0:T(8,128)(2,1)S(1)}, u32[]{:S(2)}, u32[]{:S(2)}) collective-permute-start(bf16[512,256]{1,0:T(8,128)(2,1)} %pm_ref.3), channel_id=1, source_target_pairs={{0,1},{1,0},{2,3},{3,2},{4,5},{5,4},{6,7},{7,6},{8,9},{9,8},{10,11... | collective-permute-start | bytes 786440 | tf_op jit(solution)/shard_map/ppermute | solution.py:787
  1.8 4.9 %collective-permute-start.2 = (f32[8,169]{1,0:T(8,128)}, f32[8,169]{1,0:T(8,128)S(1)}, u32[]{:S(2)}, u32[]{:S(2)}) collective-permute-start(f32[8,169]{1,0:T(8,128)} %bitcast.32), channel_id=1, source_target_pairs={{0,1},{1,0},{2,3},{3,2},{4,5},{5,4},{6,7},{7,6},{8,9},{9,8},{10,11... | collective-permute-start | bytes 16232 | tf_op jit(solution)/shard_map/ppermute | solution.py:787
  6.7 1.9 %collective-permute-start.1 = (f32[2,256]{1,0:T(2,128)S(1)}, f32[2,256]{1,0:T(2,128)S(1)}, u32[]{:S(2)}, u32[]{:S(2)}) collective-permute-start(f32[2,256]{1,0:T(2,128)S(1)} %copy-done.36), channel_id=1, source_target_pairs={{0,1},{1,0},{2,3},{3,2},{4,5},{5,4},{6,7},{7,6},{8,9},{9,8},{10,11... | collective-permute-start | bytes 6152 | tf_op jit(solution)/shard_map/ppermute | solution.py:787
  8.6 9.2 %collective-permute-start.6 = (f32[1,1024]{1,0:T(1,128)S(1)}, f32[1,1024]{1,0:T(1,128)S(1)}, u32[]{:S(2)}, u32[]{:S(2)}) collective-permute-start(f32[1,1024]{1,0:T(1,128)S(1)} %bitcast.34), channel_id=1, source_target_pairs={{0,1},{1,0},{2,3},{3,2},{4,5},{5,4},{6,7},{7,6},{8,9},{9,8},{10,11... | collective-permute-start | bytes 12296 | tf_op jit(solution)/shard_map/ppermute | solution.py:787
  9.6 8.2 %copy-start.26 = (bf16[3,512,256]{2,1,0:T(8,128)(2,1)}, bf16[3,512,256]{2,1,0:T(8,128)(2,1)S(1)}, u32[]{:S(2)}) copy-start(bf16[3,512,256]{2,1,0:T(8,128)(2,1)S(1)} %collective-permute-done.wo_ref) | copy-start | bytes 2359300
  10.8 7.1 %copy-start.38 = (f32[512]{0:T(512)S(1)}, f32[512]{0:T(512)}, u32[]{:S(2)}) copy-start(f32[512]{0:T(512)} %param.25) | copy-start | bytes 6148
  10.8 7.1 %copy-start.39 = (f32[512]{0:T(512)S(1)}, f32[512]{0:T(512)}, u32[]{:S(2)}) copy-start(f32[512]{0:T(512)} %param.26) | copy-start | bytes 6148
  17.9 6.4 %copy-start.23 = (bf16[512,1024]{1,0:T(8,128)(2,1)S(1)}, bf16[512,1024]{1,0:T(8,128)(2,1)}, u32[]{:S(2)}) copy-start(bf16[512,1024]{1,0:T(8,128)(2,1)} %w1_ref.1) | copy-start | bytes 3145732
  17.9 6.4 %copy-start.24 = (bf16[512,1024]{1,0:T(8,128)(2,1)S(1)}, bf16[512,1024]{1,0:T(8,128)(2,1)}, u32[]{:S(2)}) copy-start(bf16[512,1024]{1,0:T(8,128)(2,1)} %w2_ref.1) | copy-start | bytes 3145732
  23.7 45.8 %collective-permute-start.25 = (bf16[512,1024]{1,0:T(8,128)(2,1)S(1)}, bf16[512,1024]{1,0:T(8,128)(2,1)S(1)}, u32[]{:S(2)}, u32[]{:S(2)}) collective-permute-start(bf16[512,1024]{1,0:T(8,128)(2,1)S(1)} %get-tuple-element.126), channel_id=1, source_target_pairs={{0,1},{1,0},{2,3},{3,2},{4,5},{5,4},{6,7},{7,6},{8,9},{9,8},{10,11... | collective-permute-start | bytes 3145736 | tf_op jit(solution)/shard_map/ppermute | solution.py:787
  24.1 45.4 %collective-permute-start.26 = (bf16[512,1024]{1,0:T(8,128)(2,1)S(1)}, bf16[512,1024]{1,0:T(8,128)(2,1)S(1)}, u32[]{:S(2)}, u32[]{:S(2)}) collective-permute-start(bf16[512,1024]{1,0:T(8,128)(2,1)S(1)} %get-tuple-element.128), channel_id=1, source_target_pairs={{0,1},{1,0},{2,3},{3,2},{4,5},{5,4},{6,7},{7,6},{8,9},{9,8},{10,11... | collective-permute-start | bytes 3145736 | tf_op jit(solution)/shard_map/ppermute | solution.py:787
  29.8 39.7 %copy-start = (bf16[512,1024]{1,0:T(8,128)(2,1)}, bf16[512,1024]{1,0:T(8,128)(2,1)S(1)}, u32[]{:S(2)}) copy-start(bf16[512,1024]{1,0:T(8,128)(2,1)S(1)} %get-tuple-element.127.refs_2_.refs_3_.refs_4_) | copy-start | bytes 3145732
  29.9 9.8 %copy-start.27 = (bf16[3,512,256]{2,1,0:T(8,128)(2,1)S(1)}, bf16[3,512,256]{2,1,0:T(8,128)(2,1)}, u32[]{:S(2)}) copy-start(bf16[3,512,256]{2,1,0:T(8,128)(2,1)} %copy-done.26) | copy-start | bytes 2359300
  39.1 54.3 %copy-start.2 = (bf16[512,512]{1,0:T(8,128)(2,1)}, bf16[512,512]{1,0:T(8,128)(2,1)S(1)}, u32[]{:S(2)}) copy-start(bf16[512,512]{1,0:T(8,128)(2,1)S(1)} %get-tuple-element.106.refs_0_) | copy-start | bytes 1572868
  39.1 54.3 %copy-start.4 = (bf16[512,512]{1,0:T(8,128)(2,1)}, bf16[512,512]{1,0:T(8,128)(2,1)S(1)}, u32[]{:S(2)}) copy-start(bf16[512,512]{1,0:T(8,128)(2,1)S(1)} %get-tuple-element.108.refs_2_.refs_3_.refs_4_) | copy-start | bytes 1572868
  39.1 6.1 %collective-permute-start.16 = (bf16[512,512]{1,0:T(8,128)(2,1)S(1)}, bf16[512,512]{1,0:T(8,128)(2,1)S(1)}, u32[]{:S(2)}, u32[]{:S(2)}) collective-permute-start(bf16[512,512]{1,0:T(8,128)(2,1)S(1)} %get-tuple-element.107), channel_id=1, source_target_pairs={{0,1},{1,0},{2,3},{3,2},{4,5},{5,4},{6,7},{7,6},{8,9},{9,8},{10,11... | collective-permute-start | bytes 1572872 | tf_op jit(solution)/shard_map/ppermute | solution.py:787
  39.5 5.7 %collective-permute-start.17 = (bf16[512,512]{1,0:T(8,128)(2,1)S(1)}, bf16[512,512]{1,0:T(8,128)(2,1)S(1)}, u32[]{:S(2)}, u32[]{:S(2)}) collective-permute-start(bf16[512,512]{1,0:T(8,128)(2,1)S(1)} %get-tuple-element.109), channel_id=1, source_target_pairs={{0,1},{1,0},{2,3},{3,2},{4,5},{5,4},{6,7},{7,6},{8,9},{9,8},{10,11... | collective-permute-start | bytes 1572872 | tf_op jit(solution)/shard_map/ppermute | solution.py:787
  44.9 71.3 %collective-permute-start.8 = (f32[2,196,512]{2,0,1:T(2,128)}, f32[2,196,512]{2,0,1:T(2,128)}, u32[]{:S(2)}, u32[]{:S(2)}) collective-permute-start(f32[2,196,512]{2,0,1:T(2,128)} %copy.41), channel_id=1, source_target_pairs={{0,1},{1,0},{2,3},{3,2},{4,5},{5,4},{6,7},{7,6},{8,9},{9,8},{10,11... | collective-permute-start | bytes 2408456 | tf_op jit(solution)/shard_map/ppermute | solution.py:787
  45.2 48.2 %copy-start.6 = (bf16[512,512]{1,0:T(8,128)(2,1)}, bf16[512,512]{1,0:T(8,128)(2,1)S(1)}, u32[]{:S(2)}) copy-start(bf16[512,512]{1,0:T(8,128)(2,1)S(1)} %collective-permute-done.16.refs_1_) | copy-start | bytes 1572868
  45.2 48.2 %copy-start.8 = (bf16[512,512]{1,0:T(8,128)(2,1)}, bf16[512,512]{1,0:T(8,128)(2,1)S(1)}, u32[]{:S(2)}) copy-start(bf16[512,512]{1,0:T(8,128)(2,1)S(1)} %collective-permute-done.17.refs_3_.refs_4_.refs_5_) | copy-start | bytes 1572868
  45.9 28.9 %collective-permute-start.18 = (bf16[256,512]{1,0:T(8,128)(2,1)S(1)}, bf16[256,512]{1,0:T(8,128)(2,1)S(1)}, u32[]{:S(2)}, u32[]{:S(2)}) collective-permute-start(bf16[256,512]{1,0:T(8,128)(2,1)S(1)} %get-tuple-element.110), channel_id=1, source_target_pairs={{0,2},{2,0},{4,6},{6,4},{8,10},{10,8},{12,14},{14,12},{16,18},{18,... | collective-permute-start | bytes 786440 | tf_op jit(solution)/shard_map/ppermute | solution.py:628
  48.6 1.2 collective-permute-start.9
  50.3 7.0 %collective-permute-start.12 = (f32[16,512]{1,0:T(8,128)S(1)}, f32[16,512]{1,0:T(8,128)S(1)}, u32[]{:S(2)}, u32[]{:S(2)}) collective-permute-start(f32[16,512]{1,0:T(8,128)S(1)} %shard_map.277.a_ref), channel_id=1, source_target_pairs={{0,6},{2,4},{4,2},{6,0},{8,14},{10,12},{12,10},{14,8},{16,22},{18,... | collective-permute-start | bytes 98312 | tf_op jit(solution)/shard_map/ppermute | solution.py:628
  57.3 3.9 %collective-permute-start.11 = (f32[16,512]{1,0:T(8,128)S(1)}, f32[16,512]{1,0:T(8,128)S(1)}, u32[]{:S(2)}, u32[]{:S(2)}) collective-permute-start(f32[16,512]{1,0:T(8,128)S(1)} %shard_map.277.a_ref), channel_id=1, source_target_pairs={{0,4},{2,6},{4,0},{6,2},{8,12},{10,14},{12,8},{14,10},{16,20},{18,... | collective-permute-start | bytes 98312 | tf_op jit(solution)/shard_map/ppermute | solution.py:628
  61.2 3.9 %collective-permute-start.10 = (f32[16,512]{1,0:T(8,128)S(1)}, f32[16,512]{1,0:T(8,128)S(1)}, u32[]{:S(2)}, u32[]{:S(2)}) collective-permute-start(f32[16,512]{1,0:T(8,128)S(1)} %shard_map.277.a_ref), channel_id=1, source_target_pairs={{0,2},{2,0},{4,6},{6,4},{8,10},{10,8},{12,14},{14,12},{16,18},{18,... | collective-permute-start | bytes 98312 | tf_op jit(solution)/shard_map/ppermute | solution.py:628
  65.7 26.9 %copy-start.15 = (f32[16,512]{1,0:T(8,128)}, f32[16,512]{1,0:T(8,128)S(1)}, u32[]{:S(2)}) copy-start(f32[16,512]{1,0:T(8,128)S(1)} %shard_map.278.refs_0_) | copy-start | bytes 98308
  65.7 5.8 %collective-permute-start.15 = (f32[16,512]{1,0:T(8,128)S(1)}, f32[16,512]{1,0:T(8,128)S(1)}, u32[]{:S(2)}, u32[]{:S(2)}) collective-permute-start(f32[16,512]{1,0:T(8,128)S(1)} %shard_map.278.refs_0_), channel_id=1, source_target_pairs={{0,24},{2,26},{4,28},{6,30},{8,16},{10,18},{12,20},{14,22},{16,8},... | collective-permute-start | bytes 98312 | tf_op jit(solution)/shard_map/ppermute | solution.py:628
  69.5 4.8 %collective-permute-start.14 = (f32[16,512]{1,0:T(8,128)S(1)}, f32[16,512]{1,0:T(8,128)S(1)}, u32[]{:S(2)}, u32[]{:S(2)}) collective-permute-start(f32[16,512]{1,0:T(8,128)S(1)} %shard_map.278.refs_0_), channel_id=1, source_target_pairs={{0,16},{2,18},{4,20},{6,22},{8,24},{10,26},{12,28},{14,30},{16,0},... | collective-permute-start | bytes 98312 | tf_op jit(solution)/shard_map/ppermute | solution.py:628
  69.5 28.3 %collective-permute-start.7 = (bf16[2,196,512]{2,1,0:T(8,128)(2,1)S(1)}, bf16[2,196,512]{2,1,0:T(8,128)(2,1)S(1)}, u32[]{:S(2)}, u32[]{:S(2)}) collective-permute-start(bf16[2,196,512]{2,1,0:T(8,128)(2,1)S(1)} %get-tuple-element.86), channel_id=1, source_target_pairs={{0,1},{1,0},{2,3},{3,2},{4,5},{5,4},{6,7},{7,6},{8,9},{9,8},{10,11... | collective-permute-start | bytes 1204232 | tf_op jit(solution)/shard_map/ppermute | solution.py:787
  71.5 25.1 %copy-start.17 = (f32[16,512]{1,0:T(8,128)}, f32[16,512]{1,0:T(8,128)S(1)}, u32[]{:S(2)}) copy-start(f32[16,512]{1,0:T(8,128)S(1)} %collective-permute-done.15.refs_3_) | copy-start | bytes 98308
  71.5 40.3 %collective-permute-start.27 = (bf16[256,1024]{1,0:T(8,128)(2,1)}, bf16[256,1024]{1,0:T(8,128)(2,1)}, u32[]{:S(2)}, u32[]{:S(2)}) collective-permute-start(bf16[256,1024]{1,0:T(8,128)(2,1)} %get-tuple-element.129), channel_id=1, source_target_pairs={{0,2},{2,0},{4,6},{6,4},{8,10},{10,8},{12,14},{14,12},{16,18},{18,... | collective-permute-start | bytes 1572872 | tf_op jit(solution)/shard_map/ppermute | solution.py:628
  74.3 22.3 %copy-start.19 = (f32[16,512]{1,0:T(8,128)}, f32[16,512]{1,0:T(8,128)S(1)}, u32[]{:S(2)}) copy-start(f32[16,512]{1,0:T(8,128)S(1)} %collective-permute-done.14.refs_2_) | copy-start | bytes 98308
  74.3 38.9 %collective-permute-start.28 = (bf16[256,1024]{1,0:T(8,128)(2,1)}, bf16[256,1024]{1,0:T(8,128)(2,1)}, u32[]{:S(2)}, u32[]{:S(2)}) collective-permute-start(bf16[256,1024]{1,0:T(8,128)(2,1)} %get-tuple-element.130), channel_id=1, source_target_pairs={{0,4},{2,6},{4,0},{6,2},{8,12},{10,14},{12,8},{14,10},{16,20},{18,... | collective-permute-start | bytes 1572872 | tf_op jit(solution)/shard_map/ppermute | solution.py:628
  74.8 17.9 %collective-permute-start.19 = (bf16[256,512]{1,0:T(8,128)(2,1)S(1)}, bf16[256,512]{1,0:T(8,128)(2,1)S(1)}, u32[]{:S(2)}, u32[]{:S(2)}) collective-permute-start(bf16[256,512]{1,0:T(8,128)(2,1)S(1)} %get-tuple-element.111), channel_id=1, source_target_pairs={{0,4},{2,6},{4,0},{6,2},{8,12},{10,14},{12,8},{14,10},{16,20},{18,... | collective-permute-start | bytes 786440 | tf_op jit(solution)/shard_map/ppermute | solution.py:628
  92.7 3.9 %collective-permute-start.13 = (f32[16,512]{1,0:T(8,128)S(1)}, f32[16,512]{1,0:T(8,128)S(1)}, u32[]{:S(2)}, u32[]{:S(2)}) collective-permute-start(f32[16,512]{1,0:T(8,128)S(1)} %shard_map.278.refs_0_), channel_id=1, source_target_pairs={{0,8},{2,10},{4,12},{6,14},{8,0},{10,2},{12,4},{14,6},{16,24},{18,... | collective-permute-start | bytes 98312 | tf_op jit(solution)/shard_map/ppermute | solution.py:628
  97.2 10.3 %collective-permute-start.20 = (bf16[128,512]{1,0:T(8,128)(2,1)}, bf16[128,512]{1,0:T(8,128)(2,1)S(1)}, u32[]{:S(2)}, u32[]{:S(2)}) collective-permute-start(bf16[128,512]{1,0:T(8,128)(2,1)} %get-tuple-element.112), channel_id=1, source_target_pairs={{0,4},{2,6},{4,0},{6,2},{8,12},{10,14},{12,8},{14,10},{16,20},{18,... | collective-permute-start | bytes 393224 | tf_op jit(solution)/shard_map/ppermute | solution.py:628
  98.5 9.0 %collective-permute-start.21 = (bf16[128,512]{1,0:T(8,128)(2,1)}, bf16[128,512]{1,0:T(8,128)(2,1)}, u32[]{:S(2)}, u32[]{:S(2)}) collective-permute-start(bf16[128,512]{1,0:T(8,128)(2,1)} %get-tuple-element.113), channel_id=1, source_target_pairs={{0,2},{2,0},{4,6},{6,4},{8,10},{10,8},{12,14},{14,12},{16,18},{18,... | collective-permute-start | bytes 393224 | tf_op jit(solution)/shard_map/ppermute | solution.py:628
  108.8 12.5 %collective-permute-start.22 = (bf16[32,1024]{1,0:T(8,128)(2,1)S(1)}, bf16[32,1024]{1,0:T(8,128)(2,1)S(1)}, u32[]{:S(2)}, u32[]{:S(2)}) collective-permute-start(bf16[32,1024]{1,0:T(8,128)(2,1)S(1)} %get-tuple-element.115), channel_id=1, source_target_pairs={{0,8},{2,10},{4,12},{6,14},{8,0},{10,2},{12,4},{14,6},{16,24},{18,... | collective-permute-start | bytes 196616 | tf_op jit(solution)/shard_map/ppermute | solution.py:628
  109.4 11.9 %collective-permute-start.23 = (bf16[32,1024]{1,0:T(8,128)(2,1)S(1)}, bf16[32,1024]{1,0:T(8,128)(2,1)S(1)}, u32[]{:S(2)}, u32[]{:S(2)}) collective-permute-start(bf16[32,1024]{1,0:T(8,128)(2,1)S(1)} %get-tuple-element.116), channel_id=1, source_target_pairs={{0,16},{2,18},{4,20},{6,22},{8,24},{10,26},{12,28},{14,30},{16,0},... | collective-permute-start | bytes 196616 | tf_op jit(solution)/shard_map/ppermute | solution.py:628
  111.8 9.5 %collective-permute-start.24 = (bf16[32,1024]{1,0:T(8,128)(2,1)S(1)}, bf16[32,1024]{1,0:T(8,128)(2,1)S(1)}, u32[]{:S(2)}, u32[]{:S(2)}) collective-permute-start(bf16[32,1024]{1,0:T(8,128)(2,1)S(1)} %get-tuple-element.117), channel_id=1, source_target_pairs={{0,24},{2,26},{4,28},{6,30},{8,16},{10,18},{12,20},{14,22},{16,8},... | collective-permute-start | bytes 196616 | tf_op jit(solution)/shard_map/ppermute | solution.py:628
  114.6 7.2 %collective-permute-start.29 = (bf16[128,1024]{1,0:T(8,128)(2,1)S(1)}, bf16[128,1024]{1,0:T(8,128)(2,1)S(1)}, u32[]{:S(2)}, u32[]{:S(2)}) collective-permute-start(bf16[128,1024]{1,0:T(8,128)(2,1)S(1)} %get-tuple-element.131), channel_id=1, source_target_pairs={{0,4},{2,6},{4,0},{6,2},{8,12},{10,14},{12,8},{14,10},{16,20},{18,... | collective-permute-start | bytes 786440 | tf_op jit(solution)/shard_map/ppermute | solution.py:628
  116.2 6.4 %collective-permute-start.30 = (bf16[128,1024]{1,0:T(8,128)(2,1)S(1)}, bf16[128,1024]{1,0:T(8,128)(2,1)S(1)}, u32[]{:S(2)}, u32[]{:S(2)}) collective-permute-start(bf16[128,1024]{1,0:T(8,128)(2,1)S(1)} %get-tuple-element.132), channel_id=1, source_target_pairs={{0,2},{2,0},{4,6},{6,4},{8,10},{10,8},{12,14},{14,12},{16,18},{18,... | collective-permute-start | bytes 786440 | tf_op jit(solution)/shard_map/ppermute | solution.py:628
  124.3 6.0 %collective-permute-start.31 = (bf16[32,2048]{1,0:T(8,128)(2,1)S(1)}, bf16[32,2048]{1,0:T(8,128)(2,1)S(1)}, u32[]{:S(2)}, u32[]{:S(2)}) collective-permute-start(bf16[32,2048]{1,0:T(8,128)(2,1)S(1)} %get-tuple-element.134), channel_id=1, source_target_pairs={{0,8},{2,10},{4,12},{6,14},{8,0},{10,2},{12,4},{14,6},{16,24},{18,... | collective-permute-start | bytes 393224 | tf_op jit(solution)/shard_map/ppermute | solution.py:628
  125.0 7.7 %collective-permute-start.32 = (bf16[32,2048]{1,0:T(8,128)(2,1)S(1)}, bf16[32,2048]{1,0:T(8,128)(2,1)S(1)}, u32[]{:S(2)}, u32[]{:S(2)}) collective-permute-start(bf16[32,2048]{1,0:T(8,128)(2,1)S(1)} %get-tuple-element.135), channel_id=1, source_target_pairs={{0,16},{2,18},{4,20},{6,22},{8,24},{10,26},{12,28},{14,30},{16,0},... | collective-permute-start | bytes 393224 | tf_op jit(solution)/shard_map/ppermute | solution.py:628
  127.3 6.8 %collective-permute-start.33 = (bf16[32,2048]{1,0:T(8,128)(2,1)S(1)}, bf16[32,2048]{1,0:T(8,128)(2,1)S(1)}, u32[]{:S(2)}, u32[]{:S(2)}) collective-permute-start(bf16[32,2048]{1,0:T(8,128)(2,1)S(1)} %get-tuple-element.136), channel_id=1, source_target_pairs={{0,24},{2,26},{4,28},{6,30},{8,16},{10,18},{12,20},{14,22},{16,8},... | collective-permute-start | bytes 393224 | tf_op jit(solution)/shard_map/ppermute | solution.py:628
  (30 other events, 114.4 us)

commit v2 on v1

--- a/solution.py
+++ b/solution.py
@@ -275,7 +275,7 @@
 
 def ffn_kernel(
     images,
-    layouts,
+    layout,
     last,
     me_ref,
     resid_ref,
@@ -289,8 +289,8 @@
 ):
     if last:
         b2_ref, ln_ref, lnt_ref, cot_b_ref, cot_t_ref, ffn_in, gln_in = refs[:7]
-        g1_ref, g2_ref, gb_ref, out_ref, half_ref, gres_ref, sums_ref = refs[7:14]
-        ffn_ref, gln_ref = refs[14:]
+        g1_ref, g2_ref, gb_ref, half_ref, gres_ref, sums_ref = refs[7:13]
+        ffn_ref, gln_ref = refs[13:]
     else:
         g1_ref, g2_ref, gb_ref = refs[:3]
         ln_ref, lnt_ref, cot_b_ref, cot_t_ref, ffn_ref, gln_ref = refs[3:]
@@ -302,8 +302,9 @@
         ln_ref[...] = (normed * gain_ref[...] + shift_ref[...]).astype(BF16)
         fill_rows(cot_b_ref, cot_ref, me_ref[0] * images, images)
         width = ln_ref.shape[1]
-        lnt_ref[...] = nt(order_matrix(width, layouts[0]), ln_ref[...]).astype(BF16)
-        cot_t_ref[...] = nt(order_matrix(width, layouts[1]), cot_b_ref[...]).astype(BF16)
+        order = order_matrix(width, layout)
+        lnt_ref[...] = nt(order, ln_ref[...]).astype(BF16)
+        cot_t_ref[...] = nt(order, cot_b_ref[...]).astype(BF16)
         ffn_ref[...] = jnp.zeros(ffn_ref.shape, F32)
         gln_ref[...] = jnp.zeros(gln_ref.shape, F32)
     chunk = 256
@@ -329,9 +330,7 @@
     resid = resid_ref[...]
     result = (resid + ffn_ref[...] + b2_ref[...]).astype(BF16)
     for image in range(images):
-        piece = result[image * TPAD : image * TPAD + TOK]
-        out_ref[me_ref[0] * images + image] = piece
-        half_ref[image] = piece
+        half_ref[image] = result[image * TPAD : image * TPAD + TOK]
     normed, inverse = normalize(resid)
     upstream = gln_ref[...]
     cot = cot_b_ref[...].astype(F32)
@@ -347,7 +346,7 @@
 def attend_back_kernel(
     images,
     heads,
-    layouts,
+    layout,
     me_ref,
     gres_ref,
     ids_ref,
@@ -381,8 +380,8 @@
     mask_ref[...] = head_mask(heads)
     gres = gres_ref[...]
     gres_b = gres.astype(BF16)
-    put_rows(gvpm_ref, layouts[1], chan, tn(gres_b, merged_ref[:, :chan]))
-    put_rows(gvpo_ref, layouts[1], chan, tn(gres_b, merged_ref[:, chan:]))
+    put_rows(gvpm_ref, layout, chan, tn(gres_b, merged_ref[:, :chan]))
+    put_rows(gvpo_ref, layout, chan, tn(gres_b, merged_ref[:, chan:]))
     grad_m = jnp.concatenate(
         [nn(gres_b, pm_ref[...]).astype(BF16), nn(gres_b, po_ref[...]).astype(BF16)], axis=1
     )
@@ -436,10 +435,10 @@
     sums_ref[0:1, :] = jnp.sum(qsum_ref[...], axis=0, keepdims=True)
     sums_ref[1:2, :] = jnp.sum(vsum_ref[...], axis=0, keepdims=True)
     win = win_ref[...]
-    put_rows(gqko_ref, layouts[0], 0, tn(win, gqkv_ref[:, 3 * chan : 5 * chan]))
-    put_rows(gvpo_ref, layouts[1], 0, tn(win, gqkv_ref[:, 5 * chan :]))
-    put_rows(gqkm_ref, layouts[0], 0, tn(win, gqkv_ref[:, : 2 * chan]))
-    put_rows(gvpm_ref, layouts[1], 0, tn(win, gqkv_ref[:, 2 * chan : 3 * chan]))
+    put_rows(gqko_ref, layout, 0, tn(win, gqkv_ref[:, 3 * chan : 5 * chan]))
+    put_rows(gvpo_ref, layout, 0, tn(win, gqkv_ref[:, 5 * chan :]))
+    put_rows(gqkm_ref, layout, 0, tn(win, gqkv_ref[:, : 2 * chan]))
+    put_rows(gvpm_ref, layout, 0, tn(win, gqkv_ref[:, 2 * chan : 3 * chan]))
 
 
 def last_kernel(
@@ -458,7 +457,6 @@
     qv_ref,
     gbm_ref,
     gbo_ref,
-    full_ref,
     half_ref,
     mine_ref,
     theirs_ref,
@@ -487,9 +485,7 @@
     normed, inverse = normalize(x_ref[...])
     grad_in = gres_ref[...] + norm_back(upstream, normed, inverse, gain_ref[...])
     for image in range(images):
-        piece = grad_in[image * TPAD : image * TPAD + TOK]
-        full_ref[me_ref[0] * images + image] = piece
-        half_ref[image] = piece
+        half_ref[image] = grad_in[image * TPAD : image * TPAD + TOK]
     width = upstream.shape[1]
     gain_sum = jnp.sum(upstream * normed, axis=0, keepdims=True)
     shift_sum = jnp.sum(upstream, axis=0, keepdims=True)
@@ -537,51 +533,59 @@
     table_ref[heads // 2 :, :] = total[low:, chan : chan + entries]
 
 
-def row_block(ref, sel_ref, blocks, form):
-    index = form[0]
-    for at, factor in enumerate(form[1:]):
-        if factor:
-            index = index + factor * sel_ref[at]
-    rows = ref.shape[0] // blocks
-    if blocks == 1:
-        return ref[...].astype(F32)
-    return ref[pl.ds(pl.multiple_of(index * rows, rows), rows), :].astype(F32)
-
-
-def sum_kernel(groups, sel_ref, *refs):
-    at, outs = 0, refs[sum(len(g) for g in groups) :]
-    for picks, out_ref in zip(groups, outs):
-        total = row_block(refs[at], sel_ref, *picks[0])
-        for more in range(1, len(picks)):
-            total = total + row_block(refs[at + more], sel_ref, *picks[more])
-        out_ref[...] = total.astype(out_ref.dtype)
-        at += len(picks)
-
-
-def fan_kernel(groups, rows, sends, sel_ref, *refs):
-    flat = sum(len(g) for g in groups)
-    outs, total_ref, at, col = refs[flat:-1], refs[-1], 0, 0
-    for picks in groups:
-        total = row_block(refs[at], sel_ref, *picks[0])
-        for more in range(1, len(picks)):
-            total = total + row_block(refs[at + more], sel_ref, *picks[more])
-        total_ref[:, col : col + total.shape[1]] = total
-        col += total.shape[1]
-        at += len(picks)
-    own = sel_ref[3]
-    for s in range(1, sends + 1):
-        piece = total_ref[pl.ds(pl.multiple_of((own ^ s) * rows, rows), rows), :]
-        outs[s - 1][...] = piece.astype(BF16)
-    outs[sends][...] = total_ref[pl.ds(pl.multiple_of(own * rows, rows), rows), :]
-
-
-def total_kernel(sel_ref, own_ref, *refs):
-    ins, (a_ref, b_ref) = refs[:-2], refs[-2:]
-    total = own_ref[...]
-    for in_ref in ins:
+def rows_at(ref, start, rows):
+    return ref[pl.ds(pl.multiple_of(start, rows), rows), :].astype(F32)
+
+
+def add_kernel(rows, sel_ref, a0_ref, a1_ref, b0_ref, b1_ref, *out_refs):
+    half = a0_ref.shape[1]
+    for s, out_ref in enumerate(out_refs, 1):
+        at = (sel_ref[1] ^ s) * rows
+        out_ref[:, :half] = (rows_at(a0_ref, at, rows) + rows_at(a1_ref, at, rows)).astype(BF16)
+        out_ref[:, half:] = (rows_at(b0_ref, at, rows) + rows_at(b1_ref, at, rows)).astype(BF16)
+
+
+def fan_kernel(rows, sends, sel_ref, *refs):
+    pairs, wide, outs = refs[:4], refs[4 : -1 - sends], refs[-1 - sends :]
+    half = pairs[0].shape[1]
+    for s in range(sends + 1):
+        near = (sel_ref[2] ^ s) * rows
+        far = sel_ref[1] * (rows * (sends + 1)) + near
+        got = rows_at(wide[0], near, rows)
+        for ref in wide[1:]:
+            got = got + rows_at(ref, near, rows)
+        out_ref = outs[s - 1] if s else outs[sends]
+        for cols, first, second in (
+            (slice(0, half), pairs[0], pairs[1]),
+            (slice(half, got.shape[1]), pairs[2], pairs[3]),
+        ):
+            total = rows_at(first, far, rows) + rows_at(second, far, rows) + got[:, cols]
+            out_ref[:, cols] = total.astype(out_ref.dtype)
+
+
+def total_kernel(parts, sel_ref, own_ref, *refs):
+    total, at = own_ref[...], 0
+    for in_ref in refs[: parts - 1]:
         total = total + in_ref[...].astype(F32)
-    a_ref[...] = total[:, : a_ref.shape[1]]
-    b_ref[...] = total[:, a_ref.shape[1] :]
+    for out_ref in refs[parts - 1 :]:
+        width = out_ref.shape[-1]
+        if len(out_ref.shape) == 2:
+            out_ref[...] = total[:, at : at + width]
+            at += width
+            continue
+        for plane in range(out_ref.shape[0]):
+            out_ref[plane] = total[:, at : at + width]
+            at += width
+
+
+def join_kernel(sel_ref, own_ref, other_ref, out_ref):
+    images = own_ref.shape[0]
+    for image in range(out_ref.shape[1]):
+        mine = sel_ref[0] == image // images
+        piece = jnp.where(
+            mine, own_ref[image % images].astype(F32), other_ref[image % images].astype(F32)
+        )
+        out_ref[:, image, :] = piece.astype(out_ref.dtype)
 
 
 def pair_kernel(sel_ref, a_ref, b_ref, out_ref):
@@ -613,11 +617,7 @@
 
 def digits_of(count):
     digits, stride = [], 1
-    for size in (2, 2):
-        if (count // stride) % size == 0 and count // stride > 1:
-            digits.append((stride, size))
-            stride *= size
-    while count // stride > 1:
+    while stride < count:
         size = 4 if (count // stride) % 4 == 0 else 2
         digits.append((stride, size))
         stride *= size
@@ -628,13 +628,13 @@
     return lax.ppermute(value, axis, [(i, i ^ mask) for i in range(count)])
 
 
-def scatter_sum(addends, axis, count, digits, order):
+def scatter_sum(addends, axis, count, digits):
     index = lax.axis_index(axis)
     rows, cols = addends[0].shape
     shape = [size for _, size in reversed(digits)] + [rows // count, cols]
     addends = [a.reshape(shape) for a in addends]
     left = list(reversed(range(len(digits))))
-    for digit in order:
+    for digit in range(len(digits)):
         stride, size = digits[digit]
         place = left.index(digit)
         mine = (index // stride) % size
@@ -671,71 +671,41 @@
         (value,) = call(kernel, sel, terms, [struct(value.shape, F32)], [], 10**5, 2)
 
 
-def add_blocks(sel, groups, kind):
-    flat = [item for group in groups for item in group]
-    outs = [
-        struct((group[0][0].shape[0] // group[0][1], group[0][0].shape[1]), kind)
-        for group in groups
-    ]
-    picks = tuple(tuple((blocks, form) for _, blocks, form in group) for group in groups)
-    return call(
-        functools.partial(sum_kernel, picks), sel, [a for a, _, _ in flat], outs, [], 10**6, 4
-    )
-
-
-def scatter_pairs(sel, pair_a, pair_b, axis, count, digits):
-    (stride_x, _), (stride_y, _), (stride_z, size_z) = digits
-    (a0, a1), (b0, b1) = pair_a, pair_b
-    not_x, not_y = (1, 0, -1, 0, 0), (1, 0, 0, -1, 0)
-    send_a, send_b = add_blocks(
-        sel, [[(a0, 2, not_x), (a1, 2, not_x)], [(b0, 2, not_y), (b1, 2, not_y)]], BF16
-    )
-    got_a = xor_exchange(send_a, axis, count, stride_x)
-    got_b = xor_exchange(send_b, axis, count, stride_y)
-    at_a, at_b = (1, 0, 2, -1, 0), (1, 0, -1, 2, 0)
-    send_a, send_b = add_blocks(
+def scatter_pairs(sel, pairs, axis, count, digits, outs):
+    (stride, size), (far_stride, far_size) = digits
+    (a0, a1), (b0, b1) = pairs
+    arrays = [a0, a1, b0, b1]
+    cols = a0.shape[1] + b0.shape[1]
+    deep = a0.shape[0] // size
+    rows = deep // far_size
+
+    def exchange(sends, step):
+        received = []
+        for s, send in enumerate(sends, 1):
+            received.append(xor_exchange(send, axis, count, s * step))
+        return received
+
+    sends = call(
+        functools.partial(add_kernel, deep),
         sel,
-        [
-            [(a0, 4, at_a), (a1, 4, at_a), (got_a, 2, not_y)],
-            [(b0, 4, at_b), (b1, 4, at_b), (got_b, 2, not_x)],
-        ],
-        BF16,
-    )
-    more_a = xor_exchange(send_a, axis, count, stride_y)
-    more_b = xor_exchange(send_b, axis, count, stride_x)
-    groups = (
-        (
-            (4, (0, 0, 2, 1, 0)),
-            (4, (0, 0, 2, 1, 0)),
-            (2, (0, 0, 0, 1, 0)),
-            (1, (0, 0, 0, 0, 0)),
-        ),
-        (
-            (4, (0, 0, 1, 2, 0)),
-            (4, (0, 0, 1, 2, 0)),
-            (2, (0, 0, 1, 0, 0)),
-            (1, (0, 0, 0, 0, 0)),
-        ),
-    )
-    cols = a0.shape[1] + b0.shape[1]
-    deep = a0.shape[0] // 4
-    rows = deep // size_z
-    outs = (struct((rows, cols), BF16),) * (size_z - 1) + (struct((rows, cols), F32),)
+        arrays,
+        [struct((deep, cols), BF16)] * (size - 1),
+        [],
+        10**6,
+        4,
+    )
+    wide = exchange(sends, stride)
     *sends, own = call(
-        functools.partial(fan_kernel, groups, rows, size_z - 1),
+        functools.partial(fan_kernel, rows, far_size - 1),
         sel,
-        [a0, a1, got_a, more_a, b0, b1, got_b, more_b],
-        outs,
-        [pltpu.VMEM((deep, cols), F32)],
+        arrays + wide,
+        [struct((rows, cols), BF16)] * (far_size - 1) + [struct((rows, cols), F32)],
+        [],
         10**6,
-        6,
-    )
-    received = []
-    for s, send in enumerate(sends, 1):
-        received.append(xor_exchange(send, axis, count, s * stride_z))
-    half = a0.shape[1]
-    outs = (struct((rows, half), F32), struct((rows, cols - half), F32))
-    return call(total_kernel, sel, [own] + received, outs, [], 10**6, 4)
+        4,
+    )
+    parts = [own] + exchange(sends, far_stride)
+    return call(functools.partial(total_kernel, len(parts)), sel, parts, outs, [], 10**6, 4)
 
 
 def per_device(n_dp, n_tensor, *args):
@@ -771,16 +741,12 @@
     rows_w = images * WINS * WPAD
     half_rows = -(-entries // 16) * 16
     digits = digits_of(n_dp)
-    by_pairs = [size for _, size in digits] == [2, 2, 4] and width // n_dp % 16 == 0
-    order_a = list(range(len(digits)))
-    order_b = order_a[1:2] + order_a[:1] + order_a[2:]
-    plain = order_a[::-1]
-    layouts = tuple(
-        (width // n_dp, digits, order if by_pairs else plain) for order in (order_a, order_b)
-    )
+    by_pairs = len(digits) == 2 and width // n_dp % 16 == 0
+    order = list(range(len(digits)))
+    layout = (width // n_dp, digits, order if by_pairs else order[::-1])
     me = lax.axis_index("tensor")
     spot = lax.axis_index("dp")
-    places = [(spot // stride) % size for stride, size in digits[:3]]
+    places = [(spot // stride) % size for stride, size in digits[:2]]
     me_arr = sel = jnp.stack([me] + places).astype(jnp.int32)
 
     def swap(value):
@@ -864,7 +830,7 @@
     ins = common + (w1o, w2o, b1_o)
     outs = (weight_grad, weight_grad, struct((1, hidden), F32)) + kept
     g1o, g2o, gbo, *carried = call(
-        functools.partial(ffn_kernel, images, layouts, False),
+        functools.partial(ffn_kernel, images, layout, False),
         me_arr,
         ins,
         outs,
@@ -879,13 +845,12 @@
         weight_grad,
         weight_grad,
         struct((1, hidden), F32),
-        struct(tokens.shape, BF16),
         struct((images, TOK, width), BF16),
         acc,
         struct((8, width), F32),
     )
-    g1m, g2m, gbm, out_full, out_half, gres, sums_two = call(
-        functools.partial(ffn_kernel, images, layouts, True),
+    g1m, g2m, gbm, out_half, gres, sums_two = call(
+        functools.partial(ffn_kernel, images, layout, True),
         me_arr,
         ins,
         outs,
@@ -894,17 +859,22 @@
         LIMIT,
     )
 
-    def scatter(pair_a, pair_b):
-        if by_pairs:
-            return scatter_pairs(sel, pair_a, pair_b, "dp", n_dp, digits)
-        return (
-            scatter_sum(pair_a, "dp", n_dp, digits, order_a),
-            scatter_sum(pair_b, "dp", n_dp, digits, order_b),
+    share = width // n_dp
+
+    def join(half):
+        shape = struct((TOK, all_images, width), half.dtype)
+        (joined,) = call(join_kernel, sel, [half, swap(half)], [shape], [], 10**6, LIMIT)
+        return joined.transpose(1, 0, 2)
+
+    if by_pairs:
+        outs = [struct((share, hidden), F32)] * 2
+        sent_fc1, sent_fc2 = scatter_pairs(
+            sel, ((g1m, got1), (g2m, got2)), "dp", n_dp, digits, outs
         )
-
-    sent_fc1, sent_fc2 = scatter((g1m, got1), (g2m, got2))
-    out_other = swap(out_half)
-    output = lax.dynamic_update_slice_in_dim(out_full, out_other, (1 - me) * images, 0)
+    else:
+        sent_fc1 = scatter_sum((g1m, got1), "dp", n_dp, digits)
+        sent_fc2 = scatter_sum((g2m, got2), "dp", n_dp, digits)
+    output = join(out_half)
 
     ins = (gres, region_ids, merged, w_proj, po, q, k, v, win_in, lse, bias)
     outs = (
@@ -917,7 +887,7 @@
         bias_shape,
     )
     gqkm, gqko, gvpm, gvpo, gqkv, sums_qv, gbias = call(
-        functools.partial(attend_back_kernel, images, heads, layouts),
+        functools.partial(attend_back_kernel, images, heads, layout),
         me_arr,
         ins,
         outs,
@@ -934,16 +904,22 @@
 
     got_qk = swap(gqko)
     got_vp = swap(gvpo)
-    sent_qk, sent_vp = scatter((gqkm, got_qk), (gvpm, got_vp))
-    sent_qkv = jnp.stack(
-        [sent_qk[:, :chan], sent_qk[:, chan:], sent_vp[:, :chan]], axis=0
-    ).transpose(1, 0, 2)
-    sent_proj = sent_vp[:, chan:]
+    if by_pairs:
+        outs = [struct((3, share, chan), F32), struct((share, chan), F32)]
+        sent_qkv, sent_proj = scatter_pairs(
+            sel, ((gqkm, got_qk), (gvpm, got_vp)), "dp", n_dp, digits, outs
+        )
+    else:
+        sent_qk = scatter_sum((gqkm, got_qk), "dp", n_dp, digits)
+        sent_vp = scatter_sum((gvpm, got_vp), "dp", n_dp, digits)
+        sent_qkv = jnp.stack([sent_qk[:, :chan], sent_qk[:, chan:], sent_vp[:, :chan]], axis=0)
+        sent_proj = sent_vp[:, chan:]
+    sent_qkv = sent_qkv.transpose(1, 0, 2)
 
     ins = (tokens, gres, gqkv, wm, wo, row(norm1_gain), gbias, sums_two, sums_qv, gbm, gbo)
     pack = struct((-(-(7 + hidden // width + heads // 2) // 8) * 8, width), F32)
-    outs = (struct(tokens.shape, F32), struct((images, TOK, width), F32), pack, pack)
-    grad_full, grad_half, small, theirs = call(
+    outs = (struct((images, TOK, width), F32), pack, pack)
+    grad_half, small, theirs = call(
         functools.partial(last_kernel, images, heads, half_rows),
         me_arr,
         ins,
@@ -956,7 +932,7 @@
         2 * 10**9,
         LIMIT,
     )
-    grad_in = lax.dynamic_update_slice_in_dim(grad_full, swap(grad_half), (1 - me) * images, 0)
+    grad_in = join(grad_half)
 
     got = swap(theirs)
     (small,) = call(pair_kernel, sel, [small, got], [struct(small.shape, F32)], [], 10**5, 2)

time: 136 us -> 117 us (0.86)
  local copies, waits for them, and re-layouts: 18.7 us -> 2.35 us
  starting transfers between devices: 30.9 us -> 29.3 us
    unnamed x92 -> x32, local copies, waits for them, and re-layouts: 13.3 us -> 1.58 us
    dynamic_update_slice x2 -> x0, local copies, waits for them, and re-layouts: 3.17 us -> none  [the longest x1 1.77 us: block(): lax.dynamic_update_slice_in_dim(out_full, out_other, (1 - me) * images, 0)]
    ppermute x20 -> x18, waiting for transfers between devices: 35.9 us -> 37.5 us  [xor_exchange(): return lax.ppermute(value, axis, [(i, i ^ mask) for i in range(count)])]
    ppermute x20 -> x18, starting transfers between devices: 27 us -> 25.6 us  [xor_exchange(): return lax.ppermute(value, axis, [(i, i ^ mask) for i in range(count)])]
  transfers between devices with their start and end apart: 34 -> 32, of which waited for: 13 -> 8; matrix products, arithmetic and copies ran while one was open for 9% -> 2% of each run, Pallas kernels for 26% -> 32%
where the time goes in v2:
time: 117 us
  Pallas kernels  43.5 us (37%)
  waiting for transfers between devices  40.4 us (35%)
  starting transfers between devices  29.3 us (25%)
  local copies, waits for them, and re-layouts  2.35 us (2%)
    pallas_call x17, Pallas kernels, call(): pl.pallas_call(kernel, in_specs=[pl.BlockSpec(memory_space=pltpu.SMEM)] +...  43.5 us
    ppermute x18, waiting for transfers between devices, xor_exchange(): return lax.ppermute(value, axis, [(i, i ^ mask) for i in range(count)])  37.5 us
    ppermute x18, starting transfers between devices, xor_exchange(): return lax.ppermute(value, axis, [(i, i ^ mask) for i in range(count)])  25.6 us
    ppermute x14, starting transfers between devices, swap(): return lax.ppermute(value, 'tensor', [(i, i ^ 1) for i in range(n_tensor)])  3.7 us
    ppermute x14, waiting for transfers between devices, swap(): return lax.ppermute(value, 'tensor', [(i, i ^ 1) for i in range(n_tensor)])  2.84 us
  transfers between devices with their start and end apart: 32, of which 8 were waited for; matrix products, arithmetic and copies ran while one was open for 2% of the time, Pallas kernels for 32%

profile of v2, /device:TPU:0, one launch (start us, length us, event | category | flops | bytes accessed | tf_op | source)
XLA Modules:
  0.0 116.6 jit_solution(13757435875826184005)
XLA Ops:
  0.6 0.6 collective-permute-start
  1.3 0.4 collective-permute-start.5
  1.8 0.4 collective-permute-start.2
  2.3 1.3 %copy.35.tok_ref = bf16[4,196,512]{2,1,0:T(8,128)(2,1)S(1)} copy(bf16[4,196,512]{2,0,1:T(4,128)(2,1)} %param.16) | data formatting | bytes 1605632 | tf_op args[0]
  3.9 2.8 %collective-permute-done.2.other_ref = f32[8,169]{1,0:T(8,128)S(1)} collective-permute-done((f32[8,169]{1,0:T(8,128)}, f32[8,169]{1,0:T(8,128)S(1)}, u32[]{:S(2)}, u32[]{:S(2)}) %collective-permute-start.2) | collective-permute-done | bytes 5440 | tf_op jit(solution)/shard_map/ppermute | solution.py:753
  6.7 0.4 collective-permute-start.1
  7.1 1.5 %shard_map.271.bias_ref = f32[512,128]{1,0:T(8,128)S(1)} custom-call(s32[3]{0:T(128)S(1)} %pad_add_fusion.sel_ref.me_ref, f32[8,169]{1,0:T(8,128)S(1)} %bitcast.27, f32[8,169]{1,0:T(8,128)S(1)} %collective-permute-done.2.other_ref), custom_call_target="tpu_custom_call" | custom-call | flops 1000000000 | bytes 272960 | tf_op jit(solution)/shard_map/pallas_call | solution.py:607
  8.9 7.0 %shard_map.272 = (bf16[512,512]{1,0:T(8,128)(2,1)S(1)}, bf16[512,512]{1,0:T(8,128)(2,1)S(1)}, bf16[512,512]{1,0:T(8,128)(2,1)S(1)}, bf16[512,512]{1,0:T(8,128)(2...) custom-call(s32[3]{0:T(128)S(1)} %pad_add_fusion.sel_ref.me_ref, ...), custom_call_target="tpu_custom_call" | custom-call | flops 3000000000 | bytes 6583360 | tf_op jit(solution)/shard_map/pallas_call | solution.py:607
  16.0 4.8 %shard_map.273 = (bf16[512,1024]{1,0:T(8,128)(2,1)S(1)}, bf16[512,1024]{1,0:T(8,128)(2,1)S(1)}, f32[1,1024]{1,0:T(1,128)S(1)}, bf16[416,512]{1,0:T(8,128)(2,1)S(...) custom-call(s32[3]{0:T(128)S(1)} %pad_add_fusion.sel_ref.me_ref, ...), custom_call_target="tpu_custom_call" | custom-call | flops 3000000000 | bytes 9269248 | tf_op jit(solution)/shard_map/pallas_call | solution.py:607
  20.8 0.5 collective-permute-start.24
  21.4 4.7 %shard_map.274 = (bf16[512,1024]{1,0:T(8,128)(2,1)S(1)}, bf16[512,1024]{1,0:T(8,128)(2,1)S(1)}, f32[1,1024]{1,0:T(1,128)S(1)}, bf16[2,196,512]{2,1,0:T(8,128)(2,...) custom-call(s32[3]{0:T(128)S(1)} %pad_add_fusion.sel_ref.me_ref, f32[416,512]{1,0:T(8,128)S(1)} %get-tuple-element.74.resid_ref, ...), custom_call_target="tpu_custom_call" | custom-call | flops 3000000000 | bytes 10541056 | tf_op jit(solution)/shard_map/pallas_call | solution.py:607
  26.1 9.2 %shard_map.276 = (bf16[512,512]{1,0:T(8,128)(2,1)S(1)}, bf16[512,512]{1,0:T(8,128)(2,1)S(1)}, bf16[512,512]{1,0:T(8,128)(2,1)S(1)}, bf16[512,512]{1,0:T(8,128)(2...) custom-call(s32[3]{0:T(128)S(1)} %pad_add_fusion.sel_ref.me_ref, ...), custom_call_target="tpu_custom_call" | custom-call | flops 5000000000 | bytes 8145984 | tf_op jit(solution)/shard_map/pallas_call | solution.py:607
  35.3 0.5 collective-permute-start.16
  35.9 3.6 %shard_map.277 = (f32[2,196,512]{2,1,0:T(8,128)S(1)}, f32[16,512]{1,0:T(8,128)S(1)}, f32[16,512]{1,0:T(8,128)S(1)}) custom-call(s32[3]{0:T(128)S(1)} %pad_add_fusion.sel_ref.me_ref, bf16[4,196,512]{2,1,0:T(8,128)(2,1)S(1)} %copy.35.tok_ref, f32[416,512]{1,0:T(8,128)S(1)} %get-tuple-element.82.gres_ref, bf16[512,1536]{1,0:T(8,128)(2,1)S(1)} %get-tuple-element.89.gqkv_ref, ...), custom_call_target="tpu_custom_call" | custom-call | flops 2000000000 | bytes 5974016 | tf_op jit(solution)/shard_map/pallas_call | solution.py:607
  39.5 0.4 collective-permute-start.9
  40.0 0.7 shard_map.282
  40.7 2.7 %collective-permute-start.18 = (bf16[128,1024]{1,0:T(8,128)(2,1)S(1)}, bf16[128,1024]{1,0:T(8,128)(2,1)S(1)}, u32[]{:S(2)}, u32[]{:S(2)}) collective-permute-start(bf16[128,1024]{1,0:T(8,128)(2,1)S(1)} %get-tuple-element.104), channel_id=1, source_target_pairs={{0,2},{2,0},{4,6},{6,4},{8,10},{10,8},{12,14},{14,12},{16,18},{18,... | collective-permute-start | bytes 786440 | tf_op jit(solution)/shard_map/ppermute | solution.py:628
  43.4 1.5 %collective-permute-start.19 = (bf16[128,1024]{1,0:T(8,128)(2,1)S(1)}, bf16[128,1024]{1,0:T(8,128)(2,1)S(1)}, u32[]{:S(2)}, u32[]{:S(2)}) collective-permute-start(bf16[128,1024]{1,0:T(8,128)(2,1)S(1)} %get-tuple-element.105), channel_id=1, source_target_pairs={{0,4},{2,6},{4,0},{6,2},{8,12},{10,14},{12,8},{14,10},{16,20},{18,... | collective-permute-start | bytes 786440 | tf_op jit(solution)/shard_map/ppermute | solution.py:628
  44.8 0.5 shard_map.279.a_ref
  45.5 6.7 %collective-permute-done.12.d_ref = f32[16,512]{1,0:T(8,128)S(1)} collective-permute-done((f32[16,512]{1,0:T(8,128)S(1)}, f32[16,512]{1,0:T(8,128)S(1)}, u32[]{:S(2)}, u32[]{:S(2)}) %collective-permute-start.12) | collective-permute-done | bytes 32800 | tf_op jit(solution)/shard_map/ppermute | solution.py:628
  52.5 0.6 copy.39
  53.1 3.0 %collective-permute-done.11.c_ref = f32[16,512]{1,0:T(8,128)S(1)} collective-permute-done((f32[16,512]{1,0:T(8,128)S(1)}, f32[16,512]{1,0:T(8,128)S(1)}, u32[]{:S(2)}, u32[]{:S(2)}) %collective-permute-start.11) | collective-permute-done | bytes 32800 | tf_op jit(solution)/shard_map/ppermute | solution.py:628
  56.1 1.4 %collective-permute-start.20 = (bf16[128,1024]{1,0:T(8,128)(2,1)S(1)}, bf16[128,1024]{1,0:T(8,128)(2,1)S(1)}, u32[]{:S(2)}, u32[]{:S(2)}) collective-permute-start(bf16[128,1024]{1,0:T(8,128)(2,1)S(1)} %get-tuple-element.106), channel_id=1, source_target_pairs={{0,6},{2,4},{4,2},{6,0},{8,14},{10,12},{12,10},{14,8},{16,22},{18,... | collective-permute-start | bytes 786440 | tf_op jit(solution)/shard_map/ppermute | solution.py:628
  57.9 0.9 shard_map.285
  58.8 6.5 %collective-permute-done.10.b_ref = f32[16,512]{1,0:T(8,128)S(1)} collective-permute-done((f32[16,512]{1,0:T(8,128)S(1)}, f32[16,512]{1,0:T(8,128)S(1)}, u32[]{:S(2)}, u32[]{:S(2)}) %collective-permute-start.10) | collective-permute-done | bytes 32800 | tf_op jit(solution)/shard_map/ppermute | solution.py:628
  65.3 1.7 %collective-permute-start.26 = (bf16[128,2048]{1,0:T(8,128)(2,1)S(1)}, bf16[128,2048]{1,0:T(8,128)(2,1)S(1)}, u32[]{:S(2)}, u32[]{:S(2)}) collective-permute-start(bf16[128,2048]{1,0:T(8,128)(2,1)S(1)} %get-tuple-element.122), channel_id=1, source_target_pairs={{0,2},{2,0},{4,6},{6,4},{8,10},{10,8},{12,14},{14,12},{16,18},{18,... | collective-permute-start | bytes 1572872 | tf_op jit(solution)/shard_map/ppermute | solution.py:628
  67.0 1.4 %collective-permute-start.27 = (bf16[128,2048]{1,0:T(8,128)(2,1)S(1)}, bf16[128,2048]{1,0:T(8,128)(2,1)S(1)}, u32[]{:S(2)}, u32[]{:S(2)}) collective-permute-start(bf16[128,2048]{1,0:T(8,128)(2,1)S(1)} %get-tuple-element.123), channel_id=1, source_target_pairs={{0,4},{2,6},{4,0},{6,2},{8,12},{10,14},{12,8},{14,10},{16,20},{18,... | collective-permute-start | bytes 1572872 | tf_op jit(solution)/shard_map/ppermute | solution.py:628
  68.8 0.6 shard_map.280.refs_0_
  69.3 10.7 %collective-permute-done.26.refs_4_ = bf16[128,2048]{1,0:T(8,128)(2,1)S(1)} collective-permute-done((bf16[128,2048]{1,0:T(8,128)(2,1)S(1)}, bf16[128,2048]{1,0:T(8,128)(2,1)S(1)}, u32[]{:S(2)}, u32[]{:S(2)}) %collective-permute-start.26) | collective-permute-done | bytes 524320 | tf_op jit(solution)/shard_map/ppermute | solution.py:628
  80.1 3.8 %collective-permute-start.15 = (f32[16,512]{1,0:T(8,128)S(1)}, f32[16,512]{1,0:T(8,128)S(1)}, u32[]{:S(2)}, u32[]{:S(2)}) collective-permute-start(f32[16,512]{1,0:T(8,128)S(1)} %shard_map.280.refs_0_), channel_id=1, source_target_pairs={{0,24},{2,26},{4,28},{6,30},{8,16},{10,18},{12,20},{14,22},{16,8},... | collective-permute-start | bytes 98312 | tf_op jit(solution)/shard_map/ppermute | solution.py:628
  83.9 7.6 %collective-permute-done.27.refs_5_ = bf16[128,2048]{1,0:T(8,128)(2,1)S(1)} collective-permute-done((bf16[128,2048]{1,0:T(8,128)(2,1)S(1)}, bf16[128,2048]{1,0:T(8,128)(2,1)S(1)}, u32[]{:S(2)}, u32[]{:S(2)}) %collective-permute-start.27) | collective-permute-done | bytes 524320 | tf_op jit(solution)/shard_map/ppermute | solution.py:628
  91.4 2.5 %collective-permute-start.14 = (f32[16,512]{1,0:T(8,128)S(1)}, f32[16,512]{1,0:T(8,128)S(1)}, u32[]{:S(2)}, u32[]{:S(2)}) collective-permute-start(f32[16,512]{1,0:T(8,128)S(1)} %shard_map.280.refs_0_), channel_id=1, source_target_pairs={{0,16},{2,18},{4,20},{6,22},{8,24},{10,26},{12,28},{14,30},{16,0},... | collective-permute-start | bytes 98312 | tf_op jit(solution)/shard_map/ppermute | solution.py:628
  94.0 1.6 %collective-permute-start.13 = (f32[16,512]{1,0:T(8,128)S(1)}, f32[16,512]{1,0:T(8,128)S(1)}, u32[]{:S(2)}, u32[]{:S(2)}) collective-permute-start(f32[16,512]{1,0:T(8,128)S(1)} %shard_map.280.refs_0_), channel_id=1, source_target_pairs={{0,8},{2,10},{4,12},{6,14},{8,0},{10,2},{12,4},{14,6},{16,24},{18,... | collective-permute-start | bytes 98312 | tf_op jit(solution)/shard_map/ppermute | solution.py:628
  95.6 0.7 shard_map.283
  96.3 0.9 shard_map.286
  97.2 0.5 collective-permute-start.21
  97.7 1.6 %collective-permute-start.29 = (bf16[32,2048]{1,0:T(8,128)(2,1)S(1)}, bf16[32,2048]{1,0:T(8,128)(2,1)S(1)}, u32[]{:S(2)}, u32[]{:S(2)}) collective-permute-start(bf16[32,2048]{1,0:T(8,128)(2,1)S(1)} %get-tuple-element.126), channel_id=1, source_target_pairs={{0,8},{2,10},{4,12},{6,14},{8,0},{10,2},{12,4},{14,6},{16,24},{18,... | collective-permute-start | bytes 393224 | tf_op jit(solution)/shard_map/ppermute | solution.py:628
  99.2 0.4 collective-permute-done.13.refs_1_
  99.6 1.1 collective-permute-start.30
  100.8 1.3 %collective-permute-start.31 = (bf16[32,2048]{1,0:T(8,128)(2,1)S(1)}, bf16[32,2048]{1,0:T(8,128)(2,1)S(1)}, u32[]{:S(2)}, u32[]{:S(2)}) collective-permute-start(bf16[32,2048]{1,0:T(8,128)(2,1)S(1)} %get-tuple-element.128), channel_id=1, source_target_pairs={{0,24},{2,26},{4,28},{6,30},{8,16},{10,18},{12,20},{14,22},{16,8},... | collective-permute-start | bytes 393224 | tf_op jit(solution)/shard_map/ppermute | solution.py:628
  102.1 0.6 collective-permute-start.22
  102.6 2.9 %collective-permute-start.23 = (bf16[32,1024]{1,0:T(8,128)(2,1)S(1)}, bf16[32,1024]{1,0:T(8,128)(2,1)S(1)}, u32[]{:S(2)}, u32[]{:S(2)}) collective-permute-start(bf16[32,1024]{1,0:T(8,128)(2,1)S(1)} %get-tuple-element.110), channel_id=1, source_target_pairs={{0,24},{2,26},{4,28},{6,30},{8,16},{10,18},{12,20},{14,22},{16,8},... | collective-permute-start | bytes 196616 | tf_op jit(solution)/shard_map/ppermute | solution.py:628
  105.5 1.2 %shard_map.281 = (f32[1,512]{1,0:T(1,128)}, f32[1,512]{1,0:T(1,128)}, f32[1,512]{1,0:T(1,128)}, f32[1,512]{1,0:T(1,128)}, f32[1,512]{1,0:T(1,128)}, /*index=5*/f...) custom-call(s32[3]{0:T(128)S(1)} %pad_add_fusion.sel_ref.me_ref, ...), custom_call_target="tpu_custom_call" | custom-call | flops 100000 | bytes 154912 | tf_op jit(solution)/shard_map/pallas_call | solution.py:607
  106.7 2.6 %shard_map.275 = bf16[196,4,512]{2,1,0:T(4,128)(2,1)} custom-call(s32[3]{0:T(128)S(1)} %pad_add_fusion.sel_ref.me_ref, bf16[2,196,512]{2,1,0:T(8,128)(2,1)S(1)} %get-tuple-element.81.own_ref, bf16[2,196,512]{2,1,0:T(8,128)(2,1)S(1)} %collective-permute-done.7.other_ref), custom_call_target="tpu_custom_call" | custom-call | flops 1000000 | bytes 1605632 | tf_op jit(solution)/shard_map/pallas_call | solution.py:607
  109.4 2.1 %shard_map.278 = f32[196,4,512]{2,1,0:T(4,128)} custom-call(s32[3]{0:T(128)S(1)} %pad_add_fusion.sel_ref.me_ref, f32[2,196,512]{2,1,0:T(8,128)S(1)} %get-tuple-element.95.own_ref, f32[2,196,512]{2,1,0:T(8,128)S(1)} %copy.40.other_ref), custom_call_target="tpu_custom_call" | custom-call | flops 1000000 | bytes 3211264 | tf_op jit(solution)/shard_map/pallas_call | solution.py:607
  111.5 2.6 %collective-permute-done.22.refs_1_ = bf16[32,1024]{1,0:T(8,128)(2,1)S(1)} collective-permute-done((bf16[32,1024]{1,0:T(8,128)(2,1)S(1)}, bf16[32,1024]{1,0:T(8,128)(2,1)S(1)}, u32[]{:S(2)}, u32[]{:S(2)}) %collective-permute-start.22) | collective-permute-done | bytes 65568 | tf_op jit(solution)/shard_map/ppermute | solution.py:628
  114.1 1.2 %shard_map.284 = (f32[3,32,256]{2,1,0:T(8,128)}, f32[32,256]{1,0:T(8,128)}) custom-call(s32[3]{0:T(128)S(1)} %pad_add_fusion.sel_ref.me_ref, f32[32,1024]{1,0:T(8,128)S(1)} %get-tuple-element.107.own_ref, bf16[32,1024]{1,0:T(8,128)(2,1)S(1)} %collective-permute-done.21.refs_0_, bf16[32,1024]{1,0:T(8,128)(2,1)S(1)} %collective-permute-done.22.refs_1_, ...), custom_call_target="tpu_custom_call" | custom-call | flops 1000000 | bytes 458752 | tf_op jit(solution)/shard_map/pallas_call | solution.py:607
  115.3 1.3 %shard_map.287 = (f32[32,1024]{1,0:T(8,128)}, f32[32,1024]{1,0:T(8,128)}) custom-call(s32[3]{0:T(128)S(1)} %pad_add_fusion.sel_ref.me_ref, f32[32,2048]{1,0:T(8,128)S(1)} %get-tuple-element.125.own_ref, bf16[32,2048]{1,0:T(8,128)(2,1)S(1)} %collective-permute-done.29.refs_0_, bf16[32,2048]{1,0:T(8,128)(2,1)S(1)} %collective-permute-done.30.refs_1_, ...), custom_call_target="tpu_custom_call" | custom-call | flops 1000000 | bytes 917504 | tf_op jit(solution)/shard_map/pallas_call | solution.py:607
  (68 shorter events, 2.0 us)
Async XLA Ops:
  0.6 8.2 %collective-permute-start = (bf16[3,512,256]{2,1,0:T(8,128)(2,1)}, bf16[3,512,256]{2,1,0:T(8,128)(2,1)S(1)}, u32[]{:S(2)}, u32[]{:S(2)}) collective-permute-start(bf16[3,512,256]{2,1,0:T(8,128)(2,1)} %bitcast.23), channel_id=1, source_target_pairs={{0,1},{1,0},{2,3},{3,2},{4,5},{5,4},{6,7},{7,6},{8,9},{9,8},{10,11... | collective-permute-start | bytes 2359304 | tf_op jit(solution)/shard_map/ppermute | solution.py:753
  1.2 14.7 %collective-permute-start.4 = (bf16[512,1024]{1,0:T(8,128)(2,1)}, bf16[512,1024]{1,0:T(8,128)(2,1)S(1)}, u32[]{:S(2)}, u32[]{:S(2)}) collective-permute-start(bf16[512,1024]{1,0:T(8,128)(2,1)} %w1_ref.1), channel_id=1, source_target_pairs={{0,1},{1,0},{2,3},{3,2},{4,5},{5,4},{6,7},{7,6},{8,9},{9,8},{10,11... | collective-permute-start | bytes 3145736 | tf_op jit(solution)/shard_map/ppermute | solution.py:753
  1.3 14.7 %collective-permute-start.5 = (bf16[512,1024]{1,0:T(8,128)(2,1)}, bf16[512,1024]{1,0:T(8,128)(2,1)S(1)}, u32[]{:S(2)}, u32[]{:S(2)}) collective-permute-start(bf16[512,1024]{1,0:T(8,128)(2,1)} %w2_ref.1), channel_id=1, source_target_pairs={{0,1},{1,0},{2,3},{3,2},{4,5},{5,4},{6,7},{7,6},{8,9},{9,8},{10,11... | collective-permute-start | bytes 3145736 | tf_op jit(solution)/shard_map/ppermute | solution.py:753
  1.7 7.1 %collective-permute-start.3 = (bf16[512,256]{1,0:T(8,128)(2,1)}, bf16[512,256]{1,0:T(8,128)(2,1)S(1)}, u32[]{:S(2)}, u32[]{:S(2)}) collective-permute-start(bf16[512,256]{1,0:T(8,128)(2,1)} %pm_ref.3), channel_id=1, source_target_pairs={{0,1},{1,0},{2,3},{3,2},{4,5},{5,4},{6,7},{7,6},{8,9},{9,8},{10,11... | collective-permute-start | bytes 786440 | tf_op jit(solution)/shard_map/ppermute | solution.py:753
  1.8 4.9 %collective-permute-start.2 = (f32[8,169]{1,0:T(8,128)}, f32[8,169]{1,0:T(8,128)S(1)}, u32[]{:S(2)}, u32[]{:S(2)}) collective-permute-start(f32[8,169]{1,0:T(8,128)} %bitcast.26), channel_id=1, source_target_pairs={{0,1},{1,0},{2,3},{3,2},{4,5},{5,4},{6,7},{7,6},{8,9},{9,8},{10,11... | collective-permute-start | bytes 16232 | tf_op jit(solution)/shard_map/ppermute | solution.py:753
  2.2 1.4 %copy-start.14 = (bf16[4,196,512]{2,0,1:T(4,128)(2,1)S(1)}, bf16[4,196,512]{2,0,1:T(4,128)(2,1)}, u32[]{:S(2)}) copy-start(bf16[4,196,512]{2,0,1:T(4,128)(2,1)} %param.31) | copy-start | bytes 2408452
  2.3 4.4 %copy-start.8 = (f32[2,256]{1,0:T(2,128)S(1)}, f32[2,256]{1,0:T(2,128)}, u32[]{:S(2)}) copy-start(f32[2,256]{1,0:T(2,128)} %qvbm_ref.1) | copy-start | bytes 6148
  2.3 4.8 %copy-start.4 = (f32[169,8]{0,1:T(8,128)S(1)}, f32[169,8]{0,1:T(8,128)}, u32[]{:S(2)}) copy-start(f32[169,8]{0,1:T(8,128)} %param.22) | copy-start | bytes 16228
  3.8 4.8 %copy-start.5 = (f32[1024]{0:T(1024)S(1)}, f32[1024]{0:T(1024)}, u32[]{:S(2)}) copy-start(f32[1024]{0:T(1024)} %param.28) | copy-start | bytes 12292
  3.8 5.0 %copy-start.2 = (bf16[512,3,256]{2,0,1:T(8,128)(2,1)S(1)}, bf16[512,3,256]{2,0,1:T(8,128)(2,1)}, u32[]{:S(2)}) copy-start(bf16[512,3,256]{2,0,1:T(8,128)(2,1)} %param.20) | copy-start | bytes 2359300
  3.8 5.0 %copy-start.3 = (bf16[512,256]{1,0:T(8,128)(2,1)S(1)}, bf16[512,256]{1,0:T(8,128)(2,1)}, u32[]{:S(2)}) copy-start(bf16[512,256]{1,0:T(8,128)(2,1)} %pm_ref.3) | copy-start | bytes 786436
  3.9 5.0 %copy-start.6 = (s32[4,196]{1,0:T(4,128)S(1)}, s32[4,196]{1,0:T(4,128)}, u32[]{:S(2)}) copy-start(s32[4,196]{1,0:T(4,128)} %ids_ref.3) | copy-start | bytes 9412
  3.9 5.0 %copy-start.7 = (f32[512]{0:T(512)S(1)}, f32[512]{0:T(512)}, u32[]{:S(2)}) copy-start(f32[512]{0:T(512)} %param.19) | copy-start | bytes 6148
  3.9 5.0 %copy-start.9 = (f32[512]{0:T(512)S(1)}, f32[512]{0:T(512)}, u32[]{:S(2)}) copy-start(f32[512]{0:T(512)} %param.24) | copy-start | bytes 6148
  3.9 5.0 %copy-start.13 = (f32[512]{0:T(512)S(1)}, f32[512]{0:T(512)}, u32[]{:S(2)}) copy-start(f32[512]{0:T(512)} %param.18) | copy-start | bytes 6148
  6.7 1.9 %collective-permute-start.1 = (f32[2,256]{1,0:T(2,128)S(1)}, f32[2,256]{1,0:T(2,128)S(1)}, u32[]{:S(2)}, u32[]{:S(2)}) collective-permute-start(f32[2,256]{1,0:T(2,128)S(1)} %copy-done.8), channel_id=1, source_target_pairs={{0,1},{1,0},{2,3},{3,2},{4,5},{5,4},{6,7},{7,6},{8,9},{9,8},{10,11... | collective-permute-start | bytes 6152 | tf_op jit(solution)/shard_map/ppermute | solution.py:753
  8.7 7.3 %collective-permute-start.6 = (f32[1,1024]{1,0:T(1,128)S(1)}, f32[1,1024]{1,0:T(1,128)S(1)}, u32[]{:S(2)}, u32[]{:S(2)}) collective-permute-start(f32[1,1024]{1,0:T(1,128)S(1)} %bitcast.28), channel_id=1, source_target_pairs={{0,1},{1,0},{2,3},{3,2},{4,5},{5,4},{6,7},{7,6},{8,9},{9,8},{10,11... | collective-permute-start | bytes 12296 | tf_op jit(solution)/shard_map/ppermute | solution.py:753
  8.9 7.1 %copy-start.10 = (f32[512]{0:T(512)S(1)}, f32[512]{0:T(512)}, u32[]{:S(2)}) copy-start(f32[512]{0:T(512)} %param.25) | copy-start | bytes 6148
  8.9 7.1 %copy-start.11 = (f32[512]{0:T(512)S(1)}, f32[512]{0:T(512)}, u32[]{:S(2)}) copy-start(f32[512]{0:T(512)} %param.26) | copy-start | bytes 6148
  16.0 5.4 %copy-start = (bf16[512,1024]{1,0:T(8,128)(2,1)S(1)}, bf16[512,1024]{1,0:T(8,128)(2,1)}, u32[]{:S(2)}) copy-start(bf16[512,1024]{1,0:T(8,128)(2,1)} %w1_ref.1) | copy-start | bytes 3145732
  16.0 5.4 %copy-start.1 = (bf16[512,1024]{1,0:T(8,128)(2,1)S(1)}, bf16[512,1024]{1,0:T(8,128)(2,1)}, u32[]{:S(2)}) copy-start(bf16[512,1024]{1,0:T(8,128)(2,1)} %w2_ref.1) | copy-start | bytes 3145732
  16.0 5.4 %copy-start.12 = (f32[512]{0:T(512)S(1)}, f32[512]{0:T(512)}, u32[]{:S(2)}) copy-start(f32[512]{0:T(512)} %param.30) | copy-start | bytes 6148
  20.8 35.3 %collective-permute-start.24 = (bf16[512,1024]{1,0:T(8,128)(2,1)S(1)}, bf16[512,1024]{1,0:T(8,128)(2,1)S(1)}, u32[]{:S(2)}, u32[]{:S(2)}) collective-permute-start(bf16[512,1024]{1,0:T(8,128)(2,1)S(1)} %get-tuple-element.119), channel_id=1, source_target_pairs={{0,1},{1,0},{2,3},{3,2},{4,5},{5,4},{6,7},{7,6},{8,9},{9,8},{10,11... | collective-permute-start | bytes 3145736 | tf_op jit(solution)/shard_map/ppermute | solution.py:753
  21.3 36.3 %collective-permute-start.25 = (bf16[512,1024]{1,0:T(8,128)(2,1)S(1)}, bf16[512,1024]{1,0:T(8,128)(2,1)S(1)}, u32[]{:S(2)}, u32[]{:S(2)}) collective-permute-start(bf16[512,1024]{1,0:T(8,128)(2,1)S(1)} %get-tuple-element.121), channel_id=1, source_target_pairs={{0,1},{1,0},{2,3},{3,2},{4,5},{5,4},{6,7},{7,6},{8,9},{9,8},{10,11... | collective-permute-start | bytes 3145736 | tf_op jit(solution)/shard_map/ppermute | solution.py:753
  35.3 4.7 %collective-permute-start.16 = (bf16[512,512]{1,0:T(8,128)(2,1)S(1)}, bf16[512,512]{1,0:T(8,128)(2,1)S(1)}, u32[]{:S(2)}, u32[]{:S(2)}) collective-permute-start(bf16[512,512]{1,0:T(8,128)(2,1)S(1)} %get-tuple-element.101), channel_id=1, source_target_pairs={{0,1},{1,0},{2,3},{3,2},{4,5},{5,4},{6,7},{7,6},{8,9},{9,8},{10,11... | collective-permute-start | bytes 1572872 | tf_op jit(solution)/shard_map/ppermute | solution.py:753
  35.8 4.2 %collective-permute-start.17 = (bf16[512,512]{1,0:T(8,128)(2,1)S(1)}, bf16[512,512]{1,0:T(8,128)(2,1)S(1)}, u32[]{:S(2)}, u32[]{:S(2)}) collective-permute-start(bf16[512,512]{1,0:T(8,128)(2,1)S(1)} %get-tuple-element.103), channel_id=1, source_target_pairs={{0,1},{1,0},{2,3},{3,2},{4,5},{5,4},{6,7},{7,6},{8,9},{9,8},{10,11... | collective-permute-start | bytes 1572872 | tf_op jit(solution)/shard_map/ppermute | solution.py:753
  39.5 5.3 %collective-permute-start.9 = (f32[16,512]{1,0:T(8,128)S(1)}, f32[16,512]{1,0:T(8,128)S(1)}, u32[]{:S(2)}, u32[]{:S(2)}) collective-permute-start(f32[16,512]{1,0:T(8,128)S(1)} %get-tuple-element.97), channel_id=1, source_target_pairs={{0,1},{1,0},{2,3},{3,2},{4,5},{5,4},{6,7},{7,6},{8,9},{9,8},{10,11... | collective-permute-start | bytes 98312 | tf_op jit(solution)/shard_map/ppermute | solution.py:753
  40.7 26.3 %collective-permute-start.18 = (bf16[128,1024]{1,0:T(8,128)(2,1)S(1)}, bf16[128,1024]{1,0:T(8,128)(2,1)S(1)}, u32[]{:S(2)}, u32[]{:S(2)}) collective-permute-start(bf16[128,1024]{1,0:T(8,128)(2,1)S(1)} %get-tuple-element.104), channel_id=1, source_target_pairs={{0,2},{2,0},{4,6},{6,4},{8,10},{10,8},{12,14},{14,12},{16,18},{18,... | collective-permute-start | bytes 786440 | tf_op jit(solution)/shard_map/ppermute | solution.py:628
  43.4 25.1 %collective-permute-start.19 = (bf16[128,1024]{1,0:T(8,128)(2,1)S(1)}, bf16[128,1024]{1,0:T(8,128)(2,1)S(1)}, u32[]{:S(2)}, u32[]{:S(2)}) collective-permute-start(bf16[128,1024]{1,0:T(8,128)(2,1)S(1)} %get-tuple-element.105), channel_id=1, source_target_pairs={{0,4},{2,6},{4,0},{6,2},{8,12},{10,14},{12,8},{14,10},{16,20},{18,... | collective-permute-start | bytes 786440 | tf_op jit(solution)/shard_map/ppermute | solution.py:628
  45.4 6.8 %collective-permute-start.12 = (f32[16,512]{1,0:T(8,128)S(1)}, f32[16,512]{1,0:T(8,128)S(1)}, u32[]{:S(2)}, u32[]{:S(2)}) collective-permute-start(f32[16,512]{1,0:T(8,128)S(1)} %shard_map.279.a_ref), channel_id=1, source_target_pairs={{0,6},{2,4},{4,2},{6,0},{8,14},{10,12},{12,10},{14,8},{16,22},{18,... | collective-permute-start | bytes 98312 | tf_op jit(solution)/shard_map/ppermute | solution.py:628
  52.2 3.9 %collective-permute-start.11 = (f32[16,512]{1,0:T(8,128)S(1)}, f32[16,512]{1,0:T(8,128)S(1)}, u32[]{:S(2)}, u32[]{:S(2)}) collective-permute-start(f32[16,512]{1,0:T(8,128)S(1)} %shard_map.279.a_ref), channel_id=1, source_target_pairs={{0,4},{2,6},{4,0},{6,2},{8,12},{10,14},{12,8},{14,10},{16,20},{18,... | collective-permute-start | bytes 98312 | tf_op jit(solution)/shard_map/ppermute | solution.py:628
  56.1 45.9 %collective-permute-start.8 = (f32[2,196,512]{2,0,1:T(2,128)S(1)}, f32[2,196,512]{2,0,1:T(2,128)S(1)}, u32[]{:S(2)}, u32[]{:S(2)}) collective-permute-start(f32[2,196,512]{2,0,1:T(2,128)S(1)} %copy.39), channel_id=1, source_target_pairs={{0,1},{1,0},{2,3},{3,2},{4,5},{5,4},{6,7},{7,6},{8,9},{9,8},{10,11... | collective-permute-start | bytes 2408456 | tf_op jit(solution)/shard_map/ppermute | solution.py:753
  56.1 12.6 %collective-permute-start.20 = (bf16[128,1024]{1,0:T(8,128)(2,1)S(1)}, bf16[128,1024]{1,0:T(8,128)(2,1)S(1)}, u32[]{:S(2)}, u32[]{:S(2)}) collective-permute-start(bf16[128,1024]{1,0:T(8,128)(2,1)S(1)} %get-tuple-element.106), channel_id=1, source_target_pairs={{0,6},{2,4},{4,2},{6,0},{8,14},{10,12},{12,10},{14,8},{16,22},{18,... | collective-permute-start | bytes 786440 | tf_op jit(solution)/shard_map/ppermute | solution.py:628
  57.6 7.7 %collective-permute-start.10 = (f32[16,512]{1,0:T(8,128)S(1)}, f32[16,512]{1,0:T(8,128)S(1)}, u32[]{:S(2)}, u32[]{:S(2)}) collective-permute-start(f32[16,512]{1,0:T(8,128)S(1)} %shard_map.279.a_ref), channel_id=1, source_target_pairs={{0,2},{2,0},{4,6},{6,4},{8,10},{10,8},{12,14},{14,12},{16,18},{18,... | collective-permute-start | bytes 98312 | tf_op jit(solution)/shard_map/ppermute | solution.py:628
  65.3 14.8 %collective-permute-start.26 = (bf16[128,2048]{1,0:T(8,128)(2,1)S(1)}, bf16[128,2048]{1,0:T(8,128)(2,1)S(1)}, u32[]{:S(2)}, u32[]{:S(2)}) collective-permute-start(bf16[128,2048]{1,0:T(8,128)(2,1)S(1)} %get-tuple-element.122), channel_id=1, source_target_pairs={{0,2},{2,0},{4,6},{6,4},{8,10},{10,8},{12,14},{14,12},{16,18},{18,... | collective-permute-start | bytes 1572872 | tf_op jit(solution)/shard_map/ppermute | solution.py:628
  67.0 24.4 %collective-permute-start.27 = (bf16[128,2048]{1,0:T(8,128)(2,1)S(1)}, bf16[128,2048]{1,0:T(8,128)(2,1)S(1)}, u32[]{:S(2)}, u32[]{:S(2)}) collective-permute-start(bf16[128,2048]{1,0:T(8,128)(2,1)S(1)} %get-tuple-element.123), channel_id=1, source_target_pairs={{0,4},{2,6},{4,0},{6,2},{8,12},{10,14},{12,8},{14,10},{16,20},{18,... | collective-permute-start | bytes 1572872 | tf_op jit(solution)/shard_map/ppermute | solution.py:628
  68.4 25.5 %collective-permute-start.28 = (bf16[128,2048]{1,0:T(8,128)(2,1)S(1)}, bf16[128,2048]{1,0:T(8,128)(2,1)S(1)}, u32[]{:S(2)}, u32[]{:S(2)}) collective-permute-start(bf16[128,2048]{1,0:T(8,128)(2,1)S(1)} %get-tuple-element.124), channel_id=1, source_target_pairs={{0,6},{2,4},{4,2},{6,0},{8,14},{10,12},{12,10},{14,8},{16,22},{18,... | collective-permute-start | bytes 1572872 | tf_op jit(solution)/shard_map/ppermute | solution.py:628
  68.8 32.0 %collective-permute-start.7 = (bf16[2,196,512]{2,1,0:T(8,128)(2,1)S(1)}, bf16[2,196,512]{2,1,0:T(8,128)(2,1)S(1)}, u32[]{:S(2)}, u32[]{:S(2)}) collective-permute-start(bf16[2,196,512]{2,1,0:T(8,128)(2,1)S(1)} %get-tuple-element.81.own_ref), channel_id=1, source_target_pairs={{0,1},{1,0},{2,3},{3,2},{4,5},{5,4},{6,7},{7,6},{8,9},{9,8},{10,11... | collective-permute-start | bytes 1204232 | tf_op jit(solution)/shard_map/ppermute | solution.py:753
  80.1 17.1 %collective-permute-start.15 = (f32[16,512]{1,0:T(8,128)S(1)}, f32[16,512]{1,0:T(8,128)S(1)}, u32[]{:S(2)}, u32[]{:S(2)}) collective-permute-start(f32[16,512]{1,0:T(8,128)S(1)} %shard_map.280.refs_0_), channel_id=1, source_target_pairs={{0,24},{2,26},{4,28},{6,30},{8,16},{10,18},{12,20},{14,22},{16,8},... | collective-permute-start | bytes 98312 | tf_op jit(solution)/shard_map/ppermute | solution.py:628
  91.4 6.2 %collective-permute-start.14 = (f32[16,512]{1,0:T(8,128)S(1)}, f32[16,512]{1,0:T(8,128)S(1)}, u32[]{:S(2)}, u32[]{:S(2)}) collective-permute-start(f32[16,512]{1,0:T(8,128)S(1)} %shard_map.280.refs_0_), channel_id=1, source_target_pairs={{0,16},{2,18},{4,20},{6,22},{8,24},{10,26},{12,28},{14,30},{16,0},... | collective-permute-start | bytes 98312 | tf_op jit(solution)/shard_map/ppermute | solution.py:628
  94.0 5.7 %collective-permute-start.13 = (f32[16,512]{1,0:T(8,128)S(1)}, f32[16,512]{1,0:T(8,128)S(1)}, u32[]{:S(2)}, u32[]{:S(2)}) collective-permute-start(f32[16,512]{1,0:T(8,128)S(1)} %shard_map.280.refs_0_), channel_id=1, source_target_pairs={{0,8},{2,10},{4,12},{6,14},{8,0},{10,2},{12,4},{14,6},{16,24},{18,... | collective-permute-start | bytes 98312 | tf_op jit(solution)/shard_map/ppermute | solution.py:628
  97.2 5.5 %collective-permute-start.21 = (bf16[32,1024]{1,0:T(8,128)(2,1)S(1)}, bf16[32,1024]{1,0:T(8,128)(2,1)S(1)}, u32[]{:S(2)}, u32[]{:S(2)}) collective-permute-start(bf16[32,1024]{1,0:T(8,128)(2,1)S(1)} %get-tuple-element.108), channel_id=1, source_target_pairs={{0,8},{2,10},{4,12},{6,14},{8,0},{10,2},{12,4},{14,6},{16,24},{18,... | collective-permute-start | bytes 196616 | tf_op jit(solution)/shard_map/ppermute | solution.py:628
  97.7 17.6 %collective-permute-start.29 = (bf16[32,2048]{1,0:T(8,128)(2,1)S(1)}, bf16[32,2048]{1,0:T(8,128)(2,1)S(1)}, u32[]{:S(2)}, u32[]{:S(2)}) collective-permute-start(bf16[32,2048]{1,0:T(8,128)(2,1)S(1)} %get-tuple-element.126), channel_id=1, source_target_pairs={{0,8},{2,10},{4,12},{6,14},{8,0},{10,2},{12,4},{14,6},{16,24},{18,... | collective-permute-start | bytes 393224 | tf_op jit(solution)/shard_map/ppermute | solution.py:628
  99.6 15.7 %collective-permute-start.30 = (bf16[32,2048]{1,0:T(8,128)(2,1)S(1)}, bf16[32,2048]{1,0:T(8,128)(2,1)S(1)}, u32[]{:S(2)}, u32[]{:S(2)}) collective-permute-start(bf16[32,2048]{1,0:T(8,128)(2,1)S(1)} %get-tuple-element.127), channel_id=1, source_target_pairs={{0,16},{2,18},{4,20},{6,22},{8,24},{10,26},{12,28},{14,30},{16,0},... | collective-permute-start | bytes 393224 | tf_op jit(solution)/shard_map/ppermute | solution.py:628
  100.8 14.5 %collective-permute-start.31 = (bf16[32,2048]{1,0:T(8,128)(2,1)S(1)}, bf16[32,2048]{1,0:T(8,128)(2,1)S(1)}, u32[]{:S(2)}, u32[]{:S(2)}) collective-permute-start(bf16[32,2048]{1,0:T(8,128)(2,1)S(1)} %get-tuple-element.128), channel_id=1, source_target_pairs={{0,24},{2,26},{4,28},{6,30},{8,16},{10,18},{12,20},{14,22},{16,8},... | collective-permute-start | bytes 393224 | tf_op jit(solution)/shard_map/ppermute | solution.py:628
  102.1 12.0 %collective-permute-start.22 = (bf16[32,1024]{1,0:T(8,128)(2,1)S(1)}, bf16[32,1024]{1,0:T(8,128)(2,1)S(1)}, u32[]{:S(2)}, u32[]{:S(2)}) collective-permute-start(bf16[32,1024]{1,0:T(8,128)(2,1)S(1)} %get-tuple-element.109), channel_id=1, source_target_pairs={{0,16},{2,18},{4,20},{6,22},{8,24},{10,26},{12,28},{14,30},{16,0},... | collective-permute-start | bytes 196616 | tf_op jit(solution)/shard_map/ppermute | solution.py:628
  102.6 11.4 %collective-permute-start.23 = (bf16[32,1024]{1,0:T(8,128)(2,1)S(1)}, bf16[32,1024]{1,0:T(8,128)(2,1)S(1)}, u32[]{:S(2)}, u32[]{:S(2)}) collective-permute-start(bf16[32,1024]{1,0:T(8,128)(2,1)S(1)} %get-tuple-element.110), channel_id=1, source_target_pairs={{0,24},{2,26},{4,28},{6,30},{8,16},{10,18},{12,20},{14,22},{16,8},... | collective-permute-start | bytes 196616 | tf_op jit(solution)/shard_map/ppermute | solution.py:628

commit v3 on v2

--- a/solution.py
+++ b/solution.py
@@ -260,7 +260,7 @@
         att_ref[rows, :] = own_groups(tn(probs, v_all)).astype(BF16)
         return carry
 
-    lax.fori_loop(0, images * WINS, one_window, 0, unroll=2)
+    lax.fori_loop(0, images * WINS, one_window, 0, unroll=True)
     back = scatter_matrix()
     for image in range(images):
         merged_ref[image * TPAD : (image + 1) * TPAD, :] = nn(
@@ -430,7 +430,7 @@
             gqkv_ref[rows, base + 2 * chan : base + 3 * chan] = g_v[:, cols].astype(BF16)
         return carry
 
-    lax.fori_loop(0, images * WINS, one_window, 0, unroll=2)
+    lax.fori_loop(0, images * WINS, one_window, 0, unroll=True)
     sums_ref[...] = jnp.zeros(sums_ref.shape, F32)
     sums_ref[0:1, :] = jnp.sum(qsum_ref[...], axis=0, keepdims=True)
     sums_ref[1:2, :] = jnp.sum(vsum_ref[...], axis=0, keepdims=True)
@@ -513,12 +513,7 @@
         pack_ref[low:, chan : chan + rows_half] = half[heads // 2 :]
 
 
-def unpack_kernel(parts, sel_ref, *refs):
-    ins, outs = refs[:parts], refs[parts:]
-    if parts == 2:
-        total = ins[0][...] + ins[1][...]
-    else:
-        total = (ins[0][...] + ins[1][...]) + (ins[2][...] + ins[3][...])
+def spread_small(total, outs):
     for at in range(6):
         outs[at][...] = total[at : at + 1]
     qv_ref, b1_ref, table_ref = outs[6:]
@@ -531,6 +526,16 @@
     low = total.shape[0] - heads // 2
     table_ref[: heads // 2, :] = total[low:, :entries]
     table_ref[heads // 2 :, :] = total[low:, chan : chan + entries]
+
+
+def in_pairs(terms):
+    if len(terms) == 2:
+        return terms[0] + terms[1]
+    return (terms[0] + terms[1]) + (terms[2] + terms[3])
+
+
+def unpack_kernel(parts, sel_ref, *refs):
+    spread_small(in_pairs([ref[...] for ref in refs[:parts]]), refs[parts:])
 
 
 def rows_at(ref, start, rows):
@@ -560,7 +565,7 @@
             (slice(half, got.shape[1]), pairs[2], pairs[3]),
         ):
             total = rows_at(first, far, rows) + rows_at(second, far, rows) + got[:, cols]
-            out_ref[:, cols] = total.astype(out_ref.dtype)
+            out_ref[:rows, cols] = total.astype(out_ref.dtype)
 
 
 def total_kernel(parts, sel_ref, own_ref, *refs):
@@ -578,6 +583,28 @@
             at += width
 
 
+def fan_small_kernel(rows, sends, terms, sel_ref, *refs):
+    ins, small, outs = refs[: -terms - sends - 2], refs[-terms - sends - 2 : -sends - 2], refs[-sends - 2 :]
+    fan_kernel(rows, sends, sel_ref, *ins, *outs[:-1])
+    total = in_pairs([ref[...] for ref in small]).astype(BF16)
+    half, width = total.shape[0] // 2, total.shape[1]
+    for out_ref in outs[:sends]:
+        out_ref[rows:, :width] = total[:half]
+        out_ref[rows:, width:] = total[half:]
+    outs[-1][...] = total.astype(F32)
+
+
+def total_small_kernel(parts, main, sel_ref, own_ref, small_ref, *refs):
+    rows, width = own_ref.shape[0], small_ref.shape[1]
+    received = refs[: parts - 1]
+    total_kernel(parts, sel_ref, own_ref, *[ref.at[:rows, :] for ref in received], *refs[parts - 1 :][:main])
+    terms = [small_ref[...]]
+    for ref in received:
+        low = ref[rows:, :].astype(F32)
+        terms.append(jnp.concatenate([low[:, :width], low[:, width:]], axis=0))
+    spread_small(in_pairs(terms), refs[parts - 1 :][main:])
+
+
 def join_kernel(sel_ref, own_ref, other_ref, out_ref):
     images = own_ref.shape[0]
     for image in range(out_ref.shape[1]):
@@ -657,7 +684,7 @@
     return total(addends)
 
 
-def all_sum(sel, value, axis, count):
+def all_sum(sel, value, axis, count, last):
     mask = 1
     while True:
         size = 4 if 4 * mask <= count else 2
@@ -665,13 +692,13 @@
         for s in range(1, size):
             terms.append(xor_exchange(value, axis, count, s * mask))
         mask *= size
-        if mask >= count:
+        if mask >= last:
             return terms
         kernel = four_kernel if size == 4 else pair_kernel
         (value,) = call(kernel, sel, terms, [struct(value.shape, F32)], [], 10**5, 2)
 
 
-def scatter_pairs(sel, pairs, axis, count, digits, outs):
+def scatter_pairs(sel, pairs, axis, count, digits, outs, small=(), small_outs=()):
     (stride, size), (far_stride, far_size) = digits
     (a0, a1), (b0, b1) = pairs
     arrays = [a0, a1, b0, b1]
@@ -695,17 +722,33 @@
         4,
     )
     wide = exchange(sends, stride)
-    *sends, own = call(
-        functools.partial(fan_kernel, rows, far_size - 1),
+    own = [struct((rows, cols), F32)]
+    if not small:
+        *sends, own = call(
+            functools.partial(fan_kernel, rows, far_size - 1),
+            sel,
+            arrays + wide,
+            [struct((rows, cols), BF16)] * (far_size - 1) + own,
+            [],
+            10**6,
+            4,
+        )
+        parts = [own] + exchange(sends, far_stride)
+        kernel = functools.partial(total_kernel, len(parts))
+        return call(kernel, sel, parts, outs, [], 10**6, 4)
+    sent = struct((rows + small[0].shape[0] // 2, cols), BF16)
+    *sends, own, own_small = call(
+        functools.partial(fan_small_kernel, rows, far_size - 1, len(small)),
         sel,
-        arrays + wide,
-        [struct((rows, cols), BF16)] * (far_size - 1) + [struct((rows, cols), F32)],
+        arrays + wide + list(small),
+        [sent] * (far_size - 1) + own + [struct(small[0].shape, F32)],
         [],
         10**6,
         4,
     )
-    parts = [own] + exchange(sends, far_stride)
-    return call(functools.partial(total_kernel, len(parts)), sel, parts, outs, [], 10**6, 4)
+    parts = [own, own_small] + exchange(sends, far_stride)
+    kernel = functools.partial(total_small_kernel, len(parts) - 1, len(outs))
+    return call(kernel, sel, parts, list(outs) + list(small_outs), [], 10**6, 4)
 
 
 def per_device(n_dp, n_tensor, *args):
@@ -904,18 +947,6 @@
 
     got_qk = swap(gqko)
     got_vp = swap(gvpo)
-    if by_pairs:
-        outs = [struct((3, share, chan), F32), struct((share, chan), F32)]
-        sent_qkv, sent_proj = scatter_pairs(
-            sel, ((gqkm, got_qk), (gvpm, got_vp)), "dp", n_dp, digits, outs
-        )
-    else:
-        sent_qk = scatter_sum((gqkm, got_qk), "dp", n_dp, digits)
-        sent_vp = scatter_sum((gvpm, got_vp), "dp", n_dp, digits)
-        sent_qkv = jnp.stack([sent_qk[:, :chan], sent_qk[:, chan:], sent_vp[:, :chan]], axis=0)
-        sent_proj = sent_vp[:, chan:]
-    sent_qkv = sent_qkv.transpose(1, 0, 2)
-
     ins = (tokens, gres, gqkv, wm, wo, row(norm1_gain), gbias, sums_two, sums_qv, gbm, gbo)
     pack = struct((-(-(7 + hidden // width + heads // 2) // 8) * 8, width), F32)
     outs = (struct((images, TOK, width), F32), pack, pack)
@@ -936,15 +967,28 @@
 
     got = swap(theirs)
     (small,) = call(pair_kernel, sel, [small, got], [struct(small.shape, F32)], [], 10**5, 2)
-    terms = all_sum(sel, small, "dp", n_dp)
-    outs = (struct((1, width), F32),) * 6 + (
+    small_outs = (struct((1, width), F32),) * 6 + (
         struct((2, chan), F32),
         struct((1, hidden), F32),
         struct((heads, entries), F32),
     )
-    *vectors, sum_qv, sum_b1, sum_table = call(
-        functools.partial(unpack_kernel, len(terms)), sel, terms, outs, [], 10**5, 2
-    )
+    pairs = ((gqkm, got_qk), (gvpm, got_vp))
+    if by_pairs and 4 * chan == 2 * width:
+        terms = all_sum(sel, small, "dp", n_dp, digits[0][1])
+        outs = [struct((3, share, chan), F32), struct((share, chan), F32)]
+        sent_qkv, sent_proj, *small = scatter_pairs(
+            sel, pairs, "dp", n_dp, digits, outs, terms, small_outs
+        )
+    else:
+        terms = all_sum(sel, small, "dp", n_dp, n_dp)
+        kernel = functools.partial(unpack_kernel, len(terms))
+        small = call(kernel, sel, terms, small_outs, [], 10**5, 2)
+        sent_qk = scatter_sum(pairs[0], "dp", n_dp, digits)
+        sent_vp = scatter_sum(pairs[1], "dp", n_dp, digits)
+        sent_qkv = jnp.stack([sent_qk[:, :chan], sent_qk[:, chan:], sent_vp[:, :chan]], axis=0)
+        sent_proj = sent_vp[:, chan:]
+    sent_qkv = sent_qkv.transpose(1, 0, 2)
+    *vectors, sum_qv, sum_b1, sum_table = small
     vectors = [vec.reshape(width) for vec in vectors]
     return (
         output,

time: 117 us -> 107 us (0.915)
  starting transfers between devices: 29.3 us -> 25.2 us
  Pallas kernels: 43.5 us -> 39.6 us
  waiting for transfers between devices: 40.4 us -> 38.4 us
    ppermute x18 -> x15, starting transfers between devices: 25.6 us -> 21.5 us  [xor_exchange(): return lax.ppermute(value, axis, [(i, i ^ mask) for i in range(count)])]
    pallas_call x17 -> x15, Pallas kernels: 43.5 us -> 39.6 us  [call(): pl.pallas_call(kernel, in_specs=[pl.BlockSpec(memory_space=pltpu.SMEM)] +...]
    ppermute x18 -> x15, waiting for transfers between devices: 37.5 us -> 34.7 us  [xor_exchange(): return lax.ppermute(value, axis, [(i, i ^ mask) for i in range(count)])]
  transfers between devices with their start and end apart: 32 -> 29, of which waited for: 8 -> 7; matrix products, arithmetic and copies ran while one was open for 2% -> 2% of each run, Pallas kernels for 32% -> 31%
where the time goes in v3:
time: 107 us
  Pallas kernels  39.6 us (37%)
  waiting for transfers between devices  38.4 us (36%)
  starting transfers between devices  25.2 us (24%)
  local copies, waits for them, and re-layouts  2.57 us (2%)
    pallas_call x15, Pallas kernels, call(): pl.pallas_call(kernel, in_specs=[pl.BlockSpec(memory_space=pltpu.SMEM)] +...  39.6 us
    ppermute x15, waiting for transfers between devices, xor_exchange(): return lax.ppermute(value, axis, [(i, i ^ mask) for i in range(count)])  34.7 us
    ppermute x15, starting transfers between devices, xor_exchange(): return lax.ppermute(value, axis, [(i, i ^ mask) for i in range(count)])  21.5 us
    ppermute x14, starting transfers between devices, swap(): return lax.ppermute(value, 'tensor', [(i, i ^ 1) for i in range(n_tensor)])  3.77 us
    ppermute x14, waiting for transfers between devices, swap(): return lax.ppermute(value, 'tensor', [(i, i ^ 1) for i in range(n_tensor)])  3.7 us
  transfers between devices with their start and end apart: 29, of which 7 were waited for; matrix products, arithmetic and copies ran while one was open for 2% of the time, Pallas kernels for 31%

profile of v3, /device:TPU:0, one launch (start us, length us, event | category | flops | bytes accessed | tf_op | source)
XLA Modules:
  0.0 106.9 jit_solution(14176680664570708925)
XLA Ops:
  0.6 0.6 collective-permute-start
  1.3 0.4 collective-permute-start.5
  1.8 0.4 collective-permute-start.2
  2.3 1.3 %copy.35.tok_ref = bf16[4,196,512]{2,1,0:T(8,128)(2,1)S(1)} copy(bf16[4,196,512]{2,0,1:T(4,128)(2,1)} %param.16) | data formatting | bytes 1605632 | tf_op args[0]
  3.7 0.1 copy.37.cot_ref
  3.9 2.8 %collective-permute-done.2.other_ref = f32[8,169]{1,0:T(8,128)S(1)} collective-permute-done((f32[8,169]{1,0:T(8,128)}, f32[8,169]{1,0:T(8,128)S(1)}, u32[]{:S(2)}, u32[]{:S(2)}) %collective-permute-start.2) | collective-permute-done | bytes 5440 | tf_op jit(solution)/shard_map/ppermute | solution.py:796
  6.7 0.4 collective-permute-start.1
  7.1 1.5 %shard_map.271.bias_ref = f32[512,128]{1,0:T(8,128)S(1)} custom-call(s32[3]{0:T(128)S(1)} %pad_add_fusion.sel_ref.me_ref, f32[8,169]{1,0:T(8,128)S(1)} %bitcast.27, f32[8,169]{1,0:T(8,128)S(1)} %collective-permute-done.2.other_ref), custom_call_target="tpu_custom_call" | custom-call | flops 1000000000 | bytes 272960 | tf_op jit(solution)/shard_map/pallas_call | solution.py:634
  8.7 0.1 collective-permute-start.6
  8.9 6.1 %shard_map.272 = (bf16[512,512]{1,0:T(8,128)(2,1)S(1)}, bf16[512,512]{1,0:T(8,128)(2,1)S(1)}, bf16[512,512]{1,0:T(8,128)(2,1)S(1)}, bf16[512,512]{1,0:T(8,128)(2...) custom-call(s32[3]{0:T(128)S(1)} %pad_add_fusion.sel_ref.me_ref, ...), custom_call_target="tpu_custom_call" | custom-call | flops 3000000000 | bytes 6583360 | tf_op jit(solution)/shard_map/pallas_call | solution.py:634
  15.1 4.9 %shard_map.273 = (bf16[512,1024]{1,0:T(8,128)(2,1)S(1)}, bf16[512,1024]{1,0:T(8,128)(2,1)S(1)}, f32[1,1024]{1,0:T(1,128)S(1)}, bf16[416,512]{1,0:T(8,128)(2,1)S(...) custom-call(s32[3]{0:T(128)S(1)} %pad_add_fusion.sel_ref.me_ref, ...), custom_call_target="tpu_custom_call" | custom-call | flops 3000000000 | bytes 9269248 | tf_op jit(solution)/shard_map/pallas_call | solution.py:634
  20.0 0.5 collective-permute-start.21
  20.6 4.9 %shard_map.274 = (bf16[512,1024]{1,0:T(8,128)(2,1)S(1)}, bf16[512,1024]{1,0:T(8,128)(2,1)S(1)}, f32[1,1024]{1,0:T(1,128)S(1)}, bf16[2,196,512]{2,1,0:T(8,128)(2,...) custom-call(s32[3]{0:T(128)S(1)} %pad_add_fusion.sel_ref.me_ref, f32[416,512]{1,0:T(8,128)S(1)} %get-tuple-element.75.resid_ref, ...), custom_call_target="tpu_custom_call" | custom-call | flops 3000000000 | bytes 10541056 | tf_op jit(solution)/shard_map/pallas_call | solution.py:634
  25.5 7.6 %shard_map.276 = (bf16[512,512]{1,0:T(8,128)(2,1)S(1)}, bf16[512,512]{1,0:T(8,128)(2,1)S(1)}, bf16[512,512]{1,0:T(8,128)(2,1)S(1)}, bf16[512,512]{1,0:T(8,128)(2...) custom-call(s32[3]{0:T(128)S(1)} %pad_add_fusion.sel_ref.me_ref, ...), custom_call_target="tpu_custom_call" | custom-call | flops 5000000000 | bytes 8145984 | tf_op jit(solution)/shard_map/pallas_call | solution.py:634
  33.0 0.5 collective-permute-start.9
  33.6 3.7 %shard_map.277 = (f32[2,196,512]{2,1,0:T(8,128)S(1)}, f32[16,512]{1,0:T(8,128)S(1)}, f32[16,512]{1,0:T(8,128)S(1)}) custom-call(s32[3]{0:T(128)S(1)} %pad_add_fusion.sel_ref.me_ref, bf16[4,196,512]{2,1,0:T(8,128)(2,1)S(1)} %copy.35.tok_ref, f32[416,512]{1,0:T(8,128)S(1)} %get-tuple-element.83.gres_ref, bf16[512,1536]{1,0:T(8,128)(2,1)S(1)} %get-tuple-element.90.gqkv_ref, ...), custom_call_target="tpu_custom_call" | custom-call | flops 2000000000 | bytes 5974016 | tf_op jit(solution)/shard_map/pallas_call | solution.py:634
  37.3 0.4 collective-permute-start.14
  37.7 0.9 collective-permute-done.14.b_ref
  38.6 0.5 shard_map.280.refs_7_
  39.1 3.8 %collective-permute-start.17 = (f32[16,512]{1,0:T(8,128)S(1)}, f32[16,512]{1,0:T(8,128)S(1)}, u32[]{:S(2)}, u32[]{:S(2)}) collective-permute-start(f32[16,512]{1,0:T(8,128)S(1)} %shard_map.280.refs_7_), channel_id=1, source_target_pairs={{0,6},{2,4},{4,2},{6,0},{8,14},{10,12},{12,10},{14,8},{16,22},{18,... | collective-permute-start | bytes 98312 | tf_op jit(solution)/shard_map/ppermute | solution.py:655
  43.0 0.5 collective-permute-start.16
  43.5 0.7 shard_map.279
  44.2 0.2 collective-permute-start.11
  44.4 0.4 collective-permute-done.17.refs_10_
  44.9 2.0 %collective-permute-start.12 = (bf16[128,1024]{1,0:T(8,128)(2,1)S(1)}, bf16[128,1024]{1,0:T(8,128)(2,1)S(1)}, u32[]{:S(2)}, u32[]{:S(2)}) collective-permute-start(bf16[128,1024]{1,0:T(8,128)(2,1)S(1)} %get-tuple-element.102), channel_id=1, source_target_pairs={{0,4},{2,6},{4,0},{6,2},{8,12},{10,14},{12,8},{14,10},{16,20},{18,... | collective-permute-start | bytes 786440 | tf_op jit(solution)/shard_map/ppermute | solution.py:655
  46.9 0.8 copy.39
  47.8 1.5 %collective-permute-start.13 = (bf16[128,1024]{1,0:T(8,128)(2,1)S(1)}, bf16[128,1024]{1,0:T(8,128)(2,1)S(1)}, u32[]{:S(2)}, u32[]{:S(2)}) collective-permute-start(bf16[128,1024]{1,0:T(8,128)(2,1)S(1)} %get-tuple-element.103), channel_id=1, source_target_pairs={{0,6},{2,4},{4,2},{6,0},{8,14},{10,12},{12,10},{14,8},{16,22},{18,... | collective-permute-start | bytes 786440 | tf_op jit(solution)/shard_map/ppermute | solution.py:655
  49.3 0.1 collective-permute-start.15
  49.5 0.9 shard_map.283
  50.4 8.1 %collective-permute-done.15.refs_8_ = f32[16,512]{1,0:T(8,128)S(1)} collective-permute-done((f32[16,512]{1,0:T(8,128)S(1)}, f32[16,512]{1,0:T(8,128)S(1)}, u32[]{:S(2)}, u32[]{:S(2)}) %collective-permute-start.15) | collective-permute-done | bytes 32800 | tf_op jit(solution)/shard_map/ppermute | solution.py:655
  58.5 0.4 collective-permute-start.23
  58.9 1.6 %collective-permute-start.24 = (bf16[128,2048]{1,0:T(8,128)(2,1)S(1)}, bf16[128,2048]{1,0:T(8,128)(2,1)S(1)}, u32[]{:S(2)}, u32[]{:S(2)}) collective-permute-start(bf16[128,2048]{1,0:T(8,128)(2,1)S(1)} %get-tuple-element.125), channel_id=1, source_target_pairs={{0,4},{2,6},{4,0},{6,2},{8,12},{10,14},{12,8},{14,10},{16,20},{18,... | collective-permute-start | bytes 1572872 | tf_op jit(solution)/shard_map/ppermute | solution.py:655
  60.5 1.4 %collective-permute-start.25 = (bf16[128,2048]{1,0:T(8,128)(2,1)S(1)}, bf16[128,2048]{1,0:T(8,128)(2,1)S(1)}, u32[]{:S(2)}, u32[]{:S(2)}) collective-permute-start(bf16[128,2048]{1,0:T(8,128)(2,1)S(1)} %get-tuple-element.126), channel_id=1, source_target_pairs={{0,6},{2,4},{4,2},{6,0},{8,14},{10,12},{12,10},{14,8},{16,22},{18,... | collective-permute-start | bytes 1572872 | tf_op jit(solution)/shard_map/ppermute | solution.py:655
  62.0 0.7 shard_map.281
  62.7 10.6 %collective-permute-done.23.refs_4_ = bf16[128,2048]{1,0:T(8,128)(2,1)S(1)} collective-permute-done((bf16[128,2048]{1,0:T(8,128)(2,1)S(1)}, bf16[128,2048]{1,0:T(8,128)(2,1)S(1)}, u32[]{:S(2)}, u32[]{:S(2)}) %collective-permute-start.23) | collective-permute-done | bytes 524320 | tf_op jit(solution)/shard_map/ppermute | solution.py:655
  73.3 1.6 %collective-permute-start.18 = (bf16[40,1024]{1,0:T(8,128)(2,1)S(1)}, bf16[40,1024]{1,0:T(8,128)(2,1)S(1)}, u32[]{:S(2)}, u32[]{:S(2)}) collective-permute-start(bf16[40,1024]{1,0:T(8,128)(2,1)S(1)} %get-tuple-element.108), channel_id=1, source_target_pairs={{0,8},{2,10},{4,12},{6,14},{8,0},{10,2},{12,4},{14,6},{16,24},{18,... | collective-permute-start | bytes 245768 | tf_op jit(solution)/shard_map/ppermute | solution.py:655
  74.8 8.6 %collective-permute-done.24.refs_5_ = bf16[128,2048]{1,0:T(8,128)(2,1)S(1)} collective-permute-done((bf16[128,2048]{1,0:T(8,128)(2,1)S(1)}, bf16[128,2048]{1,0:T(8,128)(2,1)S(1)}, u32[]{:S(2)}, u32[]{:S(2)}) %collective-permute-start.24) | collective-permute-done | bytes 524320 | tf_op jit(solution)/shard_map/ppermute | solution.py:655
  83.5 0.9 shard_map.284
  84.3 1.8 %collective-permute-start.26 = (bf16[32,2048]{1,0:T(8,128)(2,1)S(1)}, bf16[32,2048]{1,0:T(8,128)(2,1)S(1)}, u32[]{:S(2)}, u32[]{:S(2)}) collective-permute-start(bf16[32,2048]{1,0:T(8,128)(2,1)S(1)} %get-tuple-element.128), channel_id=1, source_target_pairs={{0,8},{2,10},{4,12},{6,14},{8,0},{10,2},{12,4},{14,6},{16,24},{18,... | collective-permute-start | bytes 393224 | tf_op jit(solution)/shard_map/ppermute | solution.py:655
  86.1 2.6 %collective-permute-start.27 = (bf16[32,2048]{1,0:T(8,128)(2,1)S(1)}, bf16[32,2048]{1,0:T(8,128)(2,1)S(1)}, u32[]{:S(2)}, u32[]{:S(2)}) collective-permute-start(bf16[32,2048]{1,0:T(8,128)(2,1)S(1)} %get-tuple-element.129), channel_id=1, source_target_pairs={{0,16},{2,18},{4,20},{6,22},{8,24},{10,26},{12,28},{14,30},{16,0},... | collective-permute-start | bytes 393224 | tf_op jit(solution)/shard_map/ppermute | solution.py:655
  88.8 1.8 %collective-permute-start.19 = (bf16[40,1024]{1,0:T(8,128)(2,1)S(1)}, bf16[40,1024]{1,0:T(8,128)(2,1)S(1)}, u32[]{:S(2)}, u32[]{:S(2)}) collective-permute-start(bf16[40,1024]{1,0:T(8,128)(2,1)S(1)} %get-tuple-element.109), channel_id=1, source_target_pairs={{0,16},{2,18},{4,20},{6,22},{8,24},{10,26},{12,28},{14,30},{16,0},... | collective-permute-start | bytes 245768 | tf_op jit(solution)/shard_map/ppermute | solution.py:655
  90.6 2.0 %collective-permute-start.20 = (bf16[40,1024]{1,0:T(8,128)(2,1)S(1)}, bf16[40,1024]{1,0:T(8,128)(2,1)S(1)}, u32[]{:S(2)}, u32[]{:S(2)}) collective-permute-start(bf16[40,1024]{1,0:T(8,128)(2,1)S(1)} %get-tuple-element.110), channel_id=1, source_target_pairs={{0,24},{2,26},{4,28},{6,30},{8,16},{10,18},{12,20},{14,22},{16,8},... | collective-permute-start | bytes 245768 | tf_op jit(solution)/shard_map/ppermute | solution.py:655
  92.6 2.6 %shard_map.275 = bf16[196,4,512]{2,1,0:T(4,128)(2,1)} custom-call(s32[3]{0:T(128)S(1)} %pad_add_fusion.sel_ref.me_ref, bf16[2,196,512]{2,1,0:T(8,128)(2,1)S(1)} %get-tuple-element.82.own_ref, bf16[2,196,512]{2,1,0:T(8,128)(2,1)S(1)} %collective-permute-done.7.other_ref), custom_call_target="tpu_custom_call" | custom-call | flops 1000000 | bytes 1605632 | tf_op jit(solution)/shard_map/pallas_call | solution.py:634
  95.1 0.2 copy.40.other_ref
  95.3 2.1 %shard_map.278 = f32[196,4,512]{2,1,0:T(4,128)} custom-call(s32[3]{0:T(128)S(1)} %pad_add_fusion.sel_ref.me_ref, f32[2,196,512]{2,1,0:T(8,128)S(1)} %get-tuple-element.96.own_ref, f32[2,196,512]{2,1,0:T(8,128)S(1)} %copy.40.other_ref), custom_call_target="tpu_custom_call" | custom-call | flops 1000000 | bytes 3211264 | tf_op jit(solution)/shard_map/pallas_call | solution.py:634
  97.4 7.0 %collective-permute-done.19.refs_1_ = bf16[40,1024]{1,0:T(8,128)(2,1)S(1)} collective-permute-done((bf16[40,1024]{1,0:T(8,128)(2,1)S(1)}, bf16[40,1024]{1,0:T(8,128)(2,1)S(1)}, u32[]{:S(2)}, u32[]{:S(2)}) %collective-permute-start.19) | collective-permute-done | bytes 81952 | tf_op jit(solution)/shard_map/ppermute | solution.py:655
  104.3 1.2 %shard_map.282 = (f32[3,32,256]{2,1,0:T(8,128)}, f32[32,256]{1,0:T(8,128)}, f32[1,512]{1,0:T(1,128)}, f32[1,512]{1,0:T(1,128)}, f32[1,512]{1,0:T(1,128)}, /*inde...) custom-call(s32[3]{0:T(128)S(1)} %pad_add_fusion.sel_ref.me_ref, ...), custom_call_target="tpu_custom_call" | custom-call | flops 1000000 | bytes 564512 | tf_op jit(solution)/shard_map/pallas_call | solution.py:634
  105.6 1.3 %shard_map.285 = (f32[32,1024]{1,0:T(8,128)}, f32[32,1024]{1,0:T(8,128)}) custom-call(s32[3]{0:T(128)S(1)} %pad_add_fusion.sel_ref.me_ref, f32[32,2048]{1,0:T(8,128)S(1)} %get-tuple-element.127.own_ref, bf16[32,2048]{1,0:T(8,128)(2,1)S(1)} %collective-permute-done.26.refs_0_, bf16[32,2048]{1,0:T(8,128)(2,1)S(1)} %collective-permute-done.27.refs_1_, ...), custom_call_target="tpu_custom_call" | custom-call | flops 1000000 | bytes 917504 | tf_op jit(solution)/shard_map/pallas_call | solution.py:634
  (60 shorter events, 0.8 us)
Async XLA Ops:
  0.6 8.2 %collective-permute-start = (bf16[3,512,256]{2,1,0:T(8,128)(2,1)}, bf16[3,512,256]{2,1,0:T(8,128)(2,1)S(1)}, u32[]{:S(2)}, u32[]{:S(2)}) collective-permute-start(bf16[3,512,256]{2,1,0:T(8,128)(2,1)} %bitcast.23), channel_id=1, source_target_pairs={{0,1},{1,0},{2,3},{3,2},{4,5},{5,4},{6,7},{7,6},{8,9},{9,8},{10,11... | collective-permute-start | bytes 2359304 | tf_op jit(solution)/shard_map/ppermute | solution.py:796
  1.2 13.8 %collective-permute-start.4 = (bf16[512,1024]{1,0:T(8,128)(2,1)}, bf16[512,1024]{1,0:T(8,128)(2,1)S(1)}, u32[]{:S(2)}, u32[]{:S(2)}) collective-permute-start(bf16[512,1024]{1,0:T(8,128)(2,1)} %w1_ref.1), channel_id=1, source_target_pairs={{0,1},{1,0},{2,3},{3,2},{4,5},{5,4},{6,7},{7,6},{8,9},{9,8},{10,11... | collective-permute-start | bytes 3145736 | tf_op jit(solution)/shard_map/ppermute | solution.py:796
  1.3 13.8 %collective-permute-start.5 = (bf16[512,1024]{1,0:T(8,128)(2,1)}, bf16[512,1024]{1,0:T(8,128)(2,1)S(1)}, u32[]{:S(2)}, u32[]{:S(2)}) collective-permute-start(bf16[512,1024]{1,0:T(8,128)(2,1)} %w2_ref.1), channel_id=1, source_target_pairs={{0,1},{1,0},{2,3},{3,2},{4,5},{5,4},{6,7},{7,6},{8,9},{9,8},{10,11... | collective-permute-start | bytes 3145736 | tf_op jit(solution)/shard_map/ppermute | solution.py:796
  1.7 7.1 %collective-permute-start.3 = (bf16[512,256]{1,0:T(8,128)(2,1)}, bf16[512,256]{1,0:T(8,128)(2,1)S(1)}, u32[]{:S(2)}, u32[]{:S(2)}) collective-permute-start(bf16[512,256]{1,0:T(8,128)(2,1)} %pm_ref.3), channel_id=1, source_target_pairs={{0,1},{1,0},{2,3},{3,2},{4,5},{5,4},{6,7},{7,6},{8,9},{9,8},{10,11... | collective-permute-start | bytes 786440 | tf_op jit(solution)/shard_map/ppermute | solution.py:796
  1.8 4.9 %collective-permute-start.2 = (f32[8,169]{1,0:T(8,128)}, f32[8,169]{1,0:T(8,128)S(1)}, u32[]{:S(2)}, u32[]{:S(2)}) collective-permute-start(f32[8,169]{1,0:T(8,128)} %bitcast.26), channel_id=1, source_target_pairs={{0,1},{1,0},{2,3},{3,2},{4,5},{5,4},{6,7},{7,6},{8,9},{9,8},{10,11... | collective-permute-start | bytes 16232 | tf_op jit(solution)/shard_map/ppermute | solution.py:796
  2.2 1.4 %copy-start.14 = (bf16[4,196,512]{2,0,1:T(4,128)(2,1)S(1)}, bf16[4,196,512]{2,0,1:T(4,128)(2,1)}, u32[]{:S(2)}) copy-start(bf16[4,196,512]{2,0,1:T(4,128)(2,1)} %param.31) | copy-start | bytes 2408452
  2.3 4.4 %copy-start.8 = (f32[2,256]{1,0:T(2,128)S(1)}, f32[2,256]{1,0:T(2,128)}, u32[]{:S(2)}) copy-start(f32[2,256]{1,0:T(2,128)} %qvbm_ref.1) | copy-start | bytes 6148
  2.3 4.8 %copy-start.4 = (f32[169,8]{0,1:T(8,128)S(1)}, f32[169,8]{0,1:T(8,128)}, u32[]{:S(2)}) copy-start(f32[169,8]{0,1:T(8,128)} %param.22) | copy-start | bytes 16228
  3.8 4.8 %copy-start.5 = (f32[1024]{0:T(1024)S(1)}, f32[1024]{0:T(1024)}, u32[]{:S(2)}) copy-start(f32[1024]{0:T(1024)} %param.28) | copy-start | bytes 12292
  3.8 5.0 %copy-start.2 = (bf16[512,3,256]{2,0,1:T(8,128)(2,1)S(1)}, bf16[512,3,256]{2,0,1:T(8,128)(2,1)}, u32[]{:S(2)}) copy-start(bf16[512,3,256]{2,0,1:T(8,128)(2,1)} %param.20) | copy-start | bytes 2359300
  3.8 5.0 %copy-start.3 = (bf16[512,256]{1,0:T(8,128)(2,1)S(1)}, bf16[512,256]{1,0:T(8,128)(2,1)}, u32[]{:S(2)}) copy-start(bf16[512,256]{1,0:T(8,128)(2,1)} %pm_ref.3) | copy-start | bytes 786436
  3.9 5.0 %copy-start.6 = (s32[4,196]{1,0:T(4,128)S(1)}, s32[4,196]{1,0:T(4,128)}, u32[]{:S(2)}) copy-start(s32[4,196]{1,0:T(4,128)} %ids_ref.3) | copy-start | bytes 9412
  3.9 5.0 %copy-start.7 = (f32[512]{0:T(512)S(1)}, f32[512]{0:T(512)}, u32[]{:S(2)}) copy-start(f32[512]{0:T(512)} %param.19) | copy-start | bytes 6148
  3.9 5.0 %copy-start.9 = (f32[512]{0:T(512)S(1)}, f32[512]{0:T(512)}, u32[]{:S(2)}) copy-start(f32[512]{0:T(512)} %param.24) | copy-start | bytes 6148
  3.9 5.0 %copy-start.13 = (f32[512]{0:T(512)S(1)}, f32[512]{0:T(512)}, u32[]{:S(2)}) copy-start(f32[512]{0:T(512)} %param.18) | copy-start | bytes 6148
  6.7 1.9 %collective-permute-start.1 = (f32[2,256]{1,0:T(2,128)S(1)}, f32[2,256]{1,0:T(2,128)S(1)}, u32[]{:S(2)}, u32[]{:S(2)}) collective-permute-start(f32[2,256]{1,0:T(2,128)S(1)} %copy-done.8), channel_id=1, source_target_pairs={{0,1},{1,0},{2,3},{3,2},{4,5},{5,4},{6,7},{7,6},{8,9},{9,8},{10,11... | collective-permute-start | bytes 6152 | tf_op jit(solution)/shard_map/ppermute | solution.py:796
  8.7 6.4 %collective-permute-start.6 = (f32[1,1024]{1,0:T(1,128)S(1)}, f32[1,1024]{1,0:T(1,128)S(1)}, u32[]{:S(2)}, u32[]{:S(2)}) collective-permute-start(f32[1,1024]{1,0:T(1,128)S(1)} %bitcast.28), channel_id=1, source_target_pairs={{0,1},{1,0},{2,3},{3,2},{4,5},{5,4},{6,7},{7,6},{8,9},{9,8},{10,11... | collective-permute-start | bytes 12296 | tf_op jit(solution)/shard_map/ppermute | solution.py:796
  8.9 6.2 %copy-start.10 = (f32[512]{0:T(512)S(1)}, f32[512]{0:T(512)}, u32[]{:S(2)}) copy-start(f32[512]{0:T(512)} %param.25) | copy-start | bytes 6148
  8.9 6.2 %copy-start.11 = (f32[512]{0:T(512)S(1)}, f32[512]{0:T(512)}, u32[]{:S(2)}) copy-start(f32[512]{0:T(512)} %param.26) | copy-start | bytes 6148
  15.1 5.5 %copy-start = (bf16[512,1024]{1,0:T(8,128)(2,1)S(1)}, bf16[512,1024]{1,0:T(8,128)(2,1)}, u32[]{:S(2)}) copy-start(bf16[512,1024]{1,0:T(8,128)(2,1)} %w1_ref.1) | copy-start | bytes 3145732
  15.1 5.5 %copy-start.1 = (bf16[512,1024]{1,0:T(8,128)(2,1)S(1)}, bf16[512,1024]{1,0:T(8,128)(2,1)}, u32[]{:S(2)}) copy-start(bf16[512,1024]{1,0:T(8,128)(2,1)} %w2_ref.1) | copy-start | bytes 3145732
  15.1 5.5 %copy-start.12 = (f32[512]{0:T(512)S(1)}, f32[512]{0:T(512)}, u32[]{:S(2)}) copy-start(f32[512]{0:T(512)} %param.30) | copy-start | bytes 6148
  20.0 27.8 %collective-permute-start.21 = (bf16[512,1024]{1,0:T(8,128)(2,1)S(1)}, bf16[512,1024]{1,0:T(8,128)(2,1)S(1)}, u32[]{:S(2)}, u32[]{:S(2)}) collective-permute-start(bf16[512,1024]{1,0:T(8,128)(2,1)S(1)} %get-tuple-element.121), channel_id=1, source_target_pairs={{0,1},{1,0},{2,3},{3,2},{4,5},{5,4},{6,7},{7,6},{8,9},{9,8},{10,11... | collective-permute-start | bytes 3145736 | tf_op jit(solution)/shard_map/ppermute | solution.py:796
  20.5 28.8 %collective-permute-start.22 = (bf16[512,1024]{1,0:T(8,128)(2,1)S(1)}, bf16[512,1024]{1,0:T(8,128)(2,1)S(1)}, u32[]{:S(2)}, u32[]{:S(2)}) collective-permute-start(bf16[512,1024]{1,0:T(8,128)(2,1)S(1)} %get-tuple-element.123), channel_id=1, source_target_pairs={{0,1},{1,0},{2,3},{3,2},{4,5},{5,4},{6,7},{7,6},{8,9},{9,8},{10,11... | collective-permute-start | bytes 3145736 | tf_op jit(solution)/shard_map/ppermute | solution.py:796
  33.0 9.9 %collective-permute-start.9 = (bf16[512,512]{1,0:T(8,128)(2,1)S(1)}, bf16[512,512]{1,0:T(8,128)(2,1)S(1)}, u32[]{:S(2)}, u32[]{:S(2)}) collective-permute-start(bf16[512,512]{1,0:T(8,128)(2,1)S(1)} %get-tuple-element.98), channel_id=1, source_target_pairs={{0,1},{1,0},{2,3},{3,2},{4,5},{5,4},{6,7},{7,6},{8,9},{9,8},{10,11... | collective-permute-start | bytes 1572872 | tf_op jit(solution)/shard_map/ppermute | solution.py:796
  33.5 10.0 %collective-permute-start.10 = (bf16[512,512]{1,0:T(8,128)(2,1)S(1)}, bf16[512,512]{1,0:T(8,128)(2,1)S(1)}, u32[]{:S(2)}, u32[]{:S(2)}) collective-permute-start(bf16[512,512]{1,0:T(8,128)(2,1)S(1)} %get-tuple-element.100), channel_id=1, source_target_pairs={{0,1},{1,0},{2,3},{3,2},{4,5},{5,4},{6,7},{7,6},{8,9},{9,8},{10,11... | collective-permute-start | bytes 1572872 | tf_op jit(solution)/shard_map/ppermute | solution.py:796
  37.3 1.3 %collective-permute-start.14 = (f32[16,512]{1,0:T(8,128)S(1)}, f32[16,512]{1,0:T(8,128)S(1)}, u32[]{:S(2)}, u32[]{:S(2)}) collective-permute-start(f32[16,512]{1,0:T(8,128)S(1)} %get-tuple-element.105), channel_id=1, source_target_pairs={{0,1},{1,0},{2,3},{3,2},{4,5},{5,4},{6,7},{7,6},{8,9},{9,8},{10,11... | collective-permute-start | bytes 98312 | tf_op jit(solution)/shard_map/ppermute | solution.py:796
  39.1 5.7 %collective-permute-start.17 = (f32[16,512]{1,0:T(8,128)S(1)}, f32[16,512]{1,0:T(8,128)S(1)}, u32[]{:S(2)}, u32[]{:S(2)}) collective-permute-start(f32[16,512]{1,0:T(8,128)S(1)} %shard_map.280.refs_7_), channel_id=1, source_target_pairs={{0,6},{2,4},{4,2},{6,0},{8,14},{10,12},{12,10},{14,8},{16,22},{18,... | collective-permute-start | bytes 98312 | tf_op jit(solution)/shard_map/ppermute | solution.py:655
  43.0 4.7 %collective-permute-start.16 = (f32[16,512]{1,0:T(8,128)S(1)}, f32[16,512]{1,0:T(8,128)S(1)}, u32[]{:S(2)}, u32[]{:S(2)}) collective-permute-start(f32[16,512]{1,0:T(8,128)S(1)} %shard_map.280.refs_7_), channel_id=1, source_target_pairs={{0,4},{2,6},{4,0},{6,2},{8,12},{10,14},{12,8},{14,10},{16,20},{18,... | collective-permute-start | bytes 98312 | tf_op jit(solution)/shard_map/ppermute | solution.py:655
  44.2 14.7 %collective-permute-start.11 = (bf16[128,1024]{1,0:T(8,128)(2,1)S(1)}, bf16[128,1024]{1,0:T(8,128)(2,1)S(1)}, u32[]{:S(2)}, u32[]{:S(2)}) collective-permute-start(bf16[128,1024]{1,0:T(8,128)(2,1)S(1)} %get-tuple-element.101), channel_id=1, source_target_pairs={{0,2},{2,0},{4,6},{6,4},{8,10},{10,8},{12,14},{14,12},{16,18},{18,... | collective-permute-start | bytes 786440 | tf_op jit(solution)/shard_map/ppermute | solution.py:655
  44.9 15.7 %collective-permute-start.12 = (bf16[128,1024]{1,0:T(8,128)(2,1)S(1)}, bf16[128,1024]{1,0:T(8,128)(2,1)S(1)}, u32[]{:S(2)}, u32[]{:S(2)}) collective-permute-start(bf16[128,1024]{1,0:T(8,128)(2,1)S(1)} %get-tuple-element.102), channel_id=1, source_target_pairs={{0,4},{2,6},{4,0},{6,2},{8,12},{10,14},{12,8},{14,10},{16,20},{18,... | collective-permute-start | bytes 786440 | tf_op jit(solution)/shard_map/ppermute | solution.py:655
  47.7 41.1 %collective-permute-start.8 = (f32[2,196,512]{2,0,1:T(2,128)S(1)}, f32[2,196,512]{2,0,1:T(2,128)S(1)}, u32[]{:S(2)}, u32[]{:S(2)}) collective-permute-start(f32[2,196,512]{2,0,1:T(2,128)S(1)} %copy.39), channel_id=1, source_target_pairs={{0,1},{1,0},{2,3},{3,2},{4,5},{5,4},{6,7},{7,6},{8,9},{9,8},{10,11... | collective-permute-start | bytes 2408456 | tf_op jit(solution)/shard_map/ppermute | solution.py:796
  47.8 14.2 %collective-permute-start.13 = (bf16[128,1024]{1,0:T(8,128)(2,1)S(1)}, bf16[128,1024]{1,0:T(8,128)(2,1)S(1)}, u32[]{:S(2)}, u32[]{:S(2)}) collective-permute-start(bf16[128,1024]{1,0:T(8,128)(2,1)S(1)} %get-tuple-element.103), channel_id=1, source_target_pairs={{0,6},{2,4},{4,2},{6,0},{8,14},{10,12},{12,10},{14,8},{16,22},{18,... | collective-permute-start | bytes 786440 | tf_op jit(solution)/shard_map/ppermute | solution.py:655
  49.3 9.2 %collective-permute-start.15 = (f32[16,512]{1,0:T(8,128)S(1)}, f32[16,512]{1,0:T(8,128)S(1)}, u32[]{:S(2)}, u32[]{:S(2)}) collective-permute-start(f32[16,512]{1,0:T(8,128)S(1)} %shard_map.280.refs_7_), channel_id=1, source_target_pairs={{0,2},{2,0},{4,6},{6,4},{8,10},{10,8},{12,14},{14,12},{16,18},{18,... | collective-permute-start | bytes 98312 | tf_op jit(solution)/shard_map/ppermute | solution.py:655
  58.5 14.8 %collective-permute-start.23 = (bf16[128,2048]{1,0:T(8,128)(2,1)S(1)}, bf16[128,2048]{1,0:T(8,128)(2,1)S(1)}, u32[]{:S(2)}, u32[]{:S(2)}) collective-permute-start(bf16[128,2048]{1,0:T(8,128)(2,1)S(1)} %get-tuple-element.124), channel_id=1, source_target_pairs={{0,2},{2,0},{4,6},{6,4},{8,10},{10,8},{12,14},{14,12},{16,18},{18,... | collective-permute-start | bytes 1572872 | tf_op jit(solution)/shard_map/ppermute | solution.py:655
  58.9 24.5 %collective-permute-start.24 = (bf16[128,2048]{1,0:T(8,128)(2,1)S(1)}, bf16[128,2048]{1,0:T(8,128)(2,1)S(1)}, u32[]{:S(2)}, u32[]{:S(2)}) collective-permute-start(bf16[128,2048]{1,0:T(8,128)(2,1)S(1)} %get-tuple-element.125), channel_id=1, source_target_pairs={{0,4},{2,6},{4,0},{6,2},{8,12},{10,14},{12,8},{14,10},{16,20},{18,... | collective-permute-start | bytes 1572872 | tf_op jit(solution)/shard_map/ppermute | solution.py:655
  60.5 22.9 %collective-permute-start.25 = (bf16[128,2048]{1,0:T(8,128)(2,1)S(1)}, bf16[128,2048]{1,0:T(8,128)(2,1)S(1)}, u32[]{:S(2)}, u32[]{:S(2)}) collective-permute-start(bf16[128,2048]{1,0:T(8,128)(2,1)S(1)} %get-tuple-element.126), channel_id=1, source_target_pairs={{0,6},{2,4},{4,2},{6,0},{8,14},{10,12},{12,10},{14,8},{16,22},{18,... | collective-permute-start | bytes 1572872 | tf_op jit(solution)/shard_map/ppermute | solution.py:655
  62.0 26.7 %collective-permute-start.7 = (bf16[2,196,512]{2,1,0:T(8,128)(2,1)S(1)}, bf16[2,196,512]{2,1,0:T(8,128)(2,1)S(1)}, u32[]{:S(2)}, u32[]{:S(2)}) collective-permute-start(bf16[2,196,512]{2,1,0:T(8,128)(2,1)S(1)} %get-tuple-element.82.own_ref), channel_id=1, source_target_pairs={{0,1},{1,0},{2,3},{3,2},{4,5},{5,4},{6,7},{7,6},{8,9},{9,8},{10,11... | collective-permute-start | bytes 1204232 | tf_op jit(solution)/shard_map/ppermute | solution.py:796
  73.3 17.3 %collective-permute-start.18 = (bf16[40,1024]{1,0:T(8,128)(2,1)S(1)}, bf16[40,1024]{1,0:T(8,128)(2,1)S(1)}, u32[]{:S(2)}, u32[]{:S(2)}) collective-permute-start(bf16[40,1024]{1,0:T(8,128)(2,1)S(1)} %get-tuple-element.108), channel_id=1, source_target_pairs={{0,8},{2,10},{4,12},{6,14},{8,0},{10,2},{12,4},{14,6},{16,24},{18,... | collective-permute-start | bytes 245768 | tf_op jit(solution)/shard_map/ppermute | solution.py:655
  84.3 21.2 %collective-permute-start.26 = (bf16[32,2048]{1,0:T(8,128)(2,1)S(1)}, bf16[32,2048]{1,0:T(8,128)(2,1)S(1)}, u32[]{:S(2)}, u32[]{:S(2)}) collective-permute-start(bf16[32,2048]{1,0:T(8,128)(2,1)S(1)} %get-tuple-element.128), channel_id=1, source_target_pairs={{0,8},{2,10},{4,12},{6,14},{8,0},{10,2},{12,4},{14,6},{16,24},{18,... | collective-permute-start | bytes 393224 | tf_op jit(solution)/shard_map/ppermute | solution.py:655
  86.1 19.5 %collective-permute-start.27 = (bf16[32,2048]{1,0:T(8,128)(2,1)S(1)}, bf16[32,2048]{1,0:T(8,128)(2,1)S(1)}, u32[]{:S(2)}, u32[]{:S(2)}) collective-permute-start(bf16[32,2048]{1,0:T(8,128)(2,1)S(1)} %get-tuple-element.129), channel_id=1, source_target_pairs={{0,16},{2,18},{4,20},{6,22},{8,24},{10,26},{12,28},{14,30},{16,0},... | collective-permute-start | bytes 393224 | tf_op jit(solution)/shard_map/ppermute | solution.py:655
  88.7 16.9 %collective-permute-start.28 = (bf16[32,2048]{1,0:T(8,128)(2,1)S(1)}, bf16[32,2048]{1,0:T(8,128)(2,1)S(1)}, u32[]{:S(2)}, u32[]{:S(2)}) collective-permute-start(bf16[32,2048]{1,0:T(8,128)(2,1)S(1)} %get-tuple-element.130), channel_id=1, source_target_pairs={{0,24},{2,26},{4,28},{6,30},{8,16},{10,18},{12,20},{14,22},{16,8},... | collective-permute-start | bytes 393224 | tf_op jit(solution)/shard_map/ppermute | solution.py:655
  88.8 15.5 %collective-permute-start.19 = (bf16[40,1024]{1,0:T(8,128)(2,1)S(1)}, bf16[40,1024]{1,0:T(8,128)(2,1)S(1)}, u32[]{:S(2)}, u32[]{:S(2)}) collective-permute-start(bf16[40,1024]{1,0:T(8,128)(2,1)S(1)} %get-tuple-element.109), channel_id=1, source_target_pairs={{0,16},{2,18},{4,20},{6,22},{8,24},{10,26},{12,28},{14,30},{16,0},... | collective-permute-start | bytes 245768 | tf_op jit(solution)/shard_map/ppermute | solution.py:655
  90.6 13.7 %collective-permute-start.20 = (bf16[40,1024]{1,0:T(8,128)(2,1)S(1)}, bf16[40,1024]{1,0:T(8,128)(2,1)S(1)}, u32[]{:S(2)}, u32[]{:S(2)}) collective-permute-start(bf16[40,1024]{1,0:T(8,128)(2,1)S(1)} %get-tuple-element.110), channel_id=1, source_target_pairs={{0,24},{2,26},{4,28},{6,30},{8,16},{10,18},{12,20},{14,22},{16,8},... | collective-permute-start | bytes 245768 | tf_op jit(solution)/shard_map/ppermute | solution.py:655

commit v4 on v3

--- a/solution.py
+++ b/solution.py
@@ -288,9 +288,8 @@
     *refs,
 ):
     if last:
-        b2_ref, ln_ref, lnt_ref, cot_b_ref, cot_t_ref, ffn_in, gln_in = refs[:7]
-        g1_ref, g2_ref, gb_ref, half_ref, gres_ref, sums_ref = refs[7:13]
-        ffn_ref, gln_ref = refs[13:]
+        ln_ref, lnt_ref, cot_b_ref, cot_t_ref, ffn_in, gln_in = refs[:6]
+        g1_ref, g2_ref, gb_ref, ffn_ref, gln_ref = refs[6:]
     else:
         g1_ref, g2_ref, gb_ref = refs[:3]
         ln_ref, lnt_ref, cot_b_ref, cot_t_ref, ffn_ref, gln_ref = refs[3:]
@@ -307,7 +306,7 @@
         cot_t_ref[...] = nt(order, cot_b_ref[...]).astype(BF16)
         ffn_ref[...] = jnp.zeros(ffn_ref.shape, F32)
         gln_ref[...] = jnp.zeros(gln_ref.shape, F32)
-    chunk = 256
+    chunk = 512
 
     def one_chunk(at, carry):
         cols = pl.ds(pl.multiple_of(at * chunk, chunk), chunk)
@@ -325,8 +324,11 @@
         return carry
 
     lax.fori_loop(0, w1_ref.shape[1] // chunk, one_chunk, 0, unroll=True)
-    if not last:
-        return
+
+
+def second_norm_back(
+    images, resid_ref, ffn_ref, gln_ref, cot_b_ref, gain_ref, b2_ref, half_ref, gres_ref, sums_ref
+):
     resid = resid_ref[...]
     result = (resid + ffn_ref[...] + b2_ref[...]).astype(BF16)
     for image in range(images):
@@ -348,7 +350,12 @@
     heads,
     layout,
     me_ref,
-    gres_ref,
+    resid_ref,
+    ffn_ref,
+    gln_ref,
+    cot_b_ref,
+    gain_two_ref,
+    b2_ref,
     ids_ref,
     merged_ref,
     pm_ref,
@@ -366,6 +373,9 @@
     gqkv_ref,
     sums_ref,
     gbias_ref,
+    half_ref,
+    gres_ref,
+    two_ref,
     pick_ref,
     gatt_ref,
     mask_ref,
@@ -378,8 +388,19 @@
     slots = WINS * WPAD
     pick_ref[...] = gather_matrix()
     mask_ref[...] = head_mask(heads)
-    gres = gres_ref[...]
-    gres_b = gres.astype(BF16)
+    second_norm_back(
+        images,
+        resid_ref,
+        ffn_ref,
+        gln_ref,
+        cot_b_ref,
+        gain_two_ref,
+        b2_ref,
+        half_ref,
+        gres_ref,
+        two_ref,
+    )
+    gres_b = gres_ref[...].astype(BF16)
     put_rows(gvpm_ref, layout, chan, tn(gres_b, merged_ref[:, :chan]))
     put_rows(gvpo_ref, layout, chan, tn(gres_b, merged_ref[:, chan:]))
     grad_m = jnp.concatenate(
@@ -883,23 +904,16 @@
     )
     got1 = swap(g1o)
     got2 = swap(g2o)
-    ins = common + (w_fc1, w_fc2, row(b_fc1), row(b_fc2), *carried)
+    ins = common + (w_fc1, w_fc2, row(b_fc1), *carried)
     outs = (
         weight_grad,
         weight_grad,
         struct((1, hidden), F32),
-        struct((images, TOK, width), BF16),
         acc,
-        struct((8, width), F32),
-    )
-    g1m, g2m, gbm, out_half, gres, sums_two = call(
-        functools.partial(ffn_kernel, images, layout, True),
-        me_arr,
-        ins,
-        outs,
-        [pltpu.VMEM((rows_t, width), F32), pltpu.VMEM((rows_t, width), F32)],
-        3 * 10**9,
-        LIMIT,
+        acc,
+    )
+    g1m, g2m, gbm, ffn_acc, gln_acc = call(
+        functools.partial(ffn_kernel, images, layout, True), me_arr, ins, outs, [], 3 * 10**9, LIMIT
     )
 
     share = width // n_dp
@@ -917,9 +931,8 @@
     else:
         sent_fc1 = scatter_sum((g1m, got1), "dp", n_dp, digits)
         sent_fc2 = scatter_sum((g2m, got2), "dp", n_dp, digits)
-    output = join(out_half)
-
-    ins = (gres, region_ids, merged, w_proj, po, q, k, v, win_in, lse, bias)
+    before = (resid, ffn_acc, gln_acc, carried[2], row(norm2_gain), row(b_fc2))
+    ins = before + (region_ids, merged, w_proj, po, q, k, v, win_in, lse, bias)
     outs = (
         struct((width, 2 * chan), BF16),
         struct((width, 2 * chan), BF16),
@@ -928,8 +941,11 @@
         struct((rows_w, 6 * chan), BF16),
         struct((8, 2 * chan), F32),
         bias_shape,
-    )
-    gqkm, gqko, gvpm, gvpo, gqkv, sums_qv, gbias = call(
+        struct((images, TOK, width), BF16),
+        acc,
+        struct((8, width), F32),
+    )
+    gqkm, gqko, gvpm, gvpo, gqkv, sums_qv, gbias, out_half, gres, sums_two = call(
         functools.partial(attend_back_kernel, images, heads, layout),
         me_arr,
         ins,
@@ -963,6 +979,7 @@
         2 * 10**9,
         LIMIT,
     )
+    output = join(out_half)
     grad_in = join(grad_half)
 
     got = swap(theirs)

time: 107 us -> 107 us (level)
  starting transfers between devices: 25.2 us -> 26.3 us
  waiting for transfers between devices: 38.4 us -> 37.3 us
    ppermute x15, waiting for transfers between devices: 34.7 us -> 33.6 us  [xor_exchange(): return lax.ppermute(value, axis, [(i, i ^ mask) for i in range(count)])]
  transfers between devices with their start and end apart: 29 -> 29, of which waited for: 7 -> 6; matrix products, arithmetic and copies ran while one was open for 2% -> 2% of each run, Pallas kernels for 31% -> 31%
where the time goes in v4:
time: 107 us
  Pallas kernels  39.4 us (37%)
  waiting for transfers between devices  37.3 us (35%)
  starting transfers between devices  26.3 us (25%)
  local copies, waits for them, and re-layouts  2.57 us (2%)
    pallas_call x15, Pallas kernels, call(): pl.pallas_call(kernel, in_specs=[pl.BlockSpec(memory_space=pltpu.SMEM)] +...  39.4 us
    ppermute x15, waiting for transfers between devices, xor_exchange(): return lax.ppermute(value, axis, [(i, i ^ mask) for i in range(count)])  33.6 us
    ppermute x15, starting transfers between devices, xor_exchange(): return lax.ppermute(value, axis, [(i, i ^ mask) for i in range(count)])  22.5 us
    ppermute x14, starting transfers between devices, swap(): return lax.ppermute(value, 'tensor', [(i, i ^ 1) for i in range(n_tensor)])  3.77 us
    ppermute x14, waiting for transfers between devices, swap(): return lax.ppermute(value, 'tensor', [(i, i ^ 1) for i in range(n_tensor)])  3.7 us
  transfers between devices with their start and end apart: 29, of which 6 were waited for; matrix products, arithmetic and copies ran while one was open for 2% of the time, Pallas kernels for 31%

profile of v4, /device:TPU:0, one launch (start us, length us, event | category | flops | bytes accessed | tf_op | source)
XLA Modules:
  0.0 106.6 jit_solution(3311708728767487650)
XLA Ops:
  0.6 0.6 collective-permute-start
  1.3 0.4 collective-permute-start.5
  1.8 0.4 collective-permute-start.2
  2.3 1.3 %copy.35.tok_ref = bf16[4,196,512]{2,1,0:T(8,128)(2,1)S(1)} copy(bf16[4,196,512]{2,0,1:T(4,128)(2,1)} %param.16) | data formatting | bytes 1605632 | tf_op args[0]
  3.7 0.1 copy.37.cot_ref
  3.9 2.8 %collective-permute-done.2.other_ref = f32[8,169]{1,0:T(8,128)S(1)} collective-permute-done((f32[8,169]{1,0:T(8,128)}, f32[8,169]{1,0:T(8,128)S(1)}, u32[]{:S(2)}, u32[]{:S(2)}) %collective-permute-start.2) | collective-permute-done | bytes 5440 | tf_op jit(solution)/shard_map/ppermute | solution.py:817
  6.7 0.4 collective-permute-start.1
  7.1 1.5 %shard_map.271.bias_ref = f32[512,128]{1,0:T(8,128)S(1)} custom-call(s32[3]{0:T(128)S(1)} %pad_add_fusion.sel_ref.me_ref, f32[8,169]{1,0:T(8,128)S(1)} %bitcast.27, f32[8,169]{1,0:T(8,128)S(1)} %collective-permute-done.2.other_ref), custom_call_target="tpu_custom_call" | custom-call | flops 1000000000 | bytes 272960 | tf_op jit(solution)/shard_map/pallas_call | solution.py:655
  8.7 0.2 collective-permute-start.6
  8.9 6.1 %shard_map.272 = (bf16[512,512]{1,0:T(8,128)(2,1)S(1)}, bf16[512,512]{1,0:T(8,128)(2,1)S(1)}, bf16[512,512]{1,0:T(8,128)(2,1)S(1)}, bf16[512,512]{1,0:T(8,128)(2...) custom-call(s32[3]{0:T(128)S(1)} %pad_add_fusion.sel_ref.me_ref, ...), custom_call_target="tpu_custom_call" | custom-call | flops 3000000000 | bytes 6583360 | tf_op jit(solution)/shard_map/pallas_call | solution.py:655
  15.1 4.8 %shard_map.273 = (bf16[512,1024]{1,0:T(8,128)(2,1)S(1)}, bf16[512,1024]{1,0:T(8,128)(2,1)S(1)}, f32[1,1024]{1,0:T(1,128)S(1)}, bf16[416,512]{1,0:T(8,128)(2,1)S(...) custom-call(s32[3]{0:T(128)S(1)} %pad_add_fusion.sel_ref.me_ref, ...), custom_call_target="tpu_custom_call" | custom-call | flops 3000000000 | bytes 9269248 | tf_op jit(solution)/shard_map/pallas_call | solution.py:655
  19.9 0.5 collective-permute-start.21
  20.5 4.1 %shard_map.274 = (bf16[512,1024]{1,0:T(8,128)(2,1)S(1)}, bf16[512,1024]{1,0:T(8,128)(2,1)S(1)}, f32[1,1024]{1,0:T(1,128)S(1)}, f32[416,512]{1,0:T(8,128)S(1)}, f32[416,512]{1,0:T(8,128)S(1)}) custom-call(s32[3]{0:T(128)S(1)} %pad_add_fusion.sel_ref.me_ref, f32[416,512]{1,0:T(8,128)S(1)} %get-tuple-element.77.resid_ref, ...), custom_call_target="tpu_custom_call" | custom-call | flops 3000000000 | bytes 10973184 | tf_op jit(solution)/shard_map/pallas_call | solution.py:655
  24.6 8.3 %shard_map.275 = (bf16[512,512]{1,0:T(8,128)(2,1)S(1)}, bf16[512,512]{1,0:T(8,128)(2,1)S(1)}, bf16[512,512]{1,0:T(8,128)(2,1)S(1)}, bf16[512,512]{1,0:T(8,128)(2...) custom-call(s32[3]{0:T(128)S(1)} %pad_add_fusion.sel_ref.me_ref, ...), custom_call_target="tpu_custom_call" | custom-call | flops 5000000000 | bytes 11549760 | tf_op jit(solution)/shard_map/pallas_call | solution.py:655
  32.9 0.5 collective-permute-start.10
  33.3 0.1 collective-permute-start.9
  33.4 3.7 %shard_map.277 = (f32[2,196,512]{2,1,0:T(8,128)S(1)}, f32[16,512]{1,0:T(8,128)S(1)}, f32[16,512]{1,0:T(8,128)S(1)}) custom-call(s32[3]{0:T(128)S(1)} %pad_add_fusion.sel_ref.me_ref, bf16[4,196,512]{2,1,0:T(8,128)(2,1)S(1)} %copy.35.tok_ref, f32[416,512]{1,0:T(8,128)S(1)} %get-tuple-element.93.gres_ref, bf16[512,1536]{1,0:T(8,128)(2,1)S(1)} %get-tuple-element.94.gqkv_ref, ...), custom_call_target="tpu_custom_call" | custom-call | flops 2000000000 | bytes 5974016 | tf_op jit(solution)/shard_map/pallas_call | solution.py:655
  37.1 0.4 collective-permute-start.14
  37.5 0.9 collective-permute-done.14.b_ref
  38.4 0.5 shard_map.280.refs_7_
  38.9 2.9 %collective-permute-start.15 = (f32[16,512]{1,0:T(8,128)S(1)}, f32[16,512]{1,0:T(8,128)S(1)}, u32[]{:S(2)}, u32[]{:S(2)}) collective-permute-start(f32[16,512]{1,0:T(8,128)S(1)} %shard_map.280.refs_7_), channel_id=1, source_target_pairs={{0,2},{2,0},{4,6},{6,4},{8,10},{10,8},{12,14},{14,12},{16,18},{18,... | collective-permute-start | bytes 98312 | tf_op jit(solution)/shard_map/ppermute | solution.py:676
  41.8 1.5 %collective-permute-start.16 = (f32[16,512]{1,0:T(8,128)S(1)}, f32[16,512]{1,0:T(8,128)S(1)}, u32[]{:S(2)}, u32[]{:S(2)}) collective-permute-start(f32[16,512]{1,0:T(8,128)S(1)} %shard_map.280.refs_7_), channel_id=1, source_target_pairs={{0,4},{2,6},{4,0},{6,2},{8,12},{10,14},{12,8},{14,10},{16,20},{18,... | collective-permute-start | bytes 98312 | tf_op jit(solution)/shard_map/ppermute | solution.py:676
  43.4 0.7 shard_map.279
  44.1 0.6 collective-permute-start.11
  44.7 1.1 %collective-permute-start.12 = (bf16[128,1024]{1,0:T(8,128)(2,1)S(1)}, bf16[128,1024]{1,0:T(8,128)(2,1)S(1)}, u32[]{:S(2)}, u32[]{:S(2)}) collective-permute-start(bf16[128,1024]{1,0:T(8,128)(2,1)S(1)} %get-tuple-element.106), channel_id=1, source_target_pairs={{0,4},{2,6},{4,0},{6,2},{8,12},{10,14},{12,8},{14,10},{16,20},{18,... | collective-permute-start | bytes 786440 | tf_op jit(solution)/shard_map/ppermute | solution.py:676
  45.8 0.8 copy.39
  46.7 1.9 %collective-permute-start.13 = (bf16[128,1024]{1,0:T(8,128)(2,1)S(1)}, bf16[128,1024]{1,0:T(8,128)(2,1)S(1)}, u32[]{:S(2)}, u32[]{:S(2)}) collective-permute-start(bf16[128,1024]{1,0:T(8,128)(2,1)S(1)} %get-tuple-element.107), channel_id=1, source_target_pairs={{0,6},{2,4},{4,2},{6,0},{8,14},{10,12},{12,10},{14,8},{16,22},{18,... | collective-permute-start | bytes 786440 | tf_op jit(solution)/shard_map/ppermute | solution.py:676
  48.7 1.1 collective-permute-start.17
  49.7 0.9 shard_map.283
  50.6 7.7 %collective-permute-done.17.refs_10_ = f32[16,512]{1,0:T(8,128)S(1)} collective-permute-done((f32[16,512]{1,0:T(8,128)S(1)}, f32[16,512]{1,0:T(8,128)S(1)}, u32[]{:S(2)}, u32[]{:S(2)}) %collective-permute-start.17) | collective-permute-done | bytes 32800 | tf_op jit(solution)/shard_map/ppermute | solution.py:676
  58.3 0.4 collective-permute-start.23
  58.7 1.7 %collective-permute-start.24 = (bf16[128,2048]{1,0:T(8,128)(2,1)S(1)}, bf16[128,2048]{1,0:T(8,128)(2,1)S(1)}, u32[]{:S(2)}, u32[]{:S(2)}) collective-permute-start(bf16[128,2048]{1,0:T(8,128)(2,1)S(1)} %get-tuple-element.129), channel_id=1, source_target_pairs={{0,4},{2,6},{4,0},{6,2},{8,12},{10,14},{12,8},{14,10},{16,20},{18,... | collective-permute-start | bytes 1572872 | tf_op jit(solution)/shard_map/ppermute | solution.py:676
  60.4 1.4 %collective-permute-start.25 = (bf16[128,2048]{1,0:T(8,128)(2,1)S(1)}, bf16[128,2048]{1,0:T(8,128)(2,1)S(1)}, u32[]{:S(2)}, u32[]{:S(2)}) collective-permute-start(bf16[128,2048]{1,0:T(8,128)(2,1)S(1)} %get-tuple-element.130), channel_id=1, source_target_pairs={{0,6},{2,4},{4,2},{6,0},{8,14},{10,12},{12,10},{14,8},{16,22},{18,... | collective-permute-start | bytes 1572872 | tf_op jit(solution)/shard_map/ppermute | solution.py:676
  61.8 0.7 shard_map.281
  62.6 10.6 %collective-permute-done.23.refs_4_ = bf16[128,2048]{1,0:T(8,128)(2,1)S(1)} collective-permute-done((bf16[128,2048]{1,0:T(8,128)(2,1)S(1)}, bf16[128,2048]{1,0:T(8,128)(2,1)S(1)}, u32[]{:S(2)}, u32[]{:S(2)}) %collective-permute-start.23) | collective-permute-done | bytes 524320 | tf_op jit(solution)/shard_map/ppermute | solution.py:676
  73.1 1.6 %collective-permute-start.18 = (bf16[40,1024]{1,0:T(8,128)(2,1)S(1)}, bf16[40,1024]{1,0:T(8,128)(2,1)S(1)}, u32[]{:S(2)}, u32[]{:S(2)}) collective-permute-start(bf16[40,1024]{1,0:T(8,128)(2,1)S(1)} %get-tuple-element.112), channel_id=1, source_target_pairs={{0,8},{2,10},{4,12},{6,14},{8,0},{10,2},{12,4},{14,6},{16,24},{18,... | collective-permute-start | bytes 245768 | tf_op jit(solution)/shard_map/ppermute | solution.py:676
  74.7 8.4 %collective-permute-done.24.refs_5_ = bf16[128,2048]{1,0:T(8,128)(2,1)S(1)} collective-permute-done((bf16[128,2048]{1,0:T(8,128)(2,1)S(1)}, bf16[128,2048]{1,0:T(8,128)(2,1)S(1)}, u32[]{:S(2)}, u32[]{:S(2)}) %collective-permute-start.24) | collective-permute-done | bytes 524320 | tf_op jit(solution)/shard_map/ppermute | solution.py:676
  83.1 0.9 shard_map.284
  84.0 1.9 %collective-permute-start.26 = (bf16[32,2048]{1,0:T(8,128)(2,1)S(1)}, bf16[32,2048]{1,0:T(8,128)(2,1)S(1)}, u32[]{:S(2)}, u32[]{:S(2)}) collective-permute-start(bf16[32,2048]{1,0:T(8,128)(2,1)S(1)} %get-tuple-element.132), channel_id=1, source_target_pairs={{0,8},{2,10},{4,12},{6,14},{8,0},{10,2},{12,4},{14,6},{16,24},{18,... | collective-permute-start | bytes 393224 | tf_op jit(solution)/shard_map/ppermute | solution.py:676
  85.9 2.6 %collective-permute-start.27 = (bf16[32,2048]{1,0:T(8,128)(2,1)S(1)}, bf16[32,2048]{1,0:T(8,128)(2,1)S(1)}, u32[]{:S(2)}, u32[]{:S(2)}) collective-permute-start(bf16[32,2048]{1,0:T(8,128)(2,1)S(1)} %get-tuple-element.133), channel_id=1, source_target_pairs={{0,16},{2,18},{4,20},{6,22},{8,24},{10,26},{12,28},{14,30},{16,0},... | collective-permute-start | bytes 393224 | tf_op jit(solution)/shard_map/ppermute | solution.py:676
  88.5 1.9 %collective-permute-start.19 = (bf16[40,1024]{1,0:T(8,128)(2,1)S(1)}, bf16[40,1024]{1,0:T(8,128)(2,1)S(1)}, u32[]{:S(2)}, u32[]{:S(2)}) collective-permute-start(bf16[40,1024]{1,0:T(8,128)(2,1)S(1)} %get-tuple-element.113), channel_id=1, source_target_pairs={{0,16},{2,18},{4,20},{6,22},{8,24},{10,26},{12,28},{14,30},{16,0},... | collective-permute-start | bytes 245768 | tf_op jit(solution)/shard_map/ppermute | solution.py:676
  90.4 2.0 %collective-permute-start.20 = (bf16[40,1024]{1,0:T(8,128)(2,1)S(1)}, bf16[40,1024]{1,0:T(8,128)(2,1)S(1)}, u32[]{:S(2)}, u32[]{:S(2)}) collective-permute-start(bf16[40,1024]{1,0:T(8,128)(2,1)S(1)} %get-tuple-element.114), channel_id=1, source_target_pairs={{0,24},{2,26},{4,28},{6,30},{8,16},{10,18},{12,20},{14,22},{16,8},... | collective-permute-start | bytes 245768 | tf_op jit(solution)/shard_map/ppermute | solution.py:676
  92.4 2.6 %shard_map.276 = bf16[196,4,512]{2,1,0:T(4,128)(2,1)} custom-call(s32[3]{0:T(128)S(1)} %pad_add_fusion.sel_ref.me_ref, bf16[2,196,512]{2,1,0:T(8,128)(2,1)S(1)} %get-tuple-element.92.own_ref, bf16[2,196,512]{2,1,0:T(8,128)(2,1)S(1)} %collective-permute-done.7.other_ref), custom_call_target="tpu_custom_call" | custom-call | flops 1000000 | bytes 1605632 | tf_op jit(solution)/shard_map/pallas_call | solution.py:655
  94.9 0.2 copy.40.other_ref
  95.1 2.1 %shard_map.278 = f32[196,4,512]{2,1,0:T(4,128)} custom-call(s32[3]{0:T(128)S(1)} %pad_add_fusion.sel_ref.me_ref, f32[2,196,512]{2,1,0:T(8,128)S(1)} %get-tuple-element.100.own_ref, f32[2,196,512]{2,1,0:T(8,128)S(1)} %copy.40.other_ref), custom_call_target="tpu_custom_call" | custom-call | flops 1000000 | bytes 3211264 | tf_op jit(solution)/shard_map/pallas_call | solution.py:655
  97.2 6.9 %collective-permute-done.19.refs_1_ = bf16[40,1024]{1,0:T(8,128)(2,1)S(1)} collective-permute-done((bf16[40,1024]{1,0:T(8,128)(2,1)S(1)}, bf16[40,1024]{1,0:T(8,128)(2,1)S(1)}, u32[]{:S(2)}, u32[]{:S(2)}) %collective-permute-start.19) | collective-permute-done | bytes 81952 | tf_op jit(solution)/shard_map/ppermute | solution.py:676
  104.0 1.2 %shard_map.282 = (f32[3,32,256]{2,1,0:T(8,128)}, f32[32,256]{1,0:T(8,128)}, f32[1,512]{1,0:T(1,128)}, f32[1,512]{1,0:T(1,128)}, f32[1,512]{1,0:T(1,128)}, /*inde...) custom-call(s32[3]{0:T(128)S(1)} %pad_add_fusion.sel_ref.me_ref, ...), custom_call_target="tpu_custom_call" | custom-call | flops 1000000 | bytes 564512 | tf_op jit(solution)/shard_map/pallas_call | solution.py:655
  105.3 1.3 %shard_map.285 = (f32[32,1024]{1,0:T(8,128)}, f32[32,1024]{1,0:T(8,128)}) custom-call(s32[3]{0:T(128)S(1)} %pad_add_fusion.sel_ref.me_ref, f32[32,2048]{1,0:T(8,128)S(1)} %get-tuple-element.131.own_ref, bf16[32,2048]{1,0:T(8,128)(2,1)S(1)} %collective-permute-done.26.refs_0_, bf16[32,2048]{1,0:T(8,128)(2,1)S(1)} %collective-permute-done.27.refs_1_, ...), custom_call_target="tpu_custom_call" | custom-call | flops 1000000 | bytes 917504 | tf_op jit(solution)/shard_map/pallas_call | solution.py:655
  (60 shorter events, 0.5 us)
Async XLA Ops:
  0.6 8.2 %collective-permute-start = (bf16[3,512,256]{2,1,0:T(8,128)(2,1)}, bf16[3,512,256]{2,1,0:T(8,128)(2,1)S(1)}, u32[]{:S(2)}, u32[]{:S(2)}) collective-permute-start(bf16[3,512,256]{2,1,0:T(8,128)(2,1)} %bitcast.23), channel_id=1, source_target_pairs={{0,1},{1,0},{2,3},{3,2},{4,5},{5,4},{6,7},{7,6},{8,9},{9,8},{10,11... | collective-permute-start | bytes 2359304 | tf_op jit(solution)/shard_map/ppermute | solution.py:817
  1.2 13.8 %collective-permute-start.4 = (bf16[512,1024]{1,0:T(8,128)(2,1)}, bf16[512,1024]{1,0:T(8,128)(2,1)S(1)}, u32[]{:S(2)}, u32[]{:S(2)}) collective-permute-start(bf16[512,1024]{1,0:T(8,128)(2,1)} %w1_ref.1), channel_id=1, source_target_pairs={{0,1},{1,0},{2,3},{3,2},{4,5},{5,4},{6,7},{7,6},{8,9},{9,8},{10,11... | collective-permute-start | bytes 3145736 | tf_op jit(solution)/shard_map/ppermute | solution.py:817
  1.3 13.8 %collective-permute-start.5 = (bf16[512,1024]{1,0:T(8,128)(2,1)}, bf16[512,1024]{1,0:T(8,128)(2,1)S(1)}, u32[]{:S(2)}, u32[]{:S(2)}) collective-permute-start(bf16[512,1024]{1,0:T(8,128)(2,1)} %w2_ref.1), channel_id=1, source_target_pairs={{0,1},{1,0},{2,3},{3,2},{4,5},{5,4},{6,7},{7,6},{8,9},{9,8},{10,11... | collective-permute-start | bytes 3145736 | tf_op jit(solution)/shard_map/ppermute | solution.py:817
  1.7 7.1 %collective-permute-start.3 = (bf16[512,256]{1,0:T(8,128)(2,1)}, bf16[512,256]{1,0:T(8,128)(2,1)S(1)}, u32[]{:S(2)}, u32[]{:S(2)}) collective-permute-start(bf16[512,256]{1,0:T(8,128)(2,1)} %pm_ref.3), channel_id=1, source_target_pairs={{0,1},{1,0},{2,3},{3,2},{4,5},{5,4},{6,7},{7,6},{8,9},{9,8},{10,11... | collective-permute-start | bytes 786440 | tf_op jit(solution)/shard_map/ppermute | solution.py:817
  1.8 4.9 %collective-permute-start.2 = (f32[8,169]{1,0:T(8,128)}, f32[8,169]{1,0:T(8,128)S(1)}, u32[]{:S(2)}, u32[]{:S(2)}) collective-permute-start(f32[8,169]{1,0:T(8,128)} %bitcast.26), channel_id=1, source_target_pairs={{0,1},{1,0},{2,3},{3,2},{4,5},{5,4},{6,7},{7,6},{8,9},{9,8},{10,11... | collective-permute-start | bytes 16232 | tf_op jit(solution)/shard_map/ppermute | solution.py:817
  2.2 1.4 %copy-start.14 = (bf16[4,196,512]{2,0,1:T(4,128)(2,1)S(1)}, bf16[4,196,512]{2,0,1:T(4,128)(2,1)}, u32[]{:S(2)}) copy-start(bf16[4,196,512]{2,0,1:T(4,128)(2,1)} %param.31) | copy-start | bytes 2408452
  2.3 4.4 %copy-start.8 = (f32[2,256]{1,0:T(2,128)S(1)}, f32[2,256]{1,0:T(2,128)}, u32[]{:S(2)}) copy-start(f32[2,256]{1,0:T(2,128)} %qvbm_ref.1) | copy-start | bytes 6148
  2.3 4.8 %copy-start.4 = (f32[169,8]{0,1:T(8,128)S(1)}, f32[169,8]{0,1:T(8,128)}, u32[]{:S(2)}) copy-start(f32[169,8]{0,1:T(8,128)} %param.22) | copy-start | bytes 16228
  3.8 4.8 %copy-start.5 = (f32[1024]{0:T(1024)S(1)}, f32[1024]{0:T(1024)}, u32[]{:S(2)}) copy-start(f32[1024]{0:T(1024)} %param.28) | copy-start | bytes 12292
  3.8 5.0 %copy-start.2 = (bf16[512,3,256]{2,0,1:T(8,128)(2,1)S(1)}, bf16[512,3,256]{2,0,1:T(8,128)(2,1)}, u32[]{:S(2)}) copy-start(bf16[512,3,256]{2,0,1:T(8,128)(2,1)} %param.20) | copy-start | bytes 2359300
  3.8 5.0 %copy-start.3 = (bf16[512,256]{1,0:T(8,128)(2,1)S(1)}, bf16[512,256]{1,0:T(8,128)(2,1)}, u32[]{:S(2)}) copy-start(bf16[512,256]{1,0:T(8,128)(2,1)} %pm_ref.3) | copy-start | bytes 786436
  3.9 5.0 %copy-start.6 = (s32[4,196]{1,0:T(4,128)S(1)}, s32[4,196]{1,0:T(4,128)}, u32[]{:S(2)}) copy-start(s32[4,196]{1,0:T(4,128)} %ids_ref.3) | copy-start | bytes 9412
  3.9 5.0 %copy-start.7 = (f32[512]{0:T(512)S(1)}, f32[512]{0:T(512)}, u32[]{:S(2)}) copy-start(f32[512]{0:T(512)} %param.19) | copy-start | bytes 6148
  3.9 5.0 %copy-start.9 = (f32[512]{0:T(512)S(1)}, f32[512]{0:T(512)}, u32[]{:S(2)}) copy-start(f32[512]{0:T(512)} %param.24) | copy-start | bytes 6148
  3.9 5.0 %copy-start.13 = (f32[512]{0:T(512)S(1)}, f32[512]{0:T(512)}, u32[]{:S(2)}) copy-start(f32[512]{0:T(512)} %param.18) | copy-start | bytes 6148
  6.7 1.9 %collective-permute-start.1 = (f32[2,256]{1,0:T(2,128)S(1)}, f32[2,256]{1,0:T(2,128)S(1)}, u32[]{:S(2)}, u32[]{:S(2)}) collective-permute-start(f32[2,256]{1,0:T(2,128)S(1)} %copy-done.8), channel_id=1, source_target_pairs={{0,1},{1,0},{2,3},{3,2},{4,5},{5,4},{6,7},{7,6},{8,9},{9,8},{10,11... | collective-permute-start | bytes 6152 | tf_op jit(solution)/shard_map/ppermute | solution.py:817
  8.7 6.4 %collective-permute-start.6 = (f32[1,1024]{1,0:T(1,128)S(1)}, f32[1,1024]{1,0:T(1,128)S(1)}, u32[]{:S(2)}, u32[]{:S(2)}) collective-permute-start(f32[1,1024]{1,0:T(1,128)S(1)} %bitcast.28), channel_id=1, source_target_pairs={{0,1},{1,0},{2,3},{3,2},{4,5},{5,4},{6,7},{7,6},{8,9},{9,8},{10,11... | collective-permute-start | bytes 12296 | tf_op jit(solution)/shard_map/ppermute | solution.py:817
  8.9 6.2 %copy-start.10 = (f32[512]{0:T(512)S(1)}, f32[512]{0:T(512)}, u32[]{:S(2)}) copy-start(f32[512]{0:T(512)} %param.26) | copy-start | bytes 6148
  8.9 6.2 %copy-start.11 = (f32[512]{0:T(512)S(1)}, f32[512]{0:T(512)}, u32[]{:S(2)}) copy-start(f32[512]{0:T(512)} %param.25) | copy-start | bytes 6148
  15.1 5.4 %copy-start = (bf16[512,1024]{1,0:T(8,128)(2,1)S(1)}, bf16[512,1024]{1,0:T(8,128)(2,1)}, u32[]{:S(2)}) copy-start(bf16[512,1024]{1,0:T(8,128)(2,1)} %w1_ref.1) | copy-start | bytes 3145732
  15.1 5.4 %copy-start.1 = (bf16[512,1024]{1,0:T(8,128)(2,1)S(1)}, bf16[512,1024]{1,0:T(8,128)(2,1)}, u32[]{:S(2)}) copy-start(bf16[512,1024]{1,0:T(8,128)(2,1)} %w2_ref.1) | copy-start | bytes 3145732
  19.9 26.8 %collective-permute-start.21 = (bf16[512,1024]{1,0:T(8,128)(2,1)S(1)}, bf16[512,1024]{1,0:T(8,128)(2,1)S(1)}, u32[]{:S(2)}, u32[]{:S(2)}) collective-permute-start(bf16[512,1024]{1,0:T(8,128)(2,1)S(1)} %get-tuple-element.125), channel_id=1, source_target_pairs={{0,1},{1,0},{2,3},{3,2},{4,5},{5,4},{6,7},{7,6},{8,9},{9,8},{10,11... | collective-permute-start | bytes 3145736 | tf_op jit(solution)/shard_map/ppermute | solution.py:817
  20.4 28.3 %collective-permute-start.22 = (bf16[512,1024]{1,0:T(8,128)(2,1)S(1)}, bf16[512,1024]{1,0:T(8,128)(2,1)S(1)}, u32[]{:S(2)}, u32[]{:S(2)}) collective-permute-start(bf16[512,1024]{1,0:T(8,128)(2,1)S(1)} %get-tuple-element.127), channel_id=1, source_target_pairs={{0,1},{1,0},{2,3},{3,2},{4,5},{5,4},{6,7},{7,6},{8,9},{9,8},{10,11... | collective-permute-start | bytes 3145736 | tf_op jit(solution)/shard_map/ppermute | solution.py:817
  20.5 4.1 %copy-start.12 = (f32[512]{0:T(512)S(1)}, f32[512]{0:T(512)}, u32[]{:S(2)}) copy-start(f32[512]{0:T(512)} %param.30) | copy-start | bytes 6148
  32.9 9.0 %collective-permute-start.10 = (bf16[512,512]{1,0:T(8,128)(2,1)S(1)}, bf16[512,512]{1,0:T(8,128)(2,1)S(1)}, u32[]{:S(2)}, u32[]{:S(2)}) collective-permute-start(bf16[512,512]{1,0:T(8,128)(2,1)S(1)} %get-tuple-element.104), channel_id=1, source_target_pairs={{0,1},{1,0},{2,3},{3,2},{4,5},{5,4},{6,7},{7,6},{8,9},{9,8},{10,11... | collective-permute-start | bytes 1572872 | tf_op jit(solution)/shard_map/ppermute | solution.py:817
  33.3 10.0 %collective-permute-start.9 = (bf16[512,512]{1,0:T(8,128)(2,1)S(1)}, bf16[512,512]{1,0:T(8,128)(2,1)S(1)}, u32[]{:S(2)}, u32[]{:S(2)}) collective-permute-start(bf16[512,512]{1,0:T(8,128)(2,1)S(1)} %get-tuple-element.102), channel_id=1, source_target_pairs={{0,1},{1,0},{2,3},{3,2},{4,5},{5,4},{6,7},{7,6},{8,9},{9,8},{10,11... | collective-permute-start | bytes 1572872 | tf_op jit(solution)/shard_map/ppermute | solution.py:817
  37.1 1.3 %collective-permute-start.14 = (f32[16,512]{1,0:T(8,128)S(1)}, f32[16,512]{1,0:T(8,128)S(1)}, u32[]{:S(2)}, u32[]{:S(2)}) collective-permute-start(f32[16,512]{1,0:T(8,128)S(1)} %get-tuple-element.109), channel_id=1, source_target_pairs={{0,1},{1,0},{2,3},{3,2},{4,5},{5,4},{6,7},{7,6},{8,9},{9,8},{10,11... | collective-permute-start | bytes 98312 | tf_op jit(solution)/shard_map/ppermute | solution.py:817
  38.9 5.8 %collective-permute-start.15 = (f32[16,512]{1,0:T(8,128)S(1)}, f32[16,512]{1,0:T(8,128)S(1)}, u32[]{:S(2)}, u32[]{:S(2)}) collective-permute-start(f32[16,512]{1,0:T(8,128)S(1)} %shard_map.280.refs_7_), channel_id=1, source_target_pairs={{0,2},{2,0},{4,6},{6,4},{8,10},{10,8},{12,14},{14,12},{16,18},{18,... | collective-permute-start | bytes 98312 | tf_op jit(solution)/shard_map/ppermute | solution.py:676
  41.8 4.8 %collective-permute-start.16 = (f32[16,512]{1,0:T(8,128)S(1)}, f32[16,512]{1,0:T(8,128)S(1)}, u32[]{:S(2)}, u32[]{:S(2)}) collective-permute-start(f32[16,512]{1,0:T(8,128)S(1)} %shard_map.280.refs_7_), channel_id=1, source_target_pairs={{0,4},{2,6},{4,0},{6,2},{8,12},{10,14},{12,8},{14,10},{16,20},{18,... | collective-permute-start | bytes 98312 | tf_op jit(solution)/shard_map/ppermute | solution.py:676
  44.1 14.7 %collective-permute-start.11 = (bf16[128,1024]{1,0:T(8,128)(2,1)S(1)}, bf16[128,1024]{1,0:T(8,128)(2,1)S(1)}, u32[]{:S(2)}, u32[]{:S(2)}) collective-permute-start(bf16[128,1024]{1,0:T(8,128)(2,1)S(1)} %get-tuple-element.105), channel_id=1, source_target_pairs={{0,2},{2,0},{4,6},{6,4},{8,10},{10,8},{12,14},{14,12},{16,18},{18,... | collective-permute-start | bytes 786440 | tf_op jit(solution)/shard_map/ppermute | solution.py:676
  44.7 15.7 %collective-permute-start.12 = (bf16[128,1024]{1,0:T(8,128)(2,1)S(1)}, bf16[128,1024]{1,0:T(8,128)(2,1)S(1)}, u32[]{:S(2)}, u32[]{:S(2)}) collective-permute-start(bf16[128,1024]{1,0:T(8,128)(2,1)S(1)} %get-tuple-element.106), channel_id=1, source_target_pairs={{0,4},{2,6},{4,0},{6,2},{8,12},{10,14},{12,8},{14,10},{16,20},{18,... | collective-permute-start | bytes 786440 | tf_op jit(solution)/shard_map/ppermute | solution.py:676
  46.6 41.8 %collective-permute-start.8 = (f32[2,196,512]{2,0,1:T(2,128)S(1)}, f32[2,196,512]{2,0,1:T(2,128)S(1)}, u32[]{:S(2)}, u32[]{:S(2)}) collective-permute-start(f32[2,196,512]{2,0,1:T(2,128)S(1)} %copy.39), channel_id=1, source_target_pairs={{0,1},{1,0},{2,3},{3,2},{4,5},{5,4},{6,7},{7,6},{8,9},{9,8},{10,11... | collective-permute-start | bytes 2408456 | tf_op jit(solution)/shard_map/ppermute | solution.py:817
  46.7 15.1 %collective-permute-start.13 = (bf16[128,1024]{1,0:T(8,128)(2,1)S(1)}, bf16[128,1024]{1,0:T(8,128)(2,1)S(1)}, u32[]{:S(2)}, u32[]{:S(2)}) collective-permute-start(bf16[128,1024]{1,0:T(8,128)(2,1)S(1)} %get-tuple-element.107), channel_id=1, source_target_pairs={{0,6},{2,4},{4,2},{6,0},{8,14},{10,12},{12,10},{14,8},{16,22},{18,... | collective-permute-start | bytes 786440 | tf_op jit(solution)/shard_map/ppermute | solution.py:676
  48.7 9.7 %collective-permute-start.17 = (f32[16,512]{1,0:T(8,128)S(1)}, f32[16,512]{1,0:T(8,128)S(1)}, u32[]{:S(2)}, u32[]{:S(2)}) collective-permute-start(f32[16,512]{1,0:T(8,128)S(1)} %shard_map.280.refs_7_), channel_id=1, source_target_pairs={{0,6},{2,4},{4,2},{6,0},{8,14},{10,12},{12,10},{14,8},{16,22},{18,... | collective-permute-start | bytes 98312 | tf_op jit(solution)/shard_map/ppermute | solution.py:676
  58.3 14.8 %collective-permute-start.23 = (bf16[128,2048]{1,0:T(8,128)(2,1)S(1)}, bf16[128,2048]{1,0:T(8,128)(2,1)S(1)}, u32[]{:S(2)}, u32[]{:S(2)}) collective-permute-start(bf16[128,2048]{1,0:T(8,128)(2,1)S(1)} %get-tuple-element.128), channel_id=1, source_target_pairs={{0,2},{2,0},{4,6},{6,4},{8,10},{10,8},{12,14},{14,12},{16,18},{18,... | collective-permute-start | bytes 1572872 | tf_op jit(solution)/shard_map/ppermute | solution.py:676
  58.7 24.4 %collective-permute-start.24 = (bf16[128,2048]{1,0:T(8,128)(2,1)S(1)}, bf16[128,2048]{1,0:T(8,128)(2,1)S(1)}, u32[]{:S(2)}, u32[]{:S(2)}) collective-permute-start(bf16[128,2048]{1,0:T(8,128)(2,1)S(1)} %get-tuple-element.129), channel_id=1, source_target_pairs={{0,4},{2,6},{4,0},{6,2},{8,12},{10,14},{12,8},{14,10},{16,20},{18,... | collective-permute-start | bytes 1572872 | tf_op jit(solution)/shard_map/ppermute | solution.py:676
  60.4 22.7 %collective-permute-start.25 = (bf16[128,2048]{1,0:T(8,128)(2,1)S(1)}, bf16[128,2048]{1,0:T(8,128)(2,1)S(1)}, u32[]{:S(2)}, u32[]{:S(2)}) collective-permute-start(bf16[128,2048]{1,0:T(8,128)(2,1)S(1)} %get-tuple-element.130), channel_id=1, source_target_pairs={{0,6},{2,4},{4,2},{6,0},{8,14},{10,12},{12,10},{14,8},{16,22},{18,... | collective-permute-start | bytes 1572872 | tf_op jit(solution)/shard_map/ppermute | solution.py:676
  61.8 26.6 %collective-permute-start.7 = (bf16[2,196,512]{2,1,0:T(8,128)(2,1)S(1)}, bf16[2,196,512]{2,1,0:T(8,128)(2,1)S(1)}, u32[]{:S(2)}, u32[]{:S(2)}) collective-permute-start(bf16[2,196,512]{2,1,0:T(8,128)(2,1)S(1)} %get-tuple-element.92.own_ref), channel_id=1, source_target_pairs={{0,1},{1,0},{2,3},{3,2},{4,5},{5,4},{6,7},{7,6},{8,9},{9,8},{10,11... | collective-permute-start | bytes 1204232 | tf_op jit(solution)/shard_map/ppermute | solution.py:817
  73.1 17.2 %collective-permute-start.18 = (bf16[40,1024]{1,0:T(8,128)(2,1)S(1)}, bf16[40,1024]{1,0:T(8,128)(2,1)S(1)}, u32[]{:S(2)}, u32[]{:S(2)}) collective-permute-start(bf16[40,1024]{1,0:T(8,128)(2,1)S(1)} %get-tuple-element.112), channel_id=1, source_target_pairs={{0,8},{2,10},{4,12},{6,14},{8,0},{10,2},{12,4},{14,6},{16,24},{18,... | collective-permute-start | bytes 245768 | tf_op jit(solution)/shard_map/ppermute | solution.py:676
  84.0 21.3 %collective-permute-start.26 = (bf16[32,2048]{1,0:T(8,128)(2,1)S(1)}, bf16[32,2048]{1,0:T(8,128)(2,1)S(1)}, u32[]{:S(2)}, u32[]{:S(2)}) collective-permute-start(bf16[32,2048]{1,0:T(8,128)(2,1)S(1)} %get-tuple-element.132), channel_id=1, source_target_pairs={{0,8},{2,10},{4,12},{6,14},{8,0},{10,2},{12,4},{14,6},{16,24},{18,... | collective-permute-start | bytes 393224 | tf_op jit(solution)/shard_map/ppermute | solution.py:676
  85.9 19.4 %collective-permute-start.27 = (bf16[32,2048]{1,0:T(8,128)(2,1)S(1)}, bf16[32,2048]{1,0:T(8,128)(2,1)S(1)}, u32[]{:S(2)}, u32[]{:S(2)}) collective-permute-start(bf16[32,2048]{1,0:T(8,128)(2,1)S(1)} %get-tuple-element.133), channel_id=1, source_target_pairs={{0,16},{2,18},{4,20},{6,22},{8,24},{10,26},{12,28},{14,30},{16,0},... | collective-permute-start | bytes 393224 | tf_op jit(solution)/shard_map/ppermute | solution.py:676
  88.5 16.9 %collective-permute-start.28 = (bf16[32,2048]{1,0:T(8,128)(2,1)S(1)}, bf16[32,2048]{1,0:T(8,128)(2,1)S(1)}, u32[]{:S(2)}, u32[]{:S(2)}) collective-permute-start(bf16[32,2048]{1,0:T(8,128)(2,1)S(1)} %get-tuple-element.134), channel_id=1, source_target_pairs={{0,24},{2,26},{4,28},{6,30},{8,16},{10,18},{12,20},{14,22},{16,8},... | collective-permute-start | bytes 393224 | tf_op jit(solution)/shard_map/ppermute | solution.py:676
  88.5 15.6 %collective-permute-start.19 = (bf16[40,1024]{1,0:T(8,128)(2,1)S(1)}, bf16[40,1024]{1,0:T(8,128)(2,1)S(1)}, u32[]{:S(2)}, u32[]{:S(2)}) collective-permute-start(bf16[40,1024]{1,0:T(8,128)(2,1)S(1)} %get-tuple-element.113), channel_id=1, source_target_pairs={{0,16},{2,18},{4,20},{6,22},{8,24},{10,26},{12,28},{14,30},{16,0},... | collective-permute-start | bytes 245768 | tf_op jit(solution)/shard_map/ppermute | solution.py:676
  90.4 13.7 %collective-permute-start.20 = (bf16[40,1024]{1,0:T(8,128)(2,1)S(1)}, bf16[40,1024]{1,0:T(8,128)(2,1)S(1)}, u32[]{:S(2)}, u32[]{:S(2)}) collective-permute-start(bf16[40,1024]{1,0:T(8,128)(2,1)S(1)} %get-tuple-element.114), channel_id=1, source_target_pairs={{0,24},{2,26},{4,28},{6,30},{8,16},{10,18},{12,20},{14,22},{16,8},... | collective-permute-start | bytes 245768 | tf_op jit(solution)/shard_map/ppermute | solution.py:676
